TPU v7x, 32 devices: a whole 2x2x4 slice. The times are simulated.
32 devices in a mesh: gx: 4 (over y, core), gy: 2 (over x), gz: 4 (over z).
Axes of the slice: x: 2, y: 2, z: 4, core: 2. Of those that a mesh axis runs over, the one named last changes fastest.
Arguments:
- offsets: float32 [8, 4, 8, 3, 128], P('gx', 'gy', 'gz'), may hold values from 0 to 1
- velocity: float32 [8, 4, 8, 3, 128], P('gx', 'gy', 'gz'), may hold values from -6 to 6
- mass: float32 [8, 4, 8, 128], P('gx', 'gy', 'gz'), may hold values from 0.05 to 0.2
- energy: float32 [8, 4, 8, 128], P('gx', 'gy', 'gz'), may hold values from 0.5 to 2
- partner_mask: int32 [8, 4, 8, 27], P('gx', 'gy', 'gz'), may hold values from 0 to 1, as said below
- counts: int32 [8, 4, 8], P('gx', 'gy', 'gz'), may hold values from 1 to 128, as said below
Outputs:
- acceleration: float32 [8, 4, 8, 3, 128], P('gx', 'gy', 'gz')
- energy_rate: float32 [8, 4, 8, 128], P('gx', 'gy', 'gz')
Inputs may be any that keep to these rules, and one draw needn't show every extreme that they name: `partner_mask`: partner 13 (the leaf itself) is always 1. `counts`: some leaf holds 128 valid particles.
All inputs are finite; a program needn't handle non-finite values.
Results may differ from a plain program's by a relative error of at most 0.0003.
Values sent between devices are 32-bit elements; how exact they have to be, the bound alone decides.
No kernel may reach another device: no remote copies, remote signals or barrier semaphores. Data moves between devices by JAX's collectives and lax.ppermute only.
A program may use at most 64 MiB of HBM per device.

v0:
```python
import functools
import itertools

import jax
import jax.numpy as jnp
from jax import lax
from jax.experimental import pallas as pl
from jax.experimental.pallas import tpu as pltpu
from jax.sharding import PartitionSpec as P

AXES = (("gx", 0), ("gy", 1), ("gz", 2))
FAR = 1024.0
TINY = 1e-30
ROOM = 6 << 20
GROUP = 4
AHEAD = 2
WIDE = (0, 1, 2, 4, 5, 6)
OFFSETS = tuple(itertools.product((-1, 0, 1), repeat=3))


def ends_of(block, axis, dim):
    count = lax.axis_size(axis)
    size = block.shape[dim]
    last = lax.slice_in_dim(block, size - 1, None, axis=dim)
    first = lax.slice_in_dim(block, 0, 1, axis=dim)
    if count == 1:
        return last, first
    if count == 2:
        ends = block if size == 2 else jnp.concatenate([first, last], axis=dim)
        ends = lax.ppermute(ends, axis, [(0, 1), (1, 0)])
        return lax.slice_in_dim(ends, 1, 2, axis=dim), lax.slice_in_dim(ends, 0, 1, axis=dim)
    forward = [(i, (i + 1) % count) for i in range(count)]
    backward = [(target, source) for source, target in forward]
    return lax.ppermute(last, axis, forward), lax.ppermute(first, axis, backward)


def after(block, *others):
    return lax.optimization_barrier((block,) + others)[0]


def exchange(block, beside_x, beside_y):
    low, high = ends_of(block, "gx", 0)
    wide = jnp.concatenate([low, block, high], axis=0)
    first = beside_x()
    low, high = ends_of(after(wide, *first), "gy", 1)
    layers = jnp.concatenate([low, wide, high], axis=1)
    second = beside_y()
    low, high = ends_of(after(layers, *second), "gz", 2)
    return flat(layers), jnp.concatenate([flat(low), flat(high)], axis=0)


def column_constant(values, rows):
    ids = lax.broadcasted_iota(jnp.int32, (rows, 128), 0)
    out = jnp.zeros((rows, 128), jnp.float32)
    for row, value in enumerate(values):
        if value != 0.0:
            out = jnp.where(ids == row, jnp.float32(value), out)
    return out


def pair_inside(own, row):
    dx = own[0] - row(0)
    dy = own[1] - row(1)
    dz = own[2] - row(2)
    square = dx * dx + dy * dy + dz * dz
    radius = square * lax.rsqrt(jnp.maximum(square, TINY))
    return dx, dy, dz, jnp.maximum(1.0 - radius, 0.0)


def volume_pair(own, row):
    _, _, _, inside = pair_inside(own, row)
    second = inside * inside
    return ((second * second) * (1.25 - inside),)


def density_pair(own, row):
    dx, dy, dz, inside = pair_inside(own, row)
    third = inside * inside * inside
    value = third * (inside * (1.25 - inside))
    relative = (row(4) - own[4]) * dx + (row(5) - own[5]) * dy + (row(6) - own[6]) * dz
    volume = row(7)
    return (
        row(3) * value,
        volume * value,
        (volume * third) * relative,
    )


def force_pair(own, row):
    dx, dy, dz, inside = pair_inside(own, row)
    scaled = row(3) * (inside * inside * inside)
    relative = (own[4] - row(4)) * dx + (own[5] - row(5)) * dy + (own[6] - row(6)) * dz
    half = (own[10] + row(10)) / (own[8] + row(8))
    heat = own[9] + half
    push = (heat + (row(9) + half)) * scaled
    return (
        push * dx,
        push * dy,
        push * dz,
        (heat * scaled) * relative,
    )


def prepare_kernel(counts_hbm, offsets_hbm, velocity_hbm, mass_hbm, out_ref, *scratch):
    sources = (counts_hbm, offsets_hbm, velocity_hbm, mass_hbm)
    holds, sems = scratch[:4], scratch[4]
    copies = [
        pltpu.make_async_copy(source, hold, sems.at[i])
        for i, (source, hold) in enumerate(zip(sources, holds))
    ]
    for copy in copies:
        copy.start()
    for copy in copies:
        copy.wait()
    counts_ref, offsets_ref, velocity_ref, mass_ref = holds
    nx, ny, nz = mass_ref.shape[:3]
    for leaf, (x, y, z) in enumerate(itertools.product(range(nx), range(ny), range(nz))):
        for c in range(3):
            out_ref[leaf, c : c + 1, :] = offsets_ref[x, y, c, z : z + 1, :]
            out_ref[leaf, 4 + c : 5 + c, :] = velocity_ref[x, y, c, z : z + 1, :]
        out_ref[leaf, 3:4, :] = mass_ref[x, y, z : z + 1, :]
        number = counts_ref[x, y : y + 1, z : z + 1].astype(jnp.float32)
        out_ref[leaf, 7:8, :] = jnp.broadcast_to(number, (1, mass_ref.shape[3]))


def partners(grid):
    nx, ny, nz = grid
    parts = ([], [], [])
    for x, y, z in itertools.product(range(nx), range(ny), range(nz)):
        for part in parts:
            part.append([])
        for k, (ox, oy, oz) in enumerate(OFFSETS):
            tx, ty, tz = x + ox, y + oy, z + oz
            plane = (tx + 1) * (ny + 2) + ty + 1
            if not 0 <= tz < nz:
                parts[2][-1].append((k, plane + (0 if tz < 0 else (nx + 2) * (ny + 2))))
            elif 0 <= tx < nx and 0 <= ty < ny:
                parts[0][-1].append((k, (tx * ny + ty) * nz + tz))
            else:
                parts[1][-1].append((k, plane * nz + tz))
    return parts


def longest(part):
    return max(len(leaf) for leaf in part)


def list_tiles(part):
    return longest(part) + 1 + AHEAD


def split_place(start):
    return start & 127, lax.shift_right_logical(start, 7)


def put(list_ref, leaf, shift, tile, block, lanes):
    rolled = pltpu.roll(block, shift, axis=1)
    pltpu.store(list_ref.at[leaf, tile], rolled, mask=lanes >= shift)
    list_ref[leaf, tile + 1] = rolled


def close(list_ref, leaf, shift, tile, tail, lanes):
    pltpu.store(list_ref.at[leaf, tile], tail, mask=lanes >= shift)
    for step in range(1, AHEAD):
        list_ref[leaf, tile + step] = tail


def lane_ids(rows):
    return lax.broadcasted_iota(jnp.int32, (rows, 128), 1)


def pack_places(part, source_ref, list_ref, size_of, note):
    lanes = lane_ids(8)
    far = column_constant((FAR, FAR, FAR), 8)
    moves = [column_constant(offset, 8) for offset in OFFSETS]
    for leaf, found in enumerate(part):
        start = jnp.int32(0)
        for index, (k, place) in enumerate(found):
            shift, tile = split_place(start)
            note(leaf, index, shift, tile)
            put(list_ref, leaf, shift, tile, source_ref[place] + moves[k], lanes)
            start = start + size_of(leaf, k, place)
        shift, tile = split_place(start)
        note(leaf, len(found), shift, tile)
        note(leaf, None, shift, tile)
        close(list_ref, leaf, shift, tile, far, lanes)


def pack_side(part, source_ref, side_ref, shift_ref, tile_ref, tail):
    height = source_ref.shape[1]
    lanes = lane_ids(height)
    last = column_constant(tail, height)
    stride = longest(part) + 1
    for leaf, found in enumerate(part):
        for index, (_, place) in enumerate(found):
            at = leaf * stride + index
            put(side_ref, leaf, shift_ref[at], tile_ref[at], source_ref[place], lanes)
        at = leaf * stride + len(found)
        close(side_ref, leaf, shift_ref[at], tile_ref[at], last, lanes)


def widen_kernel(rows, block_ref, out_ref):
    for leaf in range(block_ref.shape[0]):
        for index, c in enumerate(rows):
            row = block_ref[leaf, c : c + 1, :]
            out_ref[leaf, index] = jnp.transpose(jnp.broadcast_to(row, (128, 128)))


def arrange_kernel(parts, *refs):
    mask_ref, refs = refs[0], refs[1:]
    count = len(parts)
    for i, part in enumerate(parts):
        counts_ref, source_ref = refs[i], refs[count + i]
        list_ref, shift_ref, tile_ref, last_ref = refs[2 * count + 4 * i : 2 * count + 4 * i + 4]
        stride = longest(part) + 1

        def size_of(leaf, k, place):
            return counts_ref[place] * mask_ref[leaf * 27 + k]

        def note(leaf, index, shift, tile):
            if index is None:
                last_ref[leaf] = tile
            else:
                shift_ref[leaf * stride + index] = shift
                tile_ref[leaf * stride + index] = tile

        pack_places(part, source_ref, list_ref, size_of, note)


def run_pairs(grid, pair, n_sums, count_of, last_of, own_of, row_of, before_ref, acc_ref):
    zero = jnp.zeros((8, 128), jnp.float32)

    def leaf_step(leaf, carry):
        count = count_of(leaf)
        steps = lax.shift_right_logical(last_of(leaf) + AHEAD, AHEAD.bit_length() - 1)

        def group_step(group, carry):
            places = [
                pl.ds(pl.multiple_of(group * (8 * GROUP) + 8 * part, 8), 8) for part in range(GROUP)
            ]
            owns = [own_of(leaf, at) for at in places]

            def partner_step(step, sums):
                for more in range(AHEAD):
                    rows = {}
                    at = step * AHEAD + more

                    def row(c):
                        if c not in rows:
                            rows[c] = jnp.broadcast_to(row_of(leaf, at, c), (8, 128))
                        return rows[c]

                    terms = [pair(own, row) for own in owns]
                    sums = tuple(
                        tuple(a + b for a, b in zip(old, new)) for old, new in zip(sums, terms)
                    )
                return sums

            start = tuple(
                tuple(zero if before_ref is None else before_ref[leaf, i, at, :] for i in range(n_sums))
                for at in places
            )
            sums = lax.fori_loop(0, steps, partner_step, start)
            for part, at in enumerate(places):
                for index in range(n_sums):
                    acc_ref[leaf, index, at, :] = sums[part][index]
            return carry

        groups = lax.shift_right_logical(count + (8 * GROUP - 1), (8 * GROUP).bit_length() - 1)
        return lax.fori_loop(0, groups, group_step, carry)

    lax.fori_loop(0, grid[0] * grid[1] * grid[2], leaf_step, 0)


def leaf_totals(grid, acc_ref, counts_ref):
    for leaf, index in enumerate(itertools.product(*map(range, grid))):
        sums = [
            jnp.sum(jnp.transpose(acc_ref[leaf, i]), axis=0, keepdims=True)
            for i in range(acc_ref.shape[1])
        ]
        yield index, leaf, sums, lax.broadcasted_iota(jnp.int32, (1, 128), 1) < counts_ref[leaf]


def own_reader(*pieces):
    def own_of(leaf, at):
        return {c: ref[leaf, i, at, :] for ref, channels in pieces for i, c in enumerate(channels)}

    return own_of


def row_reader(list_ref, side_ref=None, base=8):
    def row_of(leaf, at, c):
        if c < base:
            return list_ref[leaf, at, c : c + 1, :]
        return side_ref[leaf, at, c - base : c - base + 1, :]

    return row_of


def volume_kernel(grid, part, stage, *refs):
    refs = list(refs)
    out_ref, counts_ref, list_ref, last_ref = refs[-4:] if stage < 2 else refs[-5:-1]
    acc_ref = out_ref if stage < 2 else refs[-1]
    centers_ref = refs.pop(0) if stage else counts_ref
    source_ref, wide_ref = refs[:2]
    for place in range(source_ref.shape[0]):
        counts_ref[place] = source_ref[place, 7:8, :].astype(jnp.int32)[0, 0]

    def note(leaf, index, shift, tile):
        if index is None:
            last_ref[leaf] = tile

    pack_places(part, source_ref, list_ref, lambda leaf, k, place: counts_ref[place], note)
    run_pairs(
        grid, volume_pair, 1, lambda leaf: centers_ref[leaf], lambda leaf: last_ref[leaf],
        own_reader((wide_ref, WIDE)), row_reader(list_ref), refs[2] if stage else None, acc_ref,
    )
    if stage == 2:
        for index, leaf, sums, valid in leaf_totals(grid, acc_ref, centers_ref):
            out_ref[leaf] = jnp.where(valid, 1.0 / (1.0 + 4.0 * sums[0]), 1.0)


def density_kernel(grid, part, stage, *refs):
    counts_ref, shift_ref, tile_ref, last_ref, list_ref, wide_ref, source_ref = refs[:7]
    out_ref, side_ref = refs[-2:] if stage < 2 else refs[-3:-1]
    acc_ref = out_ref if stage < 2 else refs[-1]
    pack_side(part, source_ref, side_ref, shift_ref, tile_ref, ())
    run_pairs(
        grid, density_pair, 3, lambda leaf: counts_ref[leaf], lambda leaf: last_ref[leaf],
        own_reader((wide_ref, WIDE)), row_reader(list_ref, side_ref, 7), refs[7] if stage else None, acc_ref,
    )
    if stage == 2:
        own_ref, volume_ref, energy_ref = refs[8:11]
        for (x, y, z), leaf, sums, valid in leaf_totals(grid, acc_ref, counts_ref):
            density = (own_ref[leaf, 3:4, :] + 4.0 * sums[0]) / (volume_ref[leaf] + 4.0 * sums[1])
            density = jnp.where(valid, density, 1.0)
            energy = energy_ref[x, y, z : z + 1, :]
            out_ref[leaf, 0:1, :] = density
            out_ref[leaf, 1:2, :] = jnp.where(valid, (2.0 / 3.0) * energy / density, 0.0)
            out_ref[leaf, 2:3, :] = jnp.where(valid, jnp.maximum(20.0 * sums[2], 0.0), 0.0)
            out_ref[leaf, 3:4, :] = jnp.zeros_like(density)


def force_kernel(grid, part, stage, *refs):
    counts_ref, shift_ref, tile_ref, last_ref, list_ref, wide_ref, state_ref, source_ref = refs[:8]
    side_ref = refs[-1] if stage < 2 else refs[-2]
    acc_ref = refs[-2] if stage < 2 else refs[-1]
    pack_side(part, source_ref, side_ref, shift_ref, tile_ref, (1.0,))
    run_pairs(
        grid, force_pair, 4, lambda leaf: counts_ref[leaf], lambda leaf: last_ref[leaf],
        own_reader((wide_ref, WIDE), (state_ref, (8, 9, 10))), row_reader(list_ref, side_ref),
        refs[8] if stage else None, acc_ref,
    )
    if stage == 2:
        push_ref, heat_ref = refs[9:11]
        for (x, y, z), leaf, sums, valid in leaf_totals(grid, acc_ref, counts_ref):
            for c in range(3):
                push_ref[x, y, c, z : z + 1, :] = jnp.where(valid, 20.0 * sums[c], 0.0)
            heat_ref[x, y, z : z + 1, :] = jnp.where(valid, -20.0 * sums[3], 0.0)


def call(name, body, inputs, outs, scratch=(), cycles=0):
    def spec(x):
        scalar = x.dtype == jnp.int32 and len(x.shape) == 1
        return pl.BlockSpec(memory_space=pltpu.SMEM if scalar else pltpu.VMEM)

    return pl.pallas_call(
        body,
        out_shape=outs,
        in_specs=[spec(x) for x in inputs],
        out_specs=[spec(x) for x in outs],
        scratch_shapes=scratch,
        compiler_params=pltpu.CompilerParams(vmem_limit_bytes=ROOM),
        cost_estimate=pl.CostEstimate(flops=cycles * 4096, bytes_accessed=1 << 20, transcendentals=0),
        name=name,
    )(*inputs)


def floats(*shape):
    return jax.ShapeDtypeStruct(shape, jnp.float32)


def integers(*shape):
    return jax.ShapeDtypeStruct(shape, jnp.int32)


def flat(block):
    return block.reshape((-1,) + block.shape[3:])


def shards(offsets, velocity, mass, energy, partner_mask, counts):
    grid = counts.shape
    slots = offsets.shape[4]
    assert slots == 128
    leaves = grid[0] * grid[1] * grid[2]
    parts = partners(grid)
    inputs = (counts, jnp.swapaxes(offsets, 2, 3), jnp.swapaxes(velocity, 2, 3), mass)
    own = pl.pallas_call(
        prepare_kernel,
        out_shape=floats(leaves, 8, slots),
        in_specs=[pl.BlockSpec(memory_space=pltpu.HBM)] * 4,
        out_specs=pl.BlockSpec(memory_space=pltpu.VMEM),
        scratch_shapes=[pltpu.VMEM(x.shape, x.dtype) for x in inputs] + [pltpu.SemaphoreType.DMA((4,))],
        compiler_params=pltpu.CompilerParams(vmem_limit_bytes=ROOM),
        name="prepare",
    )(*inputs)
    mask = partner_mask.reshape(-1)
    wide = call(
        "widen", functools.partial(widen_kernel, WIDE), [own],
        [floats(leaves, len(WIDE), slots, slots)], cycles=2000,
    )[0]

    def packed_space(p, height):
        return pltpu.VMEM((leaves, list_tiles(parts[p]), height, slots), jnp.float32)

    def spread_sums(p, n_sums):
        shape = (leaves, n_sums, slots, slots)
        return ([floats(*shape)], []) if p < 2 else ([], [pltpu.VMEM(shape, jnp.float32)])

    def volume_part(p, source, centers=(), before=()):
        outs, own_space = spread_sums(p, 1)
        return call(
            f"volume_{p}", functools.partial(volume_kernel, grid, parts[p], p),
            [*centers, source, wide, *before],
            (outs or [floats(leaves, 1, slots)]) + [integers(source.shape[0])],
            [packed_space(p, 8), pltpu.SMEM((leaves,), jnp.int32)] + own_space, cycles=3000,
        )

    near_counts, lists, early = [], [], []

    def volume_own():
        part, number = volume_part(0, own)
        near_counts.append(number)
        early.append(part)
        return (part,)

    layers, ends = exchange(own.reshape(grid + (8, slots)), lambda: (wide,), volume_own)
    part, number = volume_part(1, layers, near_counts, early)
    volume, last_number = volume_part(2, ends, near_counts, [part])
    near_counts += [number, last_number]

    def arrange():
        outs = []
        for part in parts:
            stride = longest(part) + 1
            outs += [
                floats(leaves, list_tiles(part), 8, slots),
                integers(leaves * stride), integers(leaves * stride), integers(leaves),
            ]
        done = call(
            "arrange", functools.partial(arrange_kernel, parts), [mask, *near_counts, own, layers, ends],
            outs, cycles=2000,
        )
        lists.extend(tuple(done[4 * p : 4 * p + 4]) for p in range(3))
        return tuple(entry[0] for entry in lists)

    def density_part(p, source, more=()):
        packed, shifts, starts, last = lists[p]
        outs, own_space = spread_sums(p, 3)
        return call(
            f"density_{p}", functools.partial(density_kernel, grid, parts[p], p),
            [near_counts[0], shifts, starts, last, packed, wide, source, *more],
            outs or [floats(leaves, 4, slots)], [packed_space(p, 1)] + own_space, cycles=4000,
        )[0]

    def density_own():
        early[:] = [density_part(0, volume)]
        return tuple(early)

    volume_layers, volume_ends = exchange(volume.reshape(grid + (1, slots)), arrange, density_own)
    part = density_part(1, volume_layers, early)
    state = density_part(2, volume_ends, [part, own, volume, energy])

    wide_state = call(
        "widen_state", functools.partial(widen_kernel, (0, 1, 2)), [state],
        [floats(leaves, 3, slots, slots)], cycles=1000,
    )[0]

    def force_part(p, source, more=()):
        packed, shifts, starts, last = lists[p]
        outs, own_space = spread_sums(p, 4)
        return call(
            f"force_{p}", functools.partial(force_kernel, grid, parts[p], p),
            [near_counts[0], shifts, starts, last, packed, wide, wide_state, source, *more],
            outs or [floats(*grid[:2], 3, grid[2], slots), floats(*grid, slots)],
            [packed_space(p, 4)] + own_space, cycles=5000,
        )

    def force_own():
        early[:] = force_part(0, state)
        return tuple(early)

    state_layers, state_ends = exchange(state.reshape(grid + (4, slots)), lambda: (wide_state,), force_own)
    push, heat = force_part(2, state_ends, force_part(1, state_layers, early))
    return jnp.swapaxes(push, 2, 3), heat


def solution(mesh):
    placed = (
        P("gx", "gy", "gz", None, None),
        P("gx", "gy", "gz", None, None),
        P("gx", "gy", "gz", None),
        P("gx", "gy", "gz", None),
        P("gx", "gy", "gz", None),
        P("gx", "gy", "gz"),
    )
    return jax.shard_map(
        shards,
        mesh=mesh,
        in_specs=placed,
        out_specs=(P("gx", "gy", "gz", None, None), P("gx", "gy", "gz", None)),
        check_vma=False,
    )
```

profile of v0, /device:TPU:0, one launch (start us, length us, event | category | flops | bytes accessed | tf_op | source)
XLA Modules:
  0.0 57.3 jit_solution(1238946320430556349)
XLA Ops:
  4.1 2.0 %collective-permute-start.1 = (f32[1,2,2,8,128]{4,3,1,0,2:T(8,128)S(1)}, f32[1,2,2,8,128]{4,3,1,0,2:T(8,128)S(1)}, u32[]{:S(2)}, u32[]{:S(2)}) collective-permute-start(f32[1,2,2,8,128]{4,3,1,0,2:T(8,128)S(1)} %copy.9), channel_id=1, source_target_pairs={{8,0},{16,8},{24,16},{0,24},{9,1},{17,9},{25,17},{1,25},{10,2},{18... | collective-permute-start | bytes 49160 | tf_op jit(solution)/shard_map/ppermute | solution.py:34
  6.2 0.9 %widen.1.refs_1_.refs_2_.refs_5_ = f32[8,6,128,128]{3,2,1,0:T(8,128)S(1)} custom-call(f32[8,8,128]{2,1,0:T(8,128)S(1)} %prepare.1.block_ref.refs_0_.refs_4_.refs_8_), custom_call_target="tpu_custom_call" | custom-call | flops 8192000 | bytes 1048576 | tf_op jit(solution)/shard_map/widen/pallas_call | solution.py:367
  7.6 2.3 %collective-permute-start.2 = (f32[4,2,2,8,128]{4,3,1,0,2:T(8,128)S(1)}, f32[4,2,2,8,128]{4,3,1,0,2:T(8,128)S(1)}, u32[]{:S(2)}, u32[]{:S(2)}) collective-permute-start(f32[4,2,2,8,128]{4,3,1,0,2:T(8,128)S(1)} %constant_dynamic-update-slice_fusion), channel_id=1, source_target_pairs={{0,4},{4,0},{1,5},{5,1},{2,6},{6,2},{3,7},{7,3},{8,12},{12,8},{9,1... | collective-permute-start | bytes 196616 | tf_op jit(solution)/shard_map/ppermute | solution.py:30
  9.9 1.3 %volume_0.1 = (f32[8,1,128,128]{3,2,1,0:T(8,128)S(1)}, s32[8]{0:T(128)S(1)}) custom-call(f32[8,8,128]{2,1,0:T(8,128)S(1)} %prepare.1.block_ref.refs_0_.refs_4_.refs_8_, f32[8,6,128,128]{3,2,1,0:T(8,128)S(1)} %widen.1.refs_1_.refs_2_.refs_5_), custom_call_target="tpu_custom_call" | custom-call | flops 12288000 | bytes 1048576 | tf_op jit(solution)/shard_map/volume_0/pallas_call | solution.py:367
  11.2 0.9 %collective-permute-done.2 = f32[4,2,2,8,128]{4,3,1,0,2:T(8,128)S(1)} collective-permute-done((f32[4,2,2,8,128]{4,3,1,0,2:T(8,128)S(1)}, f32[4,2,2,8,128]{4,3,1,0,2:T(8,128)S(1)}, u32[]{:S(2)}, u32[]{:S(2)}) %collective-permute-start.2) | collective-permute-done | bytes 65568 | tf_op jit(solution)/shard_map/ppermute | solution.py:30
  12.2 2.3 %collective-permute-start.3 = (f32[4,4,1,8,128]{4,3,1,0,2:T(8,128)S(1)}, f32[4,4,1,8,128]{4,3,1,0,2:T(8,128)S(1)}, u32[]{:S(2)}, u32[]{:S(2)}) collective-permute-start(f32[4,4,1,8,128]{4,3,1,0,2:T(8,128)S(1)} %get-tuple-element.54), channel_id=1, source_target_pairs={{0,1},{1,2},{2,3},{3,0},{4,5},{5,6},{6,7},{7,4},{8,9},{9,10},{10,1... | collective-permute-start | bytes 196616 | tf_op jit(solution)/shard_map/ppermute | solution.py:34
  14.4 2.1 %collective-permute-start.4 = (f32[4,4,1,8,128]{4,3,1,0,2:T(8,128)S(1)}, f32[4,4,1,8,128]{4,3,1,0,2:T(8,128)S(1)}, u32[]{:S(2)}, u32[]{:S(2)}) collective-permute-start(f32[4,4,1,8,128]{4,3,1,0,2:T(8,128)S(1)} %get-tuple-element.55), channel_id=1, source_target_pairs={{1,0},{2,1},{3,2},{0,3},{5,4},{6,5},{7,6},{4,7},{9,8},{10,9},{11,1... | collective-permute-start | bytes 196616 | tf_op jit(solution)/shard_map/ppermute | solution.py:34
  16.5 2.2 %volume_1.1 = (f32[8,1,128,128]{3,2,1,0:T(8,128)S(1)}, s32[32]{0:T(128)S(1)}) custom-call(s32[8]{0:T(128)S(1)} %get-tuple-element.28.refs_0_.refs_1_, f32[32,8,128]{2,1,0:T(8,128)S(1)} %bitcast.22, f32[8,6,128,128]{3,2,1,0:T(8,128)S(1)} %widen.1.refs_1_.refs_2_.refs_5_, f32[8,1,128,128]{3,2,1,0:T(8,128)S(1)} %get-tuple-element.30.refs_3_), custom_call_target="tpu_custom_call" | custom-call | flops 12288000 | bytes 1048576 | tf_op jit(solution)/shard_map/volume_1/pallas_call | solution.py:367
  18.8 1.9 %collective-permute-done.4 = f32[4,4,1,8,128]{4,3,1,0,2:T(8,128)S(1)} collective-permute-done((f32[4,4,1,8,128]{4,3,1,0,2:T(8,128)S(1)}, f32[4,4,1,8,128]{4,3,1,0,2:T(8,128)S(1)}, u32[]{:S(2)}, u32[]{:S(2)}) %collective-permute-start.4) | collective-permute-done | bytes 65568 | tf_op jit(solution)/shard_map/ppermute | solution.py:34
  20.8 2.2 %volume_2.1 = (f32[8,1,128]{2,1,0:T(1,128)S(1)}, s32[32]{0:T(128)S(1)}) custom-call(s32[8]{0:T(128)S(1)} %get-tuple-element.28.refs_0_.refs_1_, f32[32,8,128]{2,1,0:T(8,128)S(1)} %pad_maximum_fusion.1.refs_1_.refs_6_, f32[8,6,128,128]{3,2,1,0:T(8,128)S(1)} %widen.1.refs_1_.refs_2_.refs_5_, f32[8,1,128,128]{3,2,1,0:T(8,128)S(1)} %get-tuple-element.33.refs_3_), custom_call_target="tpu_custom_call" | custom-call | flops 12288000 | bytes 1048576 | tf_op jit(solution)/shard_map/volume_2/pallas_call | solution.py:367
  23.2 1.7 %collective-permute-start.6 = (f32[1,2,2,1,128]{4,1,0,3,2:T(2,128)S(1)}, f32[1,2,2,1,128]{4,1,0,3,2:T(2,128)S(1)}, u32[]{:S(2)}, u32[]{:S(2)}) collective-permute-start(f32[1,2,2,1,128]{4,1,0,3,2:T(2,128)S(1)} %copy.13), channel_id=1, source_target_pairs={{8,0},{16,8},{24,16},{0,24},{9,1},{17,9},{25,17},{1,25},{10,2},{18... | collective-permute-start | bytes 6152 | tf_op jit(solution)/shard_map/ppermute | solution.py:34
  24.9 2.1 %arrange.1 = (f32[8,11,8,128]{3,2,1,0:T(8,128)S(1)}, s32[72]{0:T(128)S(1)}, s32[72]{0:T(128)S(1)}, s32[8]{0:T(128)S(1)}, f32[8,13,8,128]{3,2,1,0:T(8,128)S(1)}, ...) custom-call(s32[216]{0:T(256)S(1)} %reshape.49.refs_0_, ...), custom_call_target="tpu_custom_call" | custom-call | flops 8192000 | bytes 1048576 | tf_op jit(solution)/shard_map/arrange/pallas_call | solution.py:367
  27.1 1.4 %collective-permute-start.7 = (f32[4,2,2,1,128]{4,1,0,3,2:T(2,128)S(1)}, f32[4,2,2,1,128]{4,1,0,3,2:T(2,128)S(1)}, u32[]{:S(2)}, u32[]{:S(2)}) collective-permute-start(f32[4,2,2,1,128]{4,1,0,3,2:T(2,128)S(1)} %constant_dynamic-update-slice_fusion.2), channel_id=1, source_target_pairs={{0,4},{4,0},{1,5},{5,1},{2,6},{6,2},{3,7},{7,3},{8,12},{12,8},{9,1... | collective-permute-start | bytes 24584 | tf_op jit(solution)/shard_map/ppermute | solution.py:30
  28.5 1.5 %density_0.1.refs_7_ = f32[8,3,128,128]{3,2,1,0:T(8,128)S(1)} custom-call(s32[8]{0:T(128)S(1)} %get-tuple-element.28.refs_0_.refs_1_, s32[72]{0:T(128)S(1)} %get-tuple-element.43.refs_1_, s32[72]{0:T(128)S(1)} %get-tuple-element.44.refs_2_, s32[8]{0:T(128)S(1)} %get-tuple-element.45.refs_3_, f32[8,11,8,128]{3,2,1,0:T(8,128)S(1)} %get-tuple-element.40.refs_4_, ...), custom_call_target="tpu_custom_call" | custom-call | flops 16384000 | bytes 1048576 | tf_op jit(solution)/shard_map/density_0/pallas_call | solution.py:367
  30.9 1.1 %collective-permute-start.8 = (f32[4,4,1,1,128]{4,1,0,3,2:T(4,128)S(1)}, f32[4,4,1,1,128]{4,1,0,3,2:T(4,128)S(1)}, u32[]{:S(2)}, u32[]{:S(2)}) collective-permute-start(f32[4,4,1,1,128]{4,1,0,3,2:T(4,128)S(1)} %get-tuple-element.66), channel_id=1, source_target_pairs={{0,1},{1,2},{2,3},{3,0},{4,5},{5,6},{6,7},{7,4},{8,9},{9,10},{10,1... | collective-permute-start | bytes 24584 | tf_op jit(solution)/shard_map/ppermute | solution.py:34
  32.0 2.8 %collective-permute-start.9 = (f32[4,4,1,1,128]{4,1,0,3,2:T(4,128)S(1)}, f32[4,4,1,1,128]{4,1,0,3,2:T(4,128)S(1)}, u32[]{:S(2)}, u32[]{:S(2)}) collective-permute-start(f32[4,4,1,1,128]{4,1,0,3,2:T(4,128)S(1)} %get-tuple-element.67), channel_id=1, source_target_pairs={{1,0},{2,1},{3,2},{0,3},{5,4},{6,5},{7,6},{4,7},{9,8},{10,9},{11,1... | collective-permute-start | bytes 24584 | tf_op jit(solution)/shard_map/ppermute | solution.py:34
  34.8 1.9 %density_1.1.refs_7_ = f32[8,3,128,128]{3,2,1,0:T(8,128)S(1)} custom-call(s32[8]{0:T(128)S(1)} %get-tuple-element.28.refs_0_.refs_1_, s32[88]{0:T(128)S(1)} %get-tuple-element.47.refs_1_, s32[88]{0:T(128)S(1)} %get-tuple-element.48.refs_2_, s32[8]{0:T(128)S(1)} %get-tuple-element.49.refs_3_, f32[8,13,8,128]{3,2,1,0:T(8,128)S(1)} %get-tuple-element.41.refs_4_, ...), custom_call_target="tpu_custom_call" | custom-call | flops 16384000 | bytes 1048576 | tf_op jit(solution)/shard_map/density_1/pallas_call | solution.py:367
  36.8 2.4 %density_2.1.block_ref.refs_7_ = f32[8,4,128]{2,1,0:T(4,128)S(1)} custom-call(s32[8]{0:T(128)S(1)} %get-tuple-element.28.refs_0_.refs_1_, s32[80]{0:T(128)S(1)} %get-tuple-element.35.refs_1_, s32[80]{0:T(128)S(1)} %get-tuple-element.36.refs_2_, s32[8]{0:T(128)S(1)} %get-tuple-element.37.refs_3_, f32[8,12,8,128]{3,2,1,0:T(8,128)S(1)} %get-tuple-element.38.refs_4_, ...), custom_call_target="tpu_custom_call" | custom-call | flops 16384000 | bytes 1048576 | tf_op jit(solution)/shard_map/density_2/pallas_call | solution.py:367
  39.2 1.7 %collective-permute-start.11 = (f32[1,2,2,4,128]{4,3,1,0,2:T(4,128)S(1)}, f32[1,2,2,4,128]{4,3,1,0,2:T(4,128)S(1)}, u32[]{:S(2)}, u32[]{:S(2)}) collective-permute-start(f32[1,2,2,4,128]{4,3,1,0,2:T(4,128)S(1)} %copy.17), channel_id=1, source_target_pairs={{8,0},{16,8},{24,16},{0,24},{9,1},{17,9},{25,17},{1,25},{10,2},{18... | collective-permute-start | bytes 24584 | tf_op jit(solution)/shard_map/ppermute | solution.py:34
  42.4 2.9 %collective-permute-start.12 = (f32[4,2,2,4,128]{4,3,1,0,2:T(4,128)S(1)}, f32[4,2,2,4,128]{4,3,1,0,2:T(4,128)S(1)}, u32[]{:S(2)}, u32[]{:S(2)}) collective-permute-start(f32[4,2,2,4,128]{4,3,1,0,2:T(4,128)S(1)} %constant_dynamic-update-slice_fusion.5), channel_id=1, source_target_pairs={{0,4},{4,0},{1,5},{5,1},{2,6},{6,2},{3,7},{7,3},{8,12},{12,8},{9,1... | collective-permute-start | bytes 98312 | tf_op jit(solution)/shard_map/ppermute | solution.py:30
  45.3 1.7 %force_0.1.refs_8_ = f32[8,4,128,128]{3,2,1,0:T(8,128)S(1)} custom-call(s32[8]{0:T(128)S(1)} %get-tuple-element.28.refs_0_.refs_1_, s32[72]{0:T(128)S(1)} %get-tuple-element.43.refs_1_, s32[72]{0:T(128)S(1)} %get-tuple-element.44.refs_2_, s32[8]{0:T(128)S(1)} %get-tuple-element.45.refs_3_, f32[8,11,8,128]{3,2,1,0:T(8,128)S(1)} %get-tuple-element.40.refs_4_, ...), custom_call_target="tpu_custom_call" | custom-call | flops 20480000 | bytes 1048576 | tf_op jit(solution)/shard_map/force_0/pallas_call | solution.py:367
  47.4 4.3 %collective-permute-start.14 = (f32[4,4,1,4,128]{4,3,1,0,2:T(4,128)S(1)}, f32[4,4,1,4,128]{4,3,1,0,2:T(4,128)S(1)}, u32[]{:S(2)}, u32[]{:S(2)}) collective-permute-start(f32[4,4,1,4,128]{4,3,1,0,2:T(4,128)S(1)} %get-tuple-element.57), channel_id=1, source_target_pairs={{1,0},{2,1},{3,2},{0,3},{5,4},{6,5},{7,6},{4,7},{9,8},{10,9},{11,1... | collective-permute-start | bytes 98312 | tf_op jit(solution)/shard_map/ppermute | solution.py:34
  51.7 2.2 %force_1.1.refs_8_ = f32[8,4,128,128]{3,2,1,0:T(8,128)S(1)} custom-call(s32[8]{0:T(128)S(1)} %get-tuple-element.28.refs_0_.refs_1_, s32[88]{0:T(128)S(1)} %get-tuple-element.47.refs_1_, s32[88]{0:T(128)S(1)} %get-tuple-element.48.refs_2_, s32[8]{0:T(128)S(1)} %get-tuple-element.49.refs_3_, f32[8,13,8,128]{3,2,1,0:T(8,128)S(1)} %get-tuple-element.41.refs_4_, ...), custom_call_target="tpu_custom_call" | custom-call | flops 20480000 | bytes 1048576 | tf_op jit(solution)/shard_map/force_1/pallas_call | solution.py:367
  53.9 3.3 %force_2.1 = (f32[2,2,3,2,128]{4,3,2,1,0:T(2,128)}, f32[2,2,2,128]{3,2,1,0:T(2,128)}) custom-call(s32[8]{0:T(128)S(1)} %get-tuple-element.28.refs_0_.refs_1_, s32[80]{0:T(128)S(1)} %get-tuple-element.35.refs_1_, s32[80]{0:T(128)S(1)} %get-tuple-element.36.refs_2_, s32[8]{0:T(128)S(1)} %get-tuple-element.37.refs_3_, ...), custom_call_target="tpu_custom_call" | custom-call | flops 20480000 | bytes 1048576 | tf_op jit(solution)/shard_map/force_2/pallas_call | solution.py:367
  (65 shorter events, 7.2 us)
Async XLA Ops:
  0.6 0.7 %copy-start = (f32[2,2,2,3,128]{4,2,3,1,0:T(2,128)S(1)}, f32[2,2,2,3,128]{4,2,3,1,0:T(2,128)}, u32[]{:S(2)}) copy-start(f32[2,2,2,3,128]{4,2,3,1,0:T(2,128)} %param.6) | copy-start | bytes 36868
  1.3 0.7 %copy-start.1 = (f32[2,2,2,3,128]{4,2,3,1,0:T(2,128)S(1)}, f32[2,2,2,3,128]{4,2,3,1,0:T(2,128)}, u32[]{:S(2)}) copy-start(f32[2,2,2,3,128]{4,2,3,1,0:T(2,128)} %param.7) | copy-start | bytes 36868
  2.0 0.7 %copy-start.3 = (f32[2,2,2,128]{3,2,1,0:T(2,128)S(1)}, f32[2,2,2,128]{3,2,1,0:T(2,128)}, u32[]{:S(2)}) copy-start(f32[2,2,2,128]{3,2,1,0:T(2,128)} %mass_hbm.1) | copy-start | bytes 12292
  2.7 0.7 %copy-start.4 = (s32[2,2,2]{2,1,0:T(2,128)S(1)}, s32[2,2,2]{2,1,0:T(2,128)}, u32[]{:S(2)}) copy-start(s32[2,2,2]{2,1,0:T(2,128)} %counts_hbm.1) | copy-start | bytes 100
  3.6 3.9 %collective-permute-start = (f32[1,2,2,8,128]{4,3,1,0,2:T(8,128)S(1)}, f32[1,2,2,8,128]{4,3,1,0,2:T(8,128)S(1)}, u32[]{:S(2)}, u32[]{:S(2)}) collective-permute-start(f32[1,2,2,8,128]{4,3,1,0,2:T(8,128)S(1)} %copy.8), channel_id=1, source_target_pairs={{0,8},{8,16},{16,24},{24,0},{1,9},{9,17},{17,25},{25,1},{2,10},{10... | collective-permute-start | bytes 49160 | tf_op jit(solution)/shard_map/ppermute | solution.py:34
  4.1 3.5 %collective-permute-start.1 = (f32[1,2,2,8,128]{4,3,1,0,2:T(8,128)S(1)}, f32[1,2,2,8,128]{4,3,1,0,2:T(8,128)S(1)}, u32[]{:S(2)}, u32[]{:S(2)}) collective-permute-start(f32[1,2,2,8,128]{4,3,1,0,2:T(8,128)S(1)} %copy.9), channel_id=1, source_target_pairs={{8,0},{16,8},{24,16},{0,24},{9,1},{17,9},{25,17},{1,25},{10,2},{18... | collective-permute-start | bytes 49160 | tf_op jit(solution)/shard_map/ppermute | solution.py:34
  7.6 4.5 %collective-permute-start.2 = (f32[4,2,2,8,128]{4,3,1,0,2:T(8,128)S(1)}, f32[4,2,2,8,128]{4,3,1,0,2:T(8,128)S(1)}, u32[]{:S(2)}, u32[]{:S(2)}) collective-permute-start(f32[4,2,2,8,128]{4,3,1,0,2:T(8,128)S(1)} %constant_dynamic-update-slice_fusion), channel_id=1, source_target_pairs={{0,4},{4,0},{1,5},{5,1},{2,6},{6,2},{3,7},{7,3},{8,12},{12,8},{9,1... | collective-permute-start | bytes 196616 | tf_op jit(solution)/shard_map/ppermute | solution.py:30
  12.2 6.7 %collective-permute-start.3 = (f32[4,4,1,8,128]{4,3,1,0,2:T(8,128)S(1)}, f32[4,4,1,8,128]{4,3,1,0,2:T(8,128)S(1)}, u32[]{:S(2)}, u32[]{:S(2)}) collective-permute-start(f32[4,4,1,8,128]{4,3,1,0,2:T(8,128)S(1)} %get-tuple-element.54), channel_id=1, source_target_pairs={{0,1},{1,2},{2,3},{3,0},{4,5},{5,6},{6,7},{7,4},{8,9},{9,10},{10,1... | collective-permute-start | bytes 196616 | tf_op jit(solution)/shard_map/ppermute | solution.py:34
  14.4 6.3 %collective-permute-start.4 = (f32[4,4,1,8,128]{4,3,1,0,2:T(8,128)S(1)}, f32[4,4,1,8,128]{4,3,1,0,2:T(8,128)S(1)}, u32[]{:S(2)}, u32[]{:S(2)}) collective-permute-start(f32[4,4,1,8,128]{4,3,1,0,2:T(8,128)S(1)} %get-tuple-element.55), channel_id=1, source_target_pairs={{1,0},{2,1},{3,2},{0,3},{5,4},{6,5},{7,6},{4,7},{9,8},{10,9},{11,1... | collective-permute-start | bytes 196616 | tf_op jit(solution)/shard_map/ppermute | solution.py:34
  18.8 4.4 %copy-start.5 = (s32[2,2,2,27]{3,2,1,0:T(2,128)S(1)}, s32[2,2,2,27]{3,2,1,0:T(2,128)}, u32[]{:S(2)}) copy-start(s32[2,2,2,27]{3,2,1,0:T(2,128)} %param.10) | copy-start | bytes 2596
  23.0 4.1 %collective-permute-start.5 = (f32[1,2,2,1,128]{4,1,0,3,2:T(2,128)S(1)}, f32[1,2,2,1,128]{4,1,0,3,2:T(2,128)S(1)}, u32[]{:S(2)}, u32[]{:S(2)}) collective-permute-start(f32[1,2,2,1,128]{4,1,0,3,2:T(2,128)S(1)} %copy.12), channel_id=1, source_target_pairs={{0,8},{8,16},{16,24},{24,0},{1,9},{9,17},{17,25},{25,1},{2,10},{10... | collective-permute-start | bytes 6152 | tf_op jit(solution)/shard_map/ppermute | solution.py:34
  23.2 3.9 %collective-permute-start.6 = (f32[1,2,2,1,128]{4,1,0,3,2:T(2,128)S(1)}, f32[1,2,2,1,128]{4,1,0,3,2:T(2,128)S(1)}, u32[]{:S(2)}, u32[]{:S(2)}) collective-permute-start(f32[1,2,2,1,128]{4,1,0,3,2:T(2,128)S(1)} %copy.13), channel_id=1, source_target_pairs={{8,0},{16,8},{24,16},{0,24},{9,1},{17,9},{25,17},{1,25},{10,2},{18... | collective-permute-start | bytes 6152 | tf_op jit(solution)/shard_map/ppermute | solution.py:34
  27.1 3.7 %collective-permute-start.7 = (f32[4,2,2,1,128]{4,1,0,3,2:T(2,128)S(1)}, f32[4,2,2,1,128]{4,1,0,3,2:T(2,128)S(1)}, u32[]{:S(2)}, u32[]{:S(2)}) collective-permute-start(f32[4,2,2,1,128]{4,1,0,3,2:T(2,128)S(1)} %constant_dynamic-update-slice_fusion.2), channel_id=1, source_target_pairs={{0,4},{4,0},{1,5},{5,1},{2,6},{6,2},{3,7},{7,3},{8,12},{12,8},{9,1... | collective-permute-start | bytes 24584 | tf_op jit(solution)/shard_map/ppermute | solution.py:30
  30.9 5.8 %collective-permute-start.8 = (f32[4,4,1,1,128]{4,1,0,3,2:T(4,128)S(1)}, f32[4,4,1,1,128]{4,1,0,3,2:T(4,128)S(1)}, u32[]{:S(2)}, u32[]{:S(2)}) collective-permute-start(f32[4,4,1,1,128]{4,1,0,3,2:T(4,128)S(1)} %get-tuple-element.66), channel_id=1, source_target_pairs={{0,1},{1,2},{2,3},{3,0},{4,5},{5,6},{6,7},{7,4},{8,9},{9,10},{10,1... | collective-permute-start | bytes 24584 | tf_op jit(solution)/shard_map/ppermute | solution.py:34
  32.0 4.8 %collective-permute-start.9 = (f32[4,4,1,1,128]{4,1,0,3,2:T(4,128)S(1)}, f32[4,4,1,1,128]{4,1,0,3,2:T(4,128)S(1)}, u32[]{:S(2)}, u32[]{:S(2)}) collective-permute-start(f32[4,4,1,1,128]{4,1,0,3,2:T(4,128)S(1)} %get-tuple-element.67), channel_id=1, source_target_pairs={{1,0},{2,1},{3,2},{0,3},{5,4},{6,5},{7,6},{4,7},{9,8},{10,9},{11,1... | collective-permute-start | bytes 24584 | tf_op jit(solution)/shard_map/ppermute | solution.py:34
  34.8 2.0 %copy-start.2 = (f32[2,2,2,128]{3,2,1,0:T(2,128)S(1)}, f32[2,2,2,128]{3,2,1,0:T(2,128)}, u32[]{:S(2)}) copy-start(f32[2,2,2,128]{3,2,1,0:T(2,128)} %refs_10_.1) | copy-start | bytes 12292
  39.2 3.1 %collective-permute-start.10 = (f32[1,2,2,4,128]{4,3,1,0,2:T(4,128)S(1)}, f32[1,2,2,4,128]{4,3,1,0,2:T(4,128)S(1)}, u32[]{:S(2)}, u32[]{:S(2)}) collective-permute-start(f32[1,2,2,4,128]{4,3,1,0,2:T(4,128)S(1)} %copy.16), channel_id=1, source_target_pairs={{0,8},{8,16},{16,24},{24,0},{1,9},{9,17},{17,25},{25,1},{2,10},{10... | collective-permute-start | bytes 24584 | tf_op jit(solution)/shard_map/ppermute | solution.py:34
  39.2 3.1 %collective-permute-start.11 = (f32[1,2,2,4,128]{4,3,1,0,2:T(4,128)S(1)}, f32[1,2,2,4,128]{4,3,1,0,2:T(4,128)S(1)}, u32[]{:S(2)}, u32[]{:S(2)}) collective-permute-start(f32[1,2,2,4,128]{4,3,1,0,2:T(4,128)S(1)} %copy.17), channel_id=1, source_target_pairs={{8,0},{16,8},{24,16},{0,24},{9,1},{17,9},{25,17},{1,25},{10,2},{18... | collective-permute-start | bytes 24584 | tf_op jit(solution)/shard_map/ppermute | solution.py:34
  42.4 5.0 %collective-permute-start.12 = (f32[4,2,2,4,128]{4,3,1,0,2:T(4,128)S(1)}, f32[4,2,2,4,128]{4,3,1,0,2:T(4,128)S(1)}, u32[]{:S(2)}, u32[]{:S(2)}) collective-permute-start(f32[4,2,2,4,128]{4,3,1,0,2:T(4,128)S(1)} %constant_dynamic-update-slice_fusion.5), channel_id=1, source_target_pairs={{0,4},{4,0},{1,5},{5,1},{2,6},{6,2},{3,7},{7,3},{8,12},{12,8},{9,1... | collective-permute-start | bytes 98312 | tf_op jit(solution)/shard_map/ppermute | solution.py:30
  47.4 6.5 %collective-permute-start.13 = (f32[4,4,1,4,128]{4,3,1,0,2:T(4,128)S(1)}, f32[4,4,1,4,128]{4,3,1,0,2:T(4,128)S(1)}, u32[]{:S(2)}, u32[]{:S(2)}) collective-permute-start(f32[4,4,1,4,128]{4,3,1,0,2:T(4,128)S(1)} %get-tuple-element.56), channel_id=1, source_target_pairs={{0,1},{1,2},{2,3},{3,0},{4,5},{5,6},{6,7},{7,4},{8,9},{9,10},{10,1... | collective-permute-start | bytes 98312 | tf_op jit(solution)/shard_map/ppermute | solution.py:34
  47.4 6.5 %collective-permute-start.14 = (f32[4,4,1,4,128]{4,3,1,0,2:T(4,128)S(1)}, f32[4,4,1,4,128]{4,3,1,0,2:T(4,128)S(1)}, u32[]{:S(2)}, u32[]{:S(2)}) collective-permute-start(f32[4,4,1,4,128]{4,3,1,0,2:T(4,128)S(1)} %get-tuple-element.57), channel_id=1, source_target_pairs={{1,0},{2,1},{3,2},{0,3},{5,4},{6,5},{7,6},{4,7},{9,8},{10,9},{11,1... | collective-permute-start | bytes 98312 | tf_op jit(solution)/shard_map/ppermute | solution.py:34
where the time goes:
time: 58.3 us; the launch traced here: 57.3 us
  starting transfers between devices  25.3 us (43%)
  Pallas kernels  22.3 us (38%)
  waiting for transfers between devices  5.61 us (10%)
  local copies, waits for them, and re-layouts  3.01 us (5%)
  between operations  0.98 us (2%)
    pallas_call x12, Pallas kernels, call(): pl.pallas_call(body, out_shape=outs, in_specs=[spec(x) for x in inputs],...  22.1 us
    ppermute x6, starting transfers between devices, ends_of(): lax.ppermute(first, axis, backward)  14.6 us
    ppermute x3, starting transfers between devices, ends_of(): ends = lax.ppermute(ends, axis, [(0, 1), (1, 0)])  6.55 us
    ppermute x6, starting transfers between devices, ends_of(): lax.ppermute(last, axis, forward)  4.12 us
    unnamed x18, local copies, waits for them, and re-layouts  2.82 us
    ppermute x3, waiting for transfers between devices, ends_of(): ends = lax.ppermute(ends, axis, [(0, 1), (1, 0)])  2.17 us
    ppermute x6, waiting for transfers between devices, ends_of(): lax.ppermute(first, axis, backward)  2.06 us
    ppermute x6, waiting for transfers between devices, ends_of(): lax.ppermute(last, axis, forward)  1.38 us
  transfers between devices with their start and end apart: 15, of which 7 were waited for; matrix products, arithmetic and copies ran while one was open for 0% of the time, Pallas kernels for 25%

commit v1 on v0

--- a/solution.py
+++ b/solution.py
@@ -13,7 +13,6 @@
 TINY = 1e-30
 ROOM = 6 << 20
 GROUP = 4
-AHEAD = 2
 WIDE = (0, 1, 2, 4, 5, 6)
 OFFSETS = tuple(itertools.product((-1, 0, 1), repeat=3))
 
@@ -29,9 +28,16 @@
         ends = block if size == 2 else jnp.concatenate([first, last], axis=dim)
         ends = lax.ppermute(ends, axis, [(0, 1), (1, 0)])
         return lax.slice_in_dim(ends, 1, 2, axis=dim), lax.slice_in_dim(ends, 0, 1, axis=dim)
-    forward = [(i, (i + 1) % count) for i in range(count)]
-    backward = [(target, source) for source, target in forward]
-    return lax.ppermute(last, axis, forward), lax.ppermute(first, axis, backward)
+    if count % 2:
+        forward = [(i, (i + 1) % count) for i in range(count)]
+        backward = [(target, source) for source, target in forward]
+        return lax.ppermute(last, axis, forward), lax.ppermute(first, axis, backward)
+    even = lax.axis_index(axis) % 2 == 0
+    near_pairs = [(i, i + 1 - 2 * (i % 2)) for i in range(count)]
+    far_pairs = [(i, (i - 1 + 2 * (i % 2)) % count) for i in range(count)]
+    one = lax.ppermute(jnp.where(even, last, first), axis, near_pairs)
+    two = lax.ppermute(jnp.where(even, first, last), axis, far_pairs)
+    return jnp.where(even, two, one), jnp.where(even, one, two)
 
 
 def after(block, *others):
@@ -101,26 +107,13 @@
     )
 
 
-def prepare_kernel(counts_hbm, offsets_hbm, velocity_hbm, mass_hbm, out_ref, *scratch):
-    sources = (counts_hbm, offsets_hbm, velocity_hbm, mass_hbm)
-    holds, sems = scratch[:4], scratch[4]
-    copies = [
-        pltpu.make_async_copy(source, hold, sems.at[i])
-        for i, (source, hold) in enumerate(zip(sources, holds))
-    ]
-    for copy in copies:
-        copy.start()
-    for copy in copies:
-        copy.wait()
-    counts_ref, offsets_ref, velocity_ref, mass_ref = holds
-    nx, ny, nz = mass_ref.shape[:3]
+def prepare_kernel(counts_ref, base_ref, out_ref):
+    nx, ny, channels, nz, slots = base_ref.shape
     for leaf, (x, y, z) in enumerate(itertools.product(range(nx), range(ny), range(nz))):
-        for c in range(3):
-            out_ref[leaf, c : c + 1, :] = offsets_ref[x, y, c, z : z + 1, :]
-            out_ref[leaf, 4 + c : 5 + c, :] = velocity_ref[x, y, c, z : z + 1, :]
-        out_ref[leaf, 3:4, :] = mass_ref[x, y, z : z + 1, :]
+        for c in range(channels):
+            out_ref[leaf, c : c + 1, :] = base_ref[x, y, c, z : z + 1, :]
         number = counts_ref[x, y : y + 1, z : z + 1].astype(jnp.float32)
-        out_ref[leaf, 7:8, :] = jnp.broadcast_to(number, (1, mass_ref.shape[3]))
+        out_ref[leaf, channels : channels + 1, :] = jnp.broadcast_to(number, (1, slots))
 
 
 def partners(grid):
@@ -146,7 +139,7 @@
 
 
 def list_tiles(part):
-    return longest(part) + 1 + AHEAD
+    return longest(part) + 2
 
 
 def split_place(start):
@@ -161,8 +154,6 @@
 
 def close(list_ref, leaf, shift, tile, tail, lanes):
     pltpu.store(list_ref.at[leaf, tile], tail, mask=lanes >= shift)
-    for step in range(1, AHEAD):
-        list_ref[leaf, tile + step] = tail
 
 
 def lane_ids(rows):
@@ -182,16 +173,17 @@
             start = start + size_of(leaf, k, place)
         shift, tile = split_place(start)
         note(leaf, len(found), shift, tile)
-        note(leaf, None, shift, tile)
+        note(leaf, None, None, split_place(start + 127)[1])
         close(list_ref, leaf, shift, tile, far, lanes)
 
 
-def pack_side(part, source_ref, side_ref, shift_ref, tile_ref, tail):
+def pack_side(part, span, source_ref, side_ref, shift_ref, tile_ref, tail):
     height = source_ref.shape[1]
     lanes = lane_ids(height)
     last = column_constant(tail, height)
     stride = longest(part) + 1
-    for leaf, found in enumerate(part):
+    for leaf in range(*span):
+        found = part[leaf]
         for index, (_, place) in enumerate(found):
             at = leaf * stride + index
             put(side_ref, leaf, shift_ref[at], tile_ref[at], source_ref[place], lanes)
@@ -206,33 +198,37 @@
             out_ref[leaf, index] = jnp.transpose(jnp.broadcast_to(row, (128, 128)))
 
 
-def arrange_kernel(parts, *refs):
-    mask_ref, refs = refs[0], refs[1:]
-    count = len(parts)
-    for i, part in enumerate(parts):
-        counts_ref, source_ref = refs[i], refs[count + i]
-        list_ref, shift_ref, tile_ref, last_ref = refs[2 * count + 4 * i : 2 * count + 4 * i + 4]
-        stride = longest(part) + 1
-
-        def size_of(leaf, k, place):
-            return counts_ref[place] * mask_ref[leaf * 27 + k]
-
-        def note(leaf, index, shift, tile):
-            if index is None:
-                last_ref[leaf] = tile
-            else:
-                shift_ref[leaf * stride + index] = shift
-                tile_ref[leaf * stride + index] = tile
-
-        pack_places(part, source_ref, list_ref, size_of, note)
-
-
-def run_pairs(grid, pair, n_sums, count_of, last_of, own_of, row_of, before_ref, acc_ref):
+def read_counts(source_ref, counts_ref):
+    for place in range(source_ref.shape[0]):
+        counts_ref[place] = source_ref[place, 7:8, :].astype(jnp.int32)[0, 0]
+
+
+def pack_masked(part, mask_ref, counts_ref, source_ref, list_ref, shift_ref, tile_ref, last_ref):
+    stride = longest(part) + 1
+
+    def size_of(leaf, k, place):
+        return counts_ref[place] * mask_ref[leaf * 27 + k]
+
+    def note(leaf, index, shift, tile):
+        if index is None:
+            last_ref[leaf] = tile
+        else:
+            shift_ref[leaf * stride + index] = shift
+            tile_ref[leaf * stride + index] = tile
+
+    pack_places(part, source_ref, list_ref, size_of, note)
+
+
+def arrange_kernel(part, mask_ref, counts_ref, source_ref, *outs):
+    pack_masked(part, mask_ref, counts_ref, source_ref, *outs)
+
+
+def run_pairs(span, pair, n_sums, count_of, tiles_of, own_of, row_of, before_ref, acc_ref):
     zero = jnp.zeros((8, 128), jnp.float32)
 
     def leaf_step(leaf, carry):
         count = count_of(leaf)
-        steps = lax.shift_right_logical(last_of(leaf) + AHEAD, AHEAD.bit_length() - 1)
+        tiles = tiles_of(leaf)
 
         def group_step(group, carry):
             places = [
@@ -240,27 +236,26 @@
             ]
             owns = [own_of(leaf, at) for at in places]
 
-            def partner_step(step, sums):
-                for more in range(AHEAD):
-                    rows = {}
-                    at = step * AHEAD + more
-
-                    def row(c):
-                        if c not in rows:
-                            rows[c] = jnp.broadcast_to(row_of(leaf, at, c), (8, 128))
-                        return rows[c]
-
-                    terms = [pair(own, row) for own in owns]
-                    sums = tuple(
-                        tuple(a + b for a, b in zip(old, new)) for old, new in zip(sums, terms)
-                    )
-                return sums
+            def add_tile(tile, sums):
+                rows = {}
+
+                def row(c):
+                    if c not in rows:
+                        rows[c] = jnp.broadcast_to(row_of(leaf, tile, c), (8, 128))
+                    return rows[c]
+
+                terms = [pair(own, row) for own in owns]
+                return tuple(tuple(a + b for a, b in zip(old, new)) for old, new in zip(sums, terms))
+
+            def two_tiles(step, sums):
+                return add_tile(2 * step + 1, add_tile(2 * step, sums))
 
             start = tuple(
                 tuple(zero if before_ref is None else before_ref[leaf, i, at, :] for i in range(n_sums))
                 for at in places
             )
-            sums = lax.fori_loop(0, steps, partner_step, start)
+            sums = lax.fori_loop(0, lax.shift_right_logical(tiles, 1), two_tiles, start)
+            sums = lax.fori_loop(0, tiles & 1, lambda _, sums: add_tile(tiles - 1, sums), sums)
             for part, at in enumerate(places):
                 for index in range(n_sums):
                     acc_ref[leaf, index, at, :] = sums[part][index]
@@ -269,15 +264,25 @@
         groups = lax.shift_right_logical(count + (8 * GROUP - 1), (8 * GROUP).bit_length() - 1)
         return lax.fori_loop(0, groups, group_step, carry)
 
-    lax.fori_loop(0, grid[0] * grid[1] * grid[2], leaf_step, 0)
+    lax.fori_loop(*span, leaf_step, 0)
+
+
+def lane_sums(blocks):
+    rows = []
+    left = lane_ids(128) < 64
+    for i in range(0, len(blocks) - 1, 2):
+        one, two = blocks[i : i + 2]
+        both = jnp.where(left, one, two) + pltpu.roll(jnp.where(left, two, one), 64, axis=1)
+        both = jnp.transpose(both)
+        rows += [jnp.sum(half, axis=0, keepdims=True) for half in (both[:64], both[64:])]
+    if len(blocks) % 2:
+        rows.append(jnp.sum(jnp.transpose(blocks[-1]), axis=0, keepdims=True))
+    return rows
 
 
 def leaf_totals(grid, acc_ref, counts_ref):
     for leaf, index in enumerate(itertools.product(*map(range, grid))):
-        sums = [
-            jnp.sum(jnp.transpose(acc_ref[leaf, i]), axis=0, keepdims=True)
-            for i in range(acc_ref.shape[1])
-        ]
+        sums = lane_sums([acc_ref[leaf, i] for i in range(acc_ref.shape[1])])
         yield index, leaf, sums, lax.broadcasted_iota(jnp.int32, (1, 128), 1) < counts_ref[leaf]
 
 
@@ -299,34 +304,40 @@
 
 def volume_kernel(grid, part, stage, *refs):
     refs = list(refs)
-    out_ref, counts_ref, list_ref, last_ref = refs[-4:] if stage < 2 else refs[-5:-1]
+    centers_ref = refs.pop(0) if stage else None
+    mask_ref = refs.pop(0) if stage < 2 else None
+    source_ref, wide_ref = refs[:2]
+    before_ref = refs[2] if stage else None
+    out_ref, counts_ref, *masked_refs = refs[3 if stage else 2 :]
+    list_ref, last_ref = masked_refs[-2:] if stage < 2 else masked_refs[-3:-1]
     acc_ref = out_ref if stage < 2 else refs[-1]
-    centers_ref = refs.pop(0) if stage else counts_ref
-    source_ref, wide_ref = refs[:2]
-    for place in range(source_ref.shape[0]):
-        counts_ref[place] = source_ref[place, 7:8, :].astype(jnp.int32)[0, 0]
+    if centers_ref is None:
+        centers_ref = counts_ref
+    read_counts(source_ref, counts_ref)
 
     def note(leaf, index, shift, tile):
         if index is None:
             last_ref[leaf] = tile
 
     pack_places(part, source_ref, list_ref, lambda leaf, k, place: counts_ref[place], note)
+    if stage < 2:
+        pack_masked(part, mask_ref, counts_ref, source_ref, *masked_refs[:4])
     run_pairs(
-        grid, volume_pair, 1, lambda leaf: centers_ref[leaf], lambda leaf: last_ref[leaf],
-        own_reader((wide_ref, WIDE)), row_reader(list_ref), refs[2] if stage else None, acc_ref,
+        (0, len(part)), volume_pair, 1, lambda leaf: centers_ref[leaf], lambda leaf: last_ref[leaf],
+        own_reader((wide_ref, WIDE)), row_reader(list_ref), before_ref, acc_ref,
     )
     if stage == 2:
         for index, leaf, sums, valid in leaf_totals(grid, acc_ref, centers_ref):
             out_ref[leaf] = jnp.where(valid, 1.0 / (1.0 + 4.0 * sums[0]), 1.0)
 
 
-def density_kernel(grid, part, stage, *refs):
+def density_kernel(grid, part, stage, span, *refs):
     counts_ref, shift_ref, tile_ref, last_ref, list_ref, wide_ref, source_ref = refs[:7]
     out_ref, side_ref = refs[-2:] if stage < 2 else refs[-3:-1]
     acc_ref = out_ref if stage < 2 else refs[-1]
-    pack_side(part, source_ref, side_ref, shift_ref, tile_ref, ())
+    pack_side(part, span, source_ref, side_ref, shift_ref, tile_ref, ())
     run_pairs(
-        grid, density_pair, 3, lambda leaf: counts_ref[leaf], lambda leaf: last_ref[leaf],
+        span, density_pair, 3, lambda leaf: counts_ref[leaf], lambda leaf: last_ref[leaf],
         own_reader((wide_ref, WIDE)), row_reader(list_ref, side_ref, 7), refs[7] if stage else None, acc_ref,
     )
     if stage == 2:
@@ -341,13 +352,13 @@
             out_ref[leaf, 3:4, :] = jnp.zeros_like(density)
 
 
-def force_kernel(grid, part, stage, *refs):
+def force_kernel(grid, part, stage, span, *refs):
     counts_ref, shift_ref, tile_ref, last_ref, list_ref, wide_ref, state_ref, source_ref = refs[:8]
     side_ref = refs[-1] if stage < 2 else refs[-2]
     acc_ref = refs[-2] if stage < 2 else refs[-1]
-    pack_side(part, source_ref, side_ref, shift_ref, tile_ref, (1.0,))
+    pack_side(part, span, source_ref, side_ref, shift_ref, tile_ref, (1.0,))
     run_pairs(
-        grid, force_pair, 4, lambda leaf: counts_ref[leaf], lambda leaf: last_ref[leaf],
+        span, force_pair, 4, lambda leaf: counts_ref[leaf], lambda leaf: last_ref[leaf],
         own_reader((wide_ref, WIDE), (state_ref, (8, 9, 10))), row_reader(list_ref, side_ref),
         refs[8] if stage else None, acc_ref,
     )
@@ -359,7 +370,7 @@
             heat_ref[x, y, z : z + 1, :] = jnp.where(valid, -20.0 * sums[3], 0.0)
 
 
-def call(name, body, inputs, outs, scratch=(), cycles=0):
+def call(name, body, inputs, outs, scratch=(), cycles=0, aliases=()):
     def spec(x):
         scalar = x.dtype == jnp.int32 and len(x.shape) == 1
         return pl.BlockSpec(memory_space=pltpu.SMEM if scalar else pltpu.VMEM)
@@ -370,6 +381,7 @@
         in_specs=[spec(x) for x in inputs],
         out_specs=[spec(x) for x in outs],
         scratch_shapes=scratch,
+        input_output_aliases=dict(aliases),
         compiler_params=pltpu.CompilerParams(vmem_limit_bytes=ROOM),
         cost_estimate=pl.CostEstimate(flops=cycles * 4096, bytes_accessed=1 << 20, transcendentals=0),
         name=name,
@@ -394,16 +406,9 @@
     assert slots == 128
     leaves = grid[0] * grid[1] * grid[2]
     parts = partners(grid)
-    inputs = (counts, jnp.swapaxes(offsets, 2, 3), jnp.swapaxes(velocity, 2, 3), mass)
-    own = pl.pallas_call(
-        prepare_kernel,
-        out_shape=floats(leaves, 8, slots),
-        in_specs=[pl.BlockSpec(memory_space=pltpu.HBM)] * 4,
-        out_specs=pl.BlockSpec(memory_space=pltpu.VMEM),
-        scratch_shapes=[pltpu.VMEM(x.shape, x.dtype) for x in inputs] + [pltpu.SemaphoreType.DMA((4,))],
-        compiler_params=pltpu.CompilerParams(vmem_limit_bytes=ROOM),
-        name="prepare",
-    )(*inputs)
+    pieces = [jnp.swapaxes(x, 2, 3) for x in (offsets, mass[:, :, :, None], velocity)]
+    base = jnp.concatenate(pieces, axis=2)
+    own = call("prepare", prepare_kernel, [counts, base], [floats(leaves, 8, slots)])[0]
     mask = partner_mask.reshape(-1)
     wide = call(
         "widen", functools.partial(widen_kernel, WIDE), [own],
@@ -417,48 +422,52 @@
         shape = (leaves, n_sums, slots, slots)
         return ([floats(*shape)], []) if p < 2 else ([], [pltpu.VMEM(shape, jnp.float32)])
 
-    def volume_part(p, source, centers=(), before=()):
+    def masked_list(p):
+        part = parts[p]
+        stride = longest(part) + 1
+        return [
+            floats(leaves, list_tiles(part), 8, slots),
+            integers(leaves * stride), integers(leaves * stride), integers(leaves),
+        ]
+
+    near_counts, lists, early = [], [], []
+
+    def volume_part(p, source, more=()):
         outs, own_space = spread_sums(p, 1)
-        return call(
+        outs = (outs or [floats(leaves, 1, slots)]) + [integers(source.shape[0])]
+        if p < 2:
+            outs += masked_list(p)
+        out, number, *packed = call(
             f"volume_{p}", functools.partial(volume_kernel, grid, parts[p], p),
-            [*centers, source, wide, *before],
-            (outs or [floats(leaves, 1, slots)]) + [integers(source.shape[0])],
+            near_counts[:1] + ([mask] if p < 2 else []) + [source, wide, *more], outs,
             [packed_space(p, 8), pltpu.SMEM((leaves,), jnp.int32)] + own_space, cycles=3000,
         )
-
-    near_counts, lists, early = [], [], []
+        near_counts.append(number)
+        if packed:
+            lists.append(packed)
+        return out
 
     def volume_own():
-        part, number = volume_part(0, own)
-        near_counts.append(number)
-        early.append(part)
-        return (part,)
+        early.append(volume_part(0, own))
+        return tuple(early)
 
     layers, ends = exchange(own.reshape(grid + (8, slots)), lambda: (wide,), volume_own)
-    part, number = volume_part(1, layers, near_counts, early)
-    volume, last_number = volume_part(2, ends, near_counts, [part])
-    near_counts += [number, last_number]
+    volume = volume_part(2, ends, [volume_part(1, layers, early)])
 
     def arrange():
-        outs = []
-        for part in parts:
-            stride = longest(part) + 1
-            outs += [
-                floats(leaves, list_tiles(part), 8, slots),
-                integers(leaves * stride), integers(leaves * stride), integers(leaves),
-            ]
-        done = call(
-            "arrange", functools.partial(arrange_kernel, parts), [mask, *near_counts, own, layers, ends],
-            outs, cycles=2000,
+        lists.append(
+            call(
+                "arrange", functools.partial(arrange_kernel, parts[2]), [mask, near_counts[2], ends],
+                masked_list(2), cycles=1000,
+            )
         )
-        lists.extend(tuple(done[4 * p : 4 * p + 4]) for p in range(3))
-        return tuple(entry[0] for entry in lists)
-
-    def density_part(p, source, more=()):
+        return (lists[2][0],)
+
+    def density_part(p, source, more=(), span=(0, leaves)):
         packed, shifts, starts, last = lists[p]
         outs, own_space = spread_sums(p, 3)
         return call(
-            f"density_{p}", functools.partial(density_kernel, grid, parts[p], p),
+            f"density_{p}", functools.partial(density_kernel, grid, parts[p], p, span),
             [near_counts[0], shifts, starts, last, packed, wide, source, *more],
             outs or [floats(leaves, 4, slots)], [packed_space(p, 1)] + own_space, cycles=4000,
         )[0]
@@ -476,21 +485,28 @@
         [floats(leaves, 3, slots, slots)], cycles=1000,
     )[0]
 
-    def force_part(p, source, more=()):
+    def force_part(p, source, more=(), span=(0, leaves)):
         packed, shifts, starts, last = lists[p]
         outs, own_space = spread_sums(p, 4)
         return call(
-            f"force_{p}", functools.partial(force_kernel, grid, parts[p], p),
+            f"force_{p}", functools.partial(force_kernel, grid, parts[p], p, span),
             [near_counts[0], shifts, starts, last, packed, wide, wide_state, source, *more],
             outs or [floats(*grid[:2], 3, grid[2], slots), floats(*grid, slots)],
             [packed_space(p, 4)] + own_space, cycles=5000,
+            aliases=[(8, 0)] if p == 0 and more else (),
         )
 
-    def force_own():
-        early[:] = force_part(0, state)
-        return tuple(early)
-
-    state_layers, state_ends = exchange(state.reshape(grid + (4, slots)), lambda: (wide_state,), force_own)
+    def force_own(span):
+        def run():
+            early[:] = force_part(0, state, early if span[0] else (), span)
+            return tuple(early)
+
+        return run
+
+    cut = 3 * leaves // 8
+    state_layers, state_ends = exchange(
+        state.reshape(grid + (4, slots)), force_own((0, cut)), force_own((cut, leaves))
+    )
     push, heat = force_part(2, state_ends, force_part(1, state_layers, early))
     return jnp.swapaxes(push, 2, 3), heat
 

time: 58.3 us -> 55.7 us (0.955)
  starting transfers between devices: 25.3 us -> 18.3 us
  Pallas kernels: 22.3 us -> 25.8 us
  waiting for transfers between devices: 5.61 us -> 7.98 us
  local copies, waits for them, and re-layouts: 3.01 us -> 0.84 us
  other arithmetic: 0.09 us -> 0.98 us
    ppermute x12, starting transfers between devices: 18.7 us -> 14.3 us  [the longest x6 11.4 us: ends_of(): two = lax.ppermute(jnp.where(even, first, last), axis, far_pairs)]
    pallas_call x12 -> x14, Pallas kernels: 22.1 us -> 25.8 us  [call(): pl.pallas_call(body, out_shape=outs, in_specs=[spec(x) for x in inputs],...]
    ppermute x3, starting transfers between devices: 6.55 us -> 4.03 us  [ends_of(): ends = lax.ppermute(ends, axis, [(0, 1), (1, 0)])]
    ppermute x12, waiting for transfers between devices: 3.44 us -> 5.7 us  [the longest x6 3.36 us: ends_of(): two = lax.ppermute(jnp.where(even, first, last), axis, far_pairs)]
    unnamed x18 -> x6, local copies, waits for them, and re-layouts: 2.82 us -> 0.69 us
    concatenate x0 -> x4, other arithmetic: none -> 0.79 us  [the longest x1 0.76 us: shards(): base = jnp.concatenate(pieces, axis=2)]
  transfers between devices with their start and end apart: 15 -> 15, of which waited for: 7 -> 9; matrix products, arithmetic and copies ran while one was open for 0% -> 0% of each run, Pallas kernels for 25% -> 30%
where the time goes in v1:
time: 55.7 us; the launch traced here: 54.9 us
  Pallas kernels  25.8 us (46%)
  starting transfers between devices  18.3 us (33%)
  waiting for transfers between devices  7.98 us (14%)
  other arithmetic  0.98 us (2%)
  between operations  0.98 us (2%)
  local copies, waits for them, and re-layouts  0.84 us (2%)
    pallas_call x14, Pallas kernels, call(): pl.pallas_call(body, out_shape=outs, in_specs=[spec(x) for x in inputs],...  25.8 us
    ppermute x6, starting transfers between devices, ends_of(): two = lax.ppermute(jnp.where(even, first, last), axis, far_pairs)  11.4 us
    ppermute x3, starting transfers between devices, ends_of(): ends = lax.ppermute(ends, axis, [(0, 1), (1, 0)])  4.03 us
    ppermute x6, waiting for transfers between devices, ends_of(): two = lax.ppermute(jnp.where(even, first, last), axis, far_pairs)  3.36 us
    ppermute x6, starting transfers between devices, ends_of(): one = lax.ppermute(jnp.where(even, last, first), axis, near_pairs)  2.93 us
    ppermute x6, waiting for transfers between devices, ends_of(): one = lax.ppermute(jnp.where(even, last, first), axis, near_pairs)  2.35 us
    ppermute x3, waiting for transfers between devices, ends_of(): ends = lax.ppermute(ends, axis, [(0, 1), (1, 0)])  2.28 us
  transfers between devices with their start and end apart: 15, of which 9 were waited for; matrix products, arithmetic and copies ran while one was open for 0% of the time, Pallas kernels for 30%

profile of v1, /device:TPU:0, one launch (start us, length us, event | category | flops | bytes accessed | tf_op | source)
XLA Modules:
  0.0 54.9 jit_solution(9475103280901673760)
XLA Ops:
  0.7 0.8 %pad_maximum_fusion.6.base_ref = f32[2,2,7,2,128]{4,3,2,1,0:T(2,128)S(1)} fusion(f32[2,2,3,2,128]{4,3,2,1,0:T(2,128)} %bitcast.58, f32[2,2,1,2,128]{4,3,2,1,0:T(2,128)} %bitcast.66, f32[2,2,3,2,128]{4,3,2,1,0:T(2,128)} %bitcast.59), kind=kLoop, calls=%fused_computation.12 | loop fusion | flops 14336 | bytes 57344 | tf_op jit(solution)/shard_map/concatenate | solution.py:410
  2.2 2.5 %collective-permute-start = (f32[1,2,2,8,128]{4,3,1,0,2:T(8,128)S(1)}, f32[1,2,2,8,128]{4,3,1,0,2:T(8,128)S(1)}, u32[]{:S(2)}, u32[]{:S(2)}) collective-permute-start(f32[1,2,2,8,128]{4,3,1,0,2:T(8,128)S(1)} %copy.9), channel_id=1, source_target_pairs={{0,24},{8,16},{16,8},{24,0},{1,25},{9,17},{17,9},{25,1},{2,26},{10... | collective-permute-start | bytes 49160 | tf_op jit(solution)/shard_map/ppermute | solution.py:39
  5.4 0.9 %widen.1.refs_2_.refs_3_.refs_5_ = f32[8,6,128,128]{3,2,1,0:T(8,128)S(1)} custom-call(f32[8,8,128]{2,1,0:T(8,128)S(1)} %prepare.1.block_ref.refs_1_.refs_8_), custom_call_target="tpu_custom_call" | custom-call | flops 8192000 | bytes 1048576 | tf_op jit(solution)/shard_map/widen/pallas_call | solution.py:378
  6.3 2.3 %collective-permute-start.2 = (f32[4,2,2,8,128]{4,3,1,0,2:T(8,128)S(1)}, f32[4,2,2,8,128]{4,3,1,0,2:T(8,128)S(1)}, u32[]{:S(2)}, u32[]{:S(2)}) collective-permute-start(f32[4,2,2,8,128]{4,3,1,0,2:T(8,128)S(1)} %pad_maximum_fusion.2), channel_id=1, source_target_pairs={{0,4},{4,0},{1,5},{5,1},{2,6},{6,2},{3,7},{7,3},{8,12},{12,8},{9,1... | collective-permute-start | bytes 196616 | tf_op jit(solution)/shard_map/ppermute | solution.py:29
  8.7 2.6 %volume_0.1 = (f32[8,1,128,128]{3,2,1,0:T(8,128)S(1)}, s32[8]{0:T(128)S(1)}, f32[8,10,8,128]{3,2,1,0:T(8,128)S(1)}, s32[72]{0:T(128)S(1)}, s32[72]{0:T(128)S(1)}, /*index=5*/s32[8]{0:T(128)S(1)}) custom-call(s32[216]{0:T(256)S(1)} %reshape.181.refs_0_.refs_1_.mask_ref, f32[8,8,128]{2,1,0:T(8,128)S(1)} %prepare.1.block_ref.refs_1_.refs_8_, ...), custom_call_target="tpu_custom_call" | custom-call | flops 12288000 | bytes 1048576 | tf_op jit(solution)/shard_map/volume_0/pallas_call | solution.py:378
  11.4 4.0 %collective-permute-start.3 = (f32[4,4,1,8,128]{4,3,1,0,2:T(8,128)S(1)}, f32[4,4,1,8,128]{4,3,1,0,2:T(8,128)S(1)}, u32[]{:S(2)}, u32[]{:S(2)}) collective-permute-start(f32[4,4,1,8,128]{4,3,1,0,2:T(8,128)S(1)} %get-tuple-element.54), channel_id=1, source_target_pairs={{0,3},{1,2},{2,1},{3,0},{4,7},{5,6},{6,5},{7,4},{8,11},{9,10},{10,... | collective-permute-start | bytes 196616 | tf_op jit(solution)/shard_map/ppermute | solution.py:39
  15.4 2.5 %volume_1.1 = (f32[8,1,128,128]{3,2,1,0:T(8,128)S(1)}, s32[32]{0:T(128)}, f32[8,12,8,128]{3,2,1,0:T(8,128)S(1)}, s32[88]{0:T(128)S(1)}, s32[88]{0:T(128)S(1)}, /*index=5*/s32[8]{0:T(128)S(1)}) custom-call(s32[8]{0:T(128)S(1)} %get-tuple-element.27.refs_0_, s32[216]{0:T(256)S(1)} %reshape.181.refs_0_.refs_1_.mask_ref, f32[32,8,128]{2,1,0:T(8,128)S(1)} %bitcast.38, ...), custom_call_target="tpu_custom_call" | custom-call | flops 12288000 | bytes 1048576 | tf_op jit(solution)/shard_map/volume_1/pallas_call | solution.py:378
  17.9 1.8 %collective-permute-done.4 = f32[4,4,1,8,128]{4,3,1,0,2:T(8,128)S(1)} collective-permute-done((f32[4,4,1,8,128]{4,3,1,0,2:T(8,128)S(1)}, f32[4,4,1,8,128]{4,3,1,0,2:T(8,128)S(1)}, u32[]{:S(2)}, u32[]{:S(2)}) %collective-permute-start.4) | collective-permute-done | bytes 65568 | tf_op jit(solution)/shard_map/ppermute | solution.py:38
  19.7 2.5 %volume_2.1 = (f32[8,1,128]{2,1,0:T(1,128)S(1)}, s32[32]{0:T(128)S(1)}) custom-call(s32[8]{0:T(128)S(1)} %get-tuple-element.27.refs_0_, f32[32,8,128]{2,1,0:T(8,128)S(1)} %pad_maximum_fusion.1.refs_1_.source_ref, f32[8,6,128,128]{3,2,1,0:T(8,128)S(1)} %widen.1.refs_2_.refs_3_.refs_5_, f32[8,1,128,128]{3,2,1,0:T(8,128)S(1)} %get-tuple-element.31.refs_3_), custom_call_target="tpu_custom_call" | custom-call | flops 12288000 | bytes 1048576 | tf_op jit(solution)/shard_map/volume_2/pallas_call | solution.py:378
  23.5 1.4 %arrange.1 = (f32[8,11,8,128]{3,2,1,0:T(8,128)S(1)}, s32[80]{0:T(128)S(1)}, s32[80]{0:T(128)S(1)}, s32[8]{0:T(128)S(1)}) custom-call(s32[216]{0:T(256)S(1)} %reshape.181.refs_0_.refs_1_.mask_ref, s32[32]{0:T(128)S(1)} %get-tuple-element.32.counts_ref, f32[32,8,128]{2,1,0:T(8,128)S(1)} %pad_maximum_fusion.1.refs_1_.source_ref), custom_call_target="tpu_custom_call" | custom-call | flops 4096000 | bytes 1048576 | tf_op jit(solution)/shard_map/arrange/pallas_call | solution.py:378
  25.3 1.0 %collective-permute-start.7 = (f32[4,2,2,1,128]{4,1,0,3,2:T(2,128)S(1)}, f32[4,2,2,1,128]{4,1,0,3,2:T(2,128)S(1)}, u32[]{:S(2)}, u32[]{:S(2)}) collective-permute-start(f32[4,2,2,1,128]{4,1,0,3,2:T(2,128)S(1)} %pad_maximum_fusion.9), channel_id=1, source_target_pairs={{0,4},{4,0},{1,5},{5,1},{2,6},{6,2},{3,7},{7,3},{8,12},{12,8},{9,1... | collective-permute-start | bytes 24584 | tf_op jit(solution)/shard_map/ppermute | solution.py:29
  26.3 2.1 %density_0.1.refs_7_ = f32[8,3,128,128]{3,2,1,0:T(8,128)S(1)} custom-call(s32[8]{0:T(128)S(1)} %get-tuple-element.27.refs_0_, s32[72]{0:T(128)S(1)} %get-tuple-element.39.refs_1_, s32[72]{0:T(128)S(1)} %get-tuple-element.40.refs_2_, s32[8]{0:T(128)S(1)} %get-tuple-element.41.refs_3_, f32[8,10,8,128]{3,2,1,0:T(8,128)S(1)} %get-tuple-element.42.refs_4_, ...), custom_call_target="tpu_custom_call" | custom-call | flops 16384000 | bytes 1048576 | tf_op jit(solution)/shard_map/density_0/pallas_call | solution.py:378
  29.1 2.1 %collective-permute-start.8 = (f32[4,4,1,1,128]{4,1,0,3,2:T(4,128)S(1)}, f32[4,4,1,1,128]{4,1,0,3,2:T(4,128)S(1)}, u32[]{:S(2)}, u32[]{:S(2)}) collective-permute-start(f32[4,4,1,1,128]{4,1,0,3,2:T(4,128)S(1)} %get-tuple-element.74), channel_id=1, source_target_pairs={{0,3},{1,2},{2,1},{3,0},{4,7},{5,6},{6,5},{7,4},{8,11},{9,10},{10,... | collective-permute-start | bytes 24584 | tf_op jit(solution)/shard_map/ppermute | solution.py:39
  31.9 1.8 %density_1.1.refs_7_ = f32[8,3,128,128]{3,2,1,0:T(8,128)S(1)} custom-call(s32[8]{0:T(128)S(1)} %get-tuple-element.27.refs_0_, s32[88]{0:T(128)S(1)} %get-tuple-element.44.refs_1_, s32[88]{0:T(128)S(1)} %get-tuple-element.45.refs_2_, s32[8]{0:T(128)S(1)} %get-tuple-element.46.refs_3_, f32[8,12,8,128]{3,2,1,0:T(8,128)S(1)} %get-tuple-element.47.refs_4_, ...), custom_call_target="tpu_custom_call" | custom-call | flops 16384000 | bytes 1048576 | tf_op jit(solution)/shard_map/density_1/pallas_call | solution.py:378
  33.7 0.9 %collective-permute-done.8 = f32[4,4,1,1,128]{4,1,0,3,2:T(4,128)S(1)} collective-permute-done((f32[4,4,1,1,128]{4,1,0,3,2:T(4,128)S(1)}, f32[4,4,1,1,128]{4,1,0,3,2:T(4,128)S(1)}, u32[]{:S(2)}, u32[]{:S(2)}) %collective-permute-start.8) | collective-permute-done | bytes 8224 | tf_op jit(solution)/shard_map/ppermute | solution.py:39
  34.9 2.8 %density_2.1.block_ref.refs_7_ = f32[8,4,128]{2,1,0:T(4,128)S(1)} custom-call(s32[8]{0:T(128)S(1)} %get-tuple-element.27.refs_0_, s32[80]{0:T(128)S(1)} %get-tuple-element.33.refs_1_, s32[80]{0:T(128)S(1)} %get-tuple-element.34.refs_2_, s32[8]{0:T(128)S(1)} %get-tuple-element.35.refs_3_, f32[8,11,8,128]{3,2,1,0:T(8,128)S(1)} %get-tuple-element.36.refs_4_, ...), custom_call_target="tpu_custom_call" | custom-call | flops 16384000 | bytes 1048576 | tf_op jit(solution)/shard_map/density_2/pallas_call | solution.py:378
  38.9 1.4 %force_0.2.refs_8_ = f32[8,4,128,128]{3,2,1,0:T(8,128)S(1)} custom-call(s32[8]{0:T(128)S(1)} %get-tuple-element.27.refs_0_, s32[72]{0:T(128)S(1)} %get-tuple-element.39.refs_1_, s32[72]{0:T(128)S(1)} %get-tuple-element.40.refs_2_, s32[8]{0:T(128)S(1)} %get-tuple-element.41.refs_3_, f32[8,10,8,128]{3,2,1,0:T(8,128)S(1)} %get-tuple-element.42.refs_4_, ...), custom_call_target="tpu_custom_call" | custom-call | flops 20480000 | bytes 1048576 | tf_op jit(solution)/shard_map/force_0/pallas_call | solution.py:378
  40.8 0.7 %collective-permute-start.12 = (f32[4,2,2,4,128]{4,3,1,0,2:T(4,128)S(1)}, f32[4,2,2,4,128]{4,3,1,0,2:T(4,128)S(1)}, u32[]{:S(2)}, u32[]{:S(2)}) collective-permute-start(f32[4,2,2,4,128]{4,3,1,0,2:T(4,128)S(1)} %pad_maximum_fusion.5), channel_id=1, source_target_pairs={{0,4},{4,0},{1,5},{5,1},{2,6},{6,2},{3,7},{7,3},{8,12},{12,8},{9,1... | collective-permute-start | bytes 98312 | tf_op jit(solution)/shard_map/ppermute | solution.py:29
  41.6 1.6 %force_0.3.refs_8_ = f32[8,4,128,128]{3,2,1,0:T(8,128)S(1)} custom-call(s32[8]{0:T(128)S(1)} %get-tuple-element.27.refs_0_, s32[72]{0:T(128)S(1)} %get-tuple-element.39.refs_1_, s32[72]{0:T(128)S(1)} %get-tuple-element.40.refs_2_, s32[8]{0:T(128)S(1)} %get-tuple-element.41.refs_3_, ...), custom_call_target="tpu_custom_call", output_to_operand_aliasing={{}: (8, {})} | custom-call | flops 20480000 | bytes 1048576 | tf_op jit(solution)/shard_map/force_0/pallas_call | solution.py:378
  43.2 1.7 %collective-permute-done.12 = f32[4,2,2,4,128]{4,3,1,0,2:T(4,128)S(1)} collective-permute-done((f32[4,2,2,4,128]{4,3,1,0,2:T(4,128)S(1)}, f32[4,2,2,4,128]{4,3,1,0,2:T(4,128)S(1)}, u32[]{:S(2)}, u32[]{:S(2)}) %collective-permute-start.12) | collective-permute-done | bytes 32800 | tf_op jit(solution)/shard_map/ppermute | solution.py:29
  44.9 2.0 %collective-permute-start.13 = (f32[4,4,1,4,128]{4,3,1,0,2:T(4,128)S(1)}, f32[4,4,1,4,128]{4,3,1,0,2:T(4,128)S(1)}, u32[]{:S(2)}, u32[]{:S(2)}) collective-permute-start(f32[4,4,1,4,128]{4,3,1,0,2:T(4,128)S(1)} %get-tuple-element.58), channel_id=1, source_target_pairs={{0,3},{1,2},{2,1},{3,0},{4,7},{5,6},{6,5},{7,4},{8,11},{9,10},{10,... | collective-permute-start | bytes 98312 | tf_op jit(solution)/shard_map/ppermute | solution.py:39
  47.1 2.0 %force_1.1.refs_8_ = f32[8,4,128,128]{3,2,1,0:T(8,128)S(1)} custom-call(s32[8]{0:T(128)S(1)} %get-tuple-element.27.refs_0_, s32[88]{0:T(128)S(1)} %get-tuple-element.44.refs_1_, s32[88]{0:T(128)S(1)} %get-tuple-element.45.refs_2_, s32[8]{0:T(128)S(1)} %get-tuple-element.46.refs_3_, f32[8,12,8,128]{3,2,1,0:T(8,128)S(1)} %get-tuple-element.47.refs_4_, ...), custom_call_target="tpu_custom_call" | custom-call | flops 20480000 | bytes 1048576 | tf_op jit(solution)/shard_map/force_1/pallas_call | solution.py:378
  49.1 1.6 %collective-permute-done.13 = f32[4,4,1,4,128]{4,3,1,0,2:T(4,128)S(1)} collective-permute-done((f32[4,4,1,4,128]{4,3,1,0,2:T(4,128)S(1)}, f32[4,4,1,4,128]{4,3,1,0,2:T(4,128)S(1)}, u32[]{:S(2)}, u32[]{:S(2)}) %collective-permute-start.13) | collective-permute-done | bytes 32800 | tf_op jit(solution)/shard_map/ppermute | solution.py:39
  51.0 3.8 %force_2.1 = (f32[2,2,3,2,128]{4,3,2,1,0:T(2,128)}, f32[2,2,2,128]{3,2,1,0:T(2,128)}) custom-call(s32[8]{0:T(128)S(1)} %get-tuple-element.27.refs_0_, s32[80]{0:T(128)S(1)} %get-tuple-element.33.refs_1_, s32[80]{0:T(128)S(1)} %get-tuple-element.34.refs_2_, s32[8]{0:T(128)S(1)} %get-tuple-element.35.refs_3_, f32[8,11,8,128]{3,2,1,0:T(8,128)S(1)} %get-tuple-element.36.refs_4_, ...), custom_call_target="tpu_custom_call" | custom-call | flops 20480000 | bytes 1048576 | tf_op jit(solution)/shard_map/force_2/pallas_call | solution.py:378
  (62 shorter events, 7.3 us)
Async XLA Ops:
  0.6 8.0 %copy-start.2 = (s32[2,2,2,27]{3,2,1,0:T(2,128)S(1)}, s32[2,2,2,27]{3,2,1,0:T(2,128)}, u32[]{:S(2)}) copy-start(s32[2,2,2,27]{3,2,1,0:T(2,128)} %param.10) | copy-start | bytes 2596
  1.4 0.7 %copy-start.1 = (s32[2,2,2]{2,1,0:T(2,128)S(1)}, s32[2,2,2]{2,1,0:T(2,128)}, u32[]{:S(2)}) copy-start(s32[2,2,2]{2,1,0:T(2,128)} %counts_ref.1) | copy-start | bytes 100
  2.2 4.1 %collective-permute-start = (f32[1,2,2,8,128]{4,3,1,0,2:T(8,128)S(1)}, f32[1,2,2,8,128]{4,3,1,0,2:T(8,128)S(1)}, u32[]{:S(2)}, u32[]{:S(2)}) collective-permute-start(f32[1,2,2,8,128]{4,3,1,0,2:T(8,128)S(1)} %copy.9), channel_id=1, source_target_pairs={{0,24},{8,16},{16,8},{24,0},{1,25},{9,17},{17,9},{25,1},{2,26},{10... | collective-permute-start | bytes 49160 | tf_op jit(solution)/shard_map/ppermute | solution.py:39
  4.7 1.6 %collective-permute-start.1 = (f32[1,2,2,8,128]{4,3,1,0,2:T(8,128)S(1)}, f32[1,2,2,8,128]{4,3,1,0,2:T(8,128)S(1)}, u32[]{:S(2)}, u32[]{:S(2)}) collective-permute-start(f32[1,2,2,8,128]{4,3,1,0,2:T(8,128)S(1)} %copy.10), channel_id=1, source_target_pairs={{0,8},{8,0},{16,24},{24,16},{1,9},{9,1},{17,25},{25,17},{2,10},{10... | collective-permute-start | bytes 49160 | tf_op jit(solution)/shard_map/ppermute | solution.py:38
  6.3 5.0 %collective-permute-start.2 = (f32[4,2,2,8,128]{4,3,1,0,2:T(8,128)S(1)}, f32[4,2,2,8,128]{4,3,1,0,2:T(8,128)S(1)}, u32[]{:S(2)}, u32[]{:S(2)}) collective-permute-start(f32[4,2,2,8,128]{4,3,1,0,2:T(8,128)S(1)} %pad_maximum_fusion.2), channel_id=1, source_target_pairs={{0,4},{4,0},{1,5},{5,1},{2,6},{6,2},{3,7},{7,3},{8,12},{12,8},{9,1... | collective-permute-start | bytes 196616 | tf_op jit(solution)/shard_map/ppermute | solution.py:29
  11.4 6.5 %collective-permute-start.3 = (f32[4,4,1,8,128]{4,3,1,0,2:T(8,128)S(1)}, f32[4,4,1,8,128]{4,3,1,0,2:T(8,128)S(1)}, u32[]{:S(2)}, u32[]{:S(2)}) collective-permute-start(f32[4,4,1,8,128]{4,3,1,0,2:T(8,128)S(1)} %get-tuple-element.54), channel_id=1, source_target_pairs={{0,3},{1,2},{2,1},{3,0},{4,7},{5,6},{6,5},{7,4},{8,11},{9,10},{10,... | collective-permute-start | bytes 196616 | tf_op jit(solution)/shard_map/ppermute | solution.py:39
  15.4 4.3 %collective-permute-start.4 = (f32[4,4,1,8,128]{4,3,1,0,2:T(8,128)S(1)}, f32[4,4,1,8,128]{4,3,1,0,2:T(8,128)S(1)}, u32[]{:S(2)}, u32[]{:S(2)}) collective-permute-start(f32[4,4,1,8,128]{4,3,1,0,2:T(8,128)S(1)} %get-tuple-element.55), channel_id=1, source_target_pairs={{0,1},{1,0},{2,3},{3,2},{4,5},{5,4},{6,7},{7,6},{8,9},{9,8},{10,11... | collective-permute-start | bytes 196616 | tf_op jit(solution)/shard_map/ppermute | solution.py:38
  22.2 3.1 %collective-permute-start.5 = (f32[1,2,2,1,128]{4,1,0,3,2:T(2,128)S(1)}, f32[1,2,2,1,128]{4,1,0,3,2:T(2,128)S(1)}, u32[]{:S(2)}, u32[]{:S(2)}) collective-permute-start(f32[1,2,2,1,128]{4,1,0,3,2:T(2,128)S(1)} %copy.13), channel_id=1, source_target_pairs={{0,24},{8,16},{16,8},{24,0},{1,25},{9,17},{17,9},{25,1},{2,26},{10... | collective-permute-start | bytes 6152 | tf_op jit(solution)/shard_map/ppermute | solution.py:39
  22.8 2.4 %collective-permute-start.6 = (f32[1,2,2,1,128]{4,1,0,3,2:T(2,128)S(1)}, f32[1,2,2,1,128]{4,1,0,3,2:T(2,128)S(1)}, u32[]{:S(2)}, u32[]{:S(2)}) collective-permute-start(f32[1,2,2,1,128]{4,1,0,3,2:T(2,128)S(1)} %copy.14), channel_id=1, source_target_pairs={{0,8},{8,0},{16,24},{24,16},{1,9},{9,1},{17,25},{25,17},{2,10},{10... | collective-permute-start | bytes 6152 | tf_op jit(solution)/shard_map/ppermute | solution.py:38
  25.3 3.7 %collective-permute-start.7 = (f32[4,2,2,1,128]{4,1,0,3,2:T(2,128)S(1)}, f32[4,2,2,1,128]{4,1,0,3,2:T(2,128)S(1)}, u32[]{:S(2)}, u32[]{:S(2)}) collective-permute-start(f32[4,2,2,1,128]{4,1,0,3,2:T(2,128)S(1)} %pad_maximum_fusion.9), channel_id=1, source_target_pairs={{0,4},{4,0},{1,5},{5,1},{2,6},{6,2},{3,7},{7,3},{8,12},{12,8},{9,1... | collective-permute-start | bytes 24584 | tf_op jit(solution)/shard_map/ppermute | solution.py:29
  29.1 5.5 %collective-permute-start.8 = (f32[4,4,1,1,128]{4,1,0,3,2:T(4,128)S(1)}, f32[4,4,1,1,128]{4,1,0,3,2:T(4,128)S(1)}, u32[]{:S(2)}, u32[]{:S(2)}) collective-permute-start(f32[4,4,1,1,128]{4,1,0,3,2:T(4,128)S(1)} %get-tuple-element.74), channel_id=1, source_target_pairs={{0,3},{1,2},{2,1},{3,0},{4,7},{5,6},{6,5},{7,4},{8,11},{9,10},{10,... | collective-permute-start | bytes 24584 | tf_op jit(solution)/shard_map/ppermute | solution.py:39
  31.2 3.7 %collective-permute-start.9 = (f32[4,4,1,1,128]{4,1,0,3,2:T(4,128)S(1)}, f32[4,4,1,1,128]{4,1,0,3,2:T(4,128)S(1)}, u32[]{:S(2)}, u32[]{:S(2)}) collective-permute-start(f32[4,4,1,1,128]{4,1,0,3,2:T(4,128)S(1)} %get-tuple-element.75), channel_id=1, source_target_pairs={{0,1},{1,0},{2,3},{3,2},{4,5},{5,4},{6,7},{7,6},{8,9},{9,8},{10,11... | collective-permute-start | bytes 24584 | tf_op jit(solution)/shard_map/ppermute | solution.py:38
  31.9 3.0 %copy-start = (f32[2,2,2,128]{3,2,1,0:T(2,128)S(1)}, f32[2,2,2,128]{3,2,1,0:T(2,128)}, u32[]{:S(2)}) copy-start(f32[2,2,2,128]{3,2,1,0:T(2,128)} %refs_10_.1) | copy-start | bytes 12292
  37.7 3.1 %collective-permute-start.10 = (f32[1,2,2,4,128]{4,3,1,0,2:T(4,128)S(1)}, f32[1,2,2,4,128]{4,3,1,0,2:T(4,128)S(1)}, u32[]{:S(2)}, u32[]{:S(2)}) collective-permute-start(f32[1,2,2,4,128]{4,3,1,0,2:T(4,128)S(1)} %copy.17), channel_id=1, source_target_pairs={{0,24},{8,16},{16,8},{24,0},{1,25},{9,17},{17,9},{25,1},{2,26},{10... | collective-permute-start | bytes 24584 | tf_op jit(solution)/shard_map/ppermute | solution.py:39
  37.8 3.1 %collective-permute-start.11 = (f32[1,2,2,4,128]{4,3,1,0,2:T(4,128)S(1)}, f32[1,2,2,4,128]{4,3,1,0,2:T(4,128)S(1)}, u32[]{:S(2)}, u32[]{:S(2)}) collective-permute-start(f32[1,2,2,4,128]{4,3,1,0,2:T(4,128)S(1)} %copy.18), channel_id=1, source_target_pairs={{0,8},{8,0},{16,24},{24,16},{1,9},{9,1},{17,25},{25,17},{2,10},{10... | collective-permute-start | bytes 24584 | tf_op jit(solution)/shard_map/ppermute | solution.py:38
  40.8 4.0 %collective-permute-start.12 = (f32[4,2,2,4,128]{4,3,1,0,2:T(4,128)S(1)}, f32[4,2,2,4,128]{4,3,1,0,2:T(4,128)S(1)}, u32[]{:S(2)}, u32[]{:S(2)}) collective-permute-start(f32[4,2,2,4,128]{4,3,1,0,2:T(4,128)S(1)} %pad_maximum_fusion.5), channel_id=1, source_target_pairs={{0,4},{4,0},{1,5},{5,1},{2,6},{6,2},{3,7},{7,3},{8,12},{12,8},{9,1... | collective-permute-start | bytes 98312 | tf_op jit(solution)/shard_map/ppermute | solution.py:29
  44.9 5.8 %collective-permute-start.13 = (f32[4,4,1,4,128]{4,3,1,0,2:T(4,128)S(1)}, f32[4,4,1,4,128]{4,3,1,0,2:T(4,128)S(1)}, u32[]{:S(2)}, u32[]{:S(2)}) collective-permute-start(f32[4,4,1,4,128]{4,3,1,0,2:T(4,128)S(1)} %get-tuple-element.58), channel_id=1, source_target_pairs={{0,3},{1,2},{2,1},{3,0},{4,7},{5,6},{6,5},{7,4},{8,11},{9,10},{10,... | collective-permute-start | bytes 98312 | tf_op jit(solution)/shard_map/ppermute | solution.py:39
  46.9 4.1 %collective-permute-start.14 = (f32[4,4,1,4,128]{4,3,1,0,2:T(4,128)S(1)}, f32[4,4,1,4,128]{4,3,1,0,2:T(4,128)S(1)}, u32[]{:S(2)}, u32[]{:S(2)}) collective-permute-start(f32[4,4,1,4,128]{4,3,1,0,2:T(4,128)S(1)} %get-tuple-element.59), channel_id=1, source_target_pairs={{0,1},{1,0},{2,3},{3,2},{4,5},{5,4},{6,7},{7,6},{8,9},{9,8},{10,11... | collective-permute-start | bytes 98312 | tf_op jit(solution)/shard_map/ppermute | solution.py:38

commit v2 on v1

v2 whole, which is shorter than its diff:
```python
import functools
import itertools

import jax
import jax.numpy as jnp
from jax import lax
from jax.experimental import pallas as pl
from jax.experimental.pallas import tpu as pltpu
from jax.sharding import PartitionSpec as P

AXES = (("gx", 0), ("gy", 1), ("gz", 2))
FAR = 1024.0
TINY = 1e-30
ROOM = 6 << 20
GROUP = 4
WIDE = (0, 1, 2, 4, 5, 6)
OFFSETS = tuple(itertools.product((-1, 0, 1), repeat=3))


def ends_of(block, axis, dim):
    count = lax.axis_size(axis)
    size = block.shape[dim]
    last = lax.slice_in_dim(block, size - 1, None, axis=dim)
    first = lax.slice_in_dim(block, 0, 1, axis=dim)
    if count == 1:
        return first, last, True
    if count == 2:
        ends = block if size == 2 else jnp.concatenate([first, last], axis=dim)
        ends = lax.ppermute(ends, axis, [(0, 1), (1, 0)])
        return lax.slice_in_dim(ends, 0, 1, axis=dim), lax.slice_in_dim(ends, 1, 2, axis=dim), True
    if count % 2:
        forward = [(i, (i + 1) % count) for i in range(count)]
        backward = [(target, source) for source, target in forward]
        return lax.ppermute(first, axis, backward), lax.ppermute(last, axis, forward), True
    even = lax.axis_index(axis) % 2 == 0
    near_pairs = [(i, i + 1 - 2 * (i % 2)) for i in range(count)]
    far_pairs = [(i, (i - 1 + 2 * (i % 2)) % count) for i in range(count)]
    one = lax.ppermute(jnp.where(even, last, first), axis, near_pairs)
    two = lax.ppermute(jnp.where(even, first, last), axis, far_pairs)
    return one, two, even


def low_and_high(block, axis, dim):
    one, two, one_is_high = ends_of(block, axis, dim)
    if one_is_high is True:
        return two, one
    return jnp.where(one_is_high, two, one), jnp.where(one_is_high, one, two)


def after(block, *others):
    return lax.optimization_barrier((block,) + others)[0]


def exchange(block, beside_x, beside_y):
    low, high = low_and_high(block, "gx", 0)
    wide = jnp.concatenate([low, block, high], axis=0)
    first = beside_x()
    low, high = low_and_high(after(wide, *first), "gy", 1)
    layers = jnp.concatenate([low, wide, high], axis=1)
    second = beside_y()
    one, two, one_is_high = ends_of(after(layers, *second), "gz", 2)
    return flat(layers), flat(one), flat(two), one_is_high


def column_constant(values, rows):
    ids = lax.broadcasted_iota(jnp.int32, (rows, 128), 0)
    out = jnp.zeros((rows, 128), jnp.float32)
    for row, value in enumerate(values):
        if value != 0.0:
            out = jnp.where(ids == row, jnp.float32(value), out)
    return out


def apart(own, row):
    return own[0] - row(0), own[1] - row(1), own[2] - row(2)


def volume_pair(own, row, keep):
    dx, dy, dz = apart(own, row)
    square = dx * dx + dy * dy + dz * dz
    radius = square * lax.rsqrt(jnp.maximum(square, TINY))
    inside = jnp.maximum(1.0 - radius, 0.0)
    keep[...] = inside
    second = inside * inside
    return ((second * second) * (1.25 - inside),)


def density_pair(own, row, kept):
    dx, dy, dz = apart(own, row)
    inside = kept[...]
    third = inside * inside * inside
    value = third * (inside * (1.25 - inside))
    relative = (row(4) - own[4]) * dx + (row(5) - own[5]) * dy + (row(6) - own[6]) * dz
    volume = row(7)
    return (
        row(3) * value,
        volume * value,
        (volume * third) * relative,
    )


def force_pair(own, row, kept):
    dx, dy, dz = apart(own, row)
    inside = kept[...]
    scaled = row(3) * (inside * inside * inside)
    relative = (own[4] - row(4)) * dx + (own[5] - row(5)) * dy + (own[6] - row(6)) * dz
    half = (own[10] + row(10)) / (own[8] + row(8))
    heat = own[9] + half
    push = (heat + (row(9) + half)) * scaled
    return (
        push * dx,
        push * dy,
        push * dz,
        (heat * scaled) * relative,
    )


def prepare_kernel(counts_ref, base_ref, out_ref):
    nx, ny, channels, nz, slots = base_ref.shape
    for leaf, (x, y, z) in enumerate(itertools.product(range(nx), range(ny), range(nz))):
        for c in range(channels):
            out_ref[leaf, c : c + 1, :] = base_ref[x, y, c, z : z + 1, :]
        number = counts_ref[x, y : y + 1, z : z + 1].astype(jnp.float32)
        out_ref[leaf, channels : channels + 1, :] = jnp.broadcast_to(number, (1, slots))


def partners(grid):
    nx, ny, nz = grid
    parts = ([], [])
    for x, y, z in itertools.product(range(nx), range(ny), range(nz)):
        for part in parts:
            part.append([])
        for k, (ox, oy, oz) in enumerate(OFFSETS):
            tx, ty, tz = x + ox, y + oy, z + oz
            if 0 <= tz < nz:
                if 0 <= tx < nx and 0 <= ty < ny:
                    parts[0][-1].append((k, (tx * ny + ty) * nz + tz))
                else:
                    parts[1][-1].append((k, ((tx + 1) * (ny + 2) + ty + 1) * nz + tz))
    return parts


class Layers:
    def __init__(self, grid, part):
        self.lists = part
        self.mask_count = 27 * len(part)

    def bind(self, flag):
        self.moves = [column_constant(offset, 8) for offset in OFFSETS]

    def leaf(self, index):
        return index

    def mask_at(self, index, k):
        return index * 27 + k

    def move(self, k):
        return self.moves[k]


class Side:
    def __init__(self, grid, when):
        nx, ny, nz = grid
        self.depth, self.when = nz, when
        self.mask_count = 27 * nx * ny * nz
        columns = [(k, OFFSETS[k][:2]) for k in range(1, 27, 3)]
        self.lists = [
            [(k, (x + ox + 1) * (ny + 2) + y + oy + 1) for k, (ox, oy) in columns]
            for x, y in itertools.product(range(nx), range(ny))
        ]

    def bind(self, flag):
        self.high = flag if self.when else 1 - flag
        heights = lax.broadcasted_iota(jnp.int32, (8, 128), 0)
        along = jnp.where(heights == 2, (2 * self.high - 1).astype(jnp.float32), 0.0)
        self.moves = {k: column_constant(OFFSETS[k][:2], 8) + along for k in range(1, 27, 3)}

    def leaf(self, index):
        return index * self.depth + self.high * (self.depth - 1)

    def mask_at(self, index, k):
        return self.leaf(index) * 27 + (2 * self.high - 1) + k

    def move(self, k):
        return self.moves[k]


def longest(lists):
    return max(len(found) for found in lists)


def list_tiles(lists):
    return longest(lists) + 2


def split_place(start):
    return start & 127, lax.shift_right_logical(start, 7)


def put(list_ref, leaf, shift, tile, block, lanes):
    rolled = pltpu.roll(block, shift, axis=1)
    pltpu.store(list_ref.at[leaf, tile], rolled, mask=lanes >= shift)
    list_ref[leaf, tile + 1] = rolled


def close(list_ref, leaf, shift, tile, tail, lanes):
    pltpu.store(list_ref.at[leaf, tile], tail, mask=lanes >= shift)


def lane_ids(rows):
    return lax.broadcasted_iota(jnp.int32, (rows, 128), 1)


def pack_places(part, mask_ref, counts_ref, source_ref, list_ref, shift_ref, tile_ref, last_ref, all_ref):
    lanes = lane_ids(8)
    only_places = lax.broadcasted_iota(jnp.int32, (8, 128), 0) < 3
    far = column_constant((FAR, FAR, FAR), 8)
    stride = longest(part.lists) + 1
    for index, found in enumerate(part.lists):
        start = jnp.int32(0)
        for number, (k, place) in enumerate(found):
            shift, tile = split_place(start)
            shift_ref[index * stride + number] = shift
            tile_ref[index * stride + number] = tile
            put(list_ref, index, shift, tile, source_ref[place] + part.move(k), lanes)
            start = start + counts_ref[place] * mask_ref[part.mask_at(index, k)]
        shift, tile = split_place(start)
        shift_ref[index * stride + len(found)] = shift
        tile_ref[index * stride + len(found)] = tile
        last_ref[index] = split_place(start + 127)[1]
        for k, place in found:
            shift, tile = split_place(start)
            block = jnp.where(only_places, source_ref[place] + part.move(k), 0.0)
            put(list_ref, index, shift, tile, block, lanes)
            start = start + counts_ref[place] * (1 - mask_ref[part.mask_at(index, k)])
        shift, tile = split_place(start)
        close(list_ref, index, shift, tile, far, lanes)
        all_ref[index] = split_place(start + 127)[1]


def pack_side(part, span, source_ref, side_ref, shift_ref, tile_ref, tail):
    height = source_ref.shape[1]
    lanes = lane_ids(height)
    last = column_constant(tail, height)
    stride = longest(part.lists) + 1
    for index in range(*span):
        found = part.lists[index]
        for number, (_, place) in enumerate(found):
            at = index * stride + number
            put(side_ref, index, shift_ref[at], tile_ref[at], source_ref[place], lanes)
        at = index * stride + len(found)
        close(side_ref, index, shift_ref[at], tile_ref[at], last, lanes)


def widen_kernel(rows, block_ref, out_ref):
    for leaf in range(block_ref.shape[0]):
        for index, c in enumerate(rows):
            row = block_ref[leaf, c : c + 1, :]
            out_ref[leaf, index] = jnp.transpose(jnp.broadcast_to(row, (128, 128)))


def read_counts(source_ref, counts_ref):
    for place in range(source_ref.shape[0]):
        counts_ref[place] = source_ref[place, 7:8, :].astype(jnp.int32)[0, 0]


def run_pairs(part, span, pair, n_sums, counts_ref, tiles_ref, own_of, row_of, kept_ref, before_ref, acc_ref):
    zero = jnp.zeros((8, 128), jnp.float32)

    def leaf_step(index, carry):
        leaf = part.leaf(index)
        count = counts_ref[leaf]
        tiles = tiles_ref[index]

        def group_step(group, carry):
            places = [
                pl.ds(pl.multiple_of(group * (8 * GROUP) + 8 * chunk, 8), 8) for chunk in range(GROUP)
            ]
            owns = [own_of(leaf, at) for at in places]

            def add_tile(tile, sums):
                rows = {}

                def row(c):
                    if c not in rows:
                        rows[c] = jnp.broadcast_to(row_of(index, tile, c), (8, 128))
                    return rows[c]

                terms = [
                    pair(own, row, kept_ref.at[index, tile, at, :]) for own, at in zip(owns, places)
                ]
                return tuple(tuple(a + b for a, b in zip(old, new)) for old, new in zip(sums, terms))

            def two_tiles(step, sums):
                return add_tile(2 * step + 1, add_tile(2 * step, sums))

            start = tuple(
                tuple(zero if before_ref is None else before_ref[leaf, i, at, :] for i in range(n_sums))
                for at in places
            )
            sums = lax.fori_loop(0, lax.shift_right_logical(tiles, 1), two_tiles, start)
            sums = lax.fori_loop(0, tiles & 1, lambda _, sums: add_tile(tiles - 1, sums), sums)
            for at, total in zip(places, sums):
                for i in range(n_sums):
                    acc_ref[leaf, i, at, :] = total[i]
            return carry

        groups = lax.shift_right_logical(count + (8 * GROUP - 1), (8 * GROUP).bit_length() - 1)
        return lax.fori_loop(0, groups, group_step, carry)

    lax.fori_loop(*span, leaf_step, 0)


def lane_sums(blocks):
    rows = []
    left = lane_ids(128) < 64
    for i in range(0, len(blocks) - 1, 2):
        one, two = blocks[i : i + 2]
        both = jnp.where(left, one, two) + pltpu.roll(jnp.where(left, two, one), 64, axis=1)
        both = jnp.transpose(both)
        rows += [jnp.sum(half, axis=0, keepdims=True) for half in (both[:64], both[64:])]
    if len(blocks) % 2:
        rows.append(jnp.sum(jnp.transpose(blocks[-1]), axis=0, keepdims=True))
    return rows


def leaf_totals(grid, acc_ref, counts_ref):
    for leaf, index in enumerate(itertools.product(*map(range, grid))):
        sums = lane_sums([acc_ref[leaf, i] for i in range(acc_ref.shape[1])])
        yield index, leaf, sums, lax.broadcasted_iota(jnp.int32, (1, 128), 1) < counts_ref[leaf]


def own_reader(*pieces):
    def own_of(leaf, at):
        return {c: ref[leaf, i, at, :] for ref, channels in pieces for i, c in enumerate(channels)}

    return own_of


def row_reader(list_ref, side_ref=None, base=8):
    def row_of(leaf, at, c):
        if c < base:
            return list_ref[leaf, at, c : c + 1, :]
        return side_ref[leaf, at, c - base : c - base + 1, :]

    return row_of


def volume_kernel(grid, part, stage, *refs):
    refs = list(refs)
    numbers_ref = refs.pop(0) if stage else None
    mask_ref, source_ref, wide_ref = refs[:3]
    before_ref = refs[3] if stage else None
    acc_ref, counts_ref, list_ref, shift_ref, tile_ref, last_ref, kept_ref = refs[4 if stage else 3 :][:7]
    all_ref = refs[-1]
    read_counts(source_ref, counts_ref)
    if numbers_ref is None:
        numbers_ref = counts_ref
        numbers_ref[source_ref.shape[0]] = mask_ref[part.mask_count]
    part.bind(mask_ref[part.mask_count])
    pack_places(part, mask_ref, counts_ref, source_ref, list_ref, shift_ref, tile_ref, last_ref, all_ref)
    run_pairs(
        part, (0, len(part.lists)), volume_pair, 1, numbers_ref, all_ref,
        own_reader((wide_ref, WIDE)), row_reader(list_ref), kept_ref, before_ref, acc_ref,
    )
    if stage == 3:
        out_ref = refs[-2]
        for index, leaf, sums, valid in leaf_totals(grid, acc_ref, numbers_ref):
            out_ref[leaf] = jnp.where(valid, 1.0 / (1.0 + 4.0 * sums[0]), 1.0)


def density_kernel(grid, part, stage, span, *refs):
    numbers_ref, list_ref, shift_ref, tile_ref, last_ref, kept_ref, wide_ref, source_ref = refs[:8]
    before_ref = refs[8] if stage or span[0] else None
    acc_ref = refs[12 if stage == 3 else 9 if before_ref is not None else 8]
    side_ref = refs[-1]
    part.bind(numbers_ref[numbers_ref.shape[0] - 1])
    pack_side(part, span, source_ref, side_ref, shift_ref, tile_ref, ())
    run_pairs(
        part, span, density_pair, 3, numbers_ref, last_ref, own_reader((wide_ref, WIDE)),
        row_reader(list_ref, side_ref, 7), kept_ref, before_ref if stage else None, acc_ref,
    )
    if stage == 3:
        own_ref, volume_ref, energy_ref = refs[9:12]
        out_ref = refs[13]
        for (x, y, z), leaf, sums, valid in leaf_totals(grid, acc_ref, numbers_ref):
            density = (own_ref[leaf, 3:4, :] + 4.0 * sums[0]) / (volume_ref[leaf] + 4.0 * sums[1])
            density = jnp.where(valid, density, 1.0)
            energy = energy_ref[x, y, z : z + 1, :]
            out_ref[leaf, 0:1, :] = density
            out_ref[leaf, 1:2, :] = jnp.where(valid, (2.0 / 3.0) * energy / density, 0.0)
            out_ref[leaf, 2:3, :] = jnp.where(valid, jnp.maximum(20.0 * sums[2], 0.0), 0.0)
            out_ref[leaf, 3:4, :] = jnp.zeros_like(density)


def force_kernel(grid, part, stage, span, *refs):
    numbers_ref, list_ref, shift_ref, tile_ref, last_ref, kept_ref, wide_ref, state_ref, source_ref = refs[:9]
    before_ref = refs[9] if stage or span[0] else None
    acc_ref = refs[10 if before_ref is not None else 9]
    side_ref = refs[-1]
    part.bind(numbers_ref[numbers_ref.shape[0] - 1])
    pack_side(part, span, source_ref, side_ref, shift_ref, tile_ref, (1.0,))
    run_pairs(
        part, span, force_pair, 4, numbers_ref, last_ref,
        own_reader((wide_ref, WIDE), (state_ref, (8, 9, 10))), row_reader(list_ref, side_ref),
        kept_ref, before_ref if stage else None, acc_ref,
    )
    if stage == 3:
        push_ref, heat_ref = refs[11:13]
        for (x, y, z), leaf, sums, valid in leaf_totals(grid, acc_ref, numbers_ref):
            for c in range(3):
                push_ref[x, y, c, z : z + 1, :] = jnp.where(valid, 20.0 * sums[c], 0.0)
            heat_ref[x, y, z : z + 1, :] = jnp.where(valid, -20.0 * sums[3], 0.0)


def call(name, body, inputs, outs, scratch=(), cycles=0, aliases=()):
    def spec(x):
        scalar = x.dtype == jnp.int32 and len(x.shape) == 1
        return pl.BlockSpec(memory_space=pltpu.SMEM if scalar else pltpu.VMEM)

    return pl.pallas_call(
        body,
        out_shape=outs,
        in_specs=[spec(x) for x in inputs],
        out_specs=[spec(x) for x in outs],
        scratch_shapes=scratch,
        input_output_aliases=dict(aliases),
        compiler_params=pltpu.CompilerParams(vmem_limit_bytes=ROOM),
        cost_estimate=pl.CostEstimate(flops=cycles * 4096, bytes_accessed=1 << 20, transcendentals=0),
        name=name,
    )(*inputs)


def floats(*shape):
    return jax.ShapeDtypeStruct(shape, jnp.float32)


def integers(*shape):
    return jax.ShapeDtypeStruct(shape, jnp.int32)


def flat(block):
    return block.reshape((-1,) + block.shape[3:])


def shards(offsets, velocity, mass, energy, partner_mask, counts):
    grid = counts.shape
    slots = offsets.shape[4]
    assert slots == 128
    leaves = grid[0] * grid[1] * grid[2]
    parts = [Layers(grid, part) for part in partners(grid)] + [Side(grid, True), Side(grid, False)]
    pieces = [jnp.swapaxes(x, 2, 3) for x in (offsets, mass[:, :, :, None], velocity)]
    base = jnp.concatenate(pieces, axis=2)
    own = call("prepare", prepare_kernel, [counts, base], [floats(leaves, 8, slots)])[0]
    one_is_high = jnp.ones((1,), jnp.int32)
    if lax.axis_size("gz") > 2 and lax.axis_size("gz") % 2 == 0:
        one_is_high = 1 - lax.axis_index("gz").astype(jnp.int32)[None] % 2
    mask = jnp.concatenate([partner_mask.reshape(-1), one_is_high])
    wide = call(
        "widen", functools.partial(widen_kernel, WIDE), [own],
        [floats(leaves, len(WIDE), slots, slots)], cycles=2000,
    )[0]

    cut = 3 * leaves // 8

    def side_space(p, height):
        lists = parts[p].lists
        return pltpu.VMEM((len(lists), list_tiles(lists), height, slots), jnp.float32)

    def spread(n_sums):
        return floats(leaves, n_sums, slots, slots)

    def list_outs(p):
        lists = parts[p].lists
        count, tiles = len(lists), list_tiles(lists)
        numbers = integers(count * (longest(lists) + 1))
        return [
            floats(count, tiles, 8, slots), numbers, numbers, integers(count),
            floats(count, tiles, slots, slots),
        ]

    numbers, packs = [], []

    def volume_part(p, source, before=()):
        inputs = numbers[:1] + [mask, source, wide, *before]
        outs = [spread(1), integers(source.shape[0] + (p == 0))] + list_outs(p)
        acc, number, *packed = call(
            f"volume_{p}", functools.partial(volume_kernel, grid, parts[p], p), inputs,
            outs + ([floats(leaves, 1, slots)] if p == 3 else []),
            [pltpu.SMEM((len(parts[p].lists),), jnp.int32)], cycles=3000,
            aliases=[(len(inputs) - 1, 0)] if before else (),
        )
        numbers.append(number)
        packs.append(packed[:5])
        return [packed[5] if p == 3 else acc]

    def density_part(p, source, before=(), more=(), span=None):
        span = span or (0, len(parts[p].lists))
        return call(
            f"density_{p}", functools.partial(density_kernel, grid, parts[p], p, span),
            [numbers[0], *packs[p], wide, source, *before, *more],
            [spread(3)] + ([floats(leaves, 4, slots)] if p == 3 else []),
            [side_space(p, 1)], cycles=4000, aliases=[(8, 0)] if before else (),
        )[-1:]

    def force_part(p, source, before=(), span=None):
        span = span or (0, len(parts[p].lists))
        final = [floats(*grid[:2], 3, grid[2], slots), floats(*grid, slots)]
        return call(
            f"force_{p}", functools.partial(force_kernel, grid, parts[p], p, span),
            [numbers[0], *packs[p], wide, wide_state, source, *before],
            [spread(4)] + (final if p == 3 else []),
            [side_space(p, 4)], cycles=5000, aliases=[(9, 0)] if before else (),
        )[-2:]

    early = []

    def keep(run):
        def beside():
            early[:] = run()
            return tuple(early)

        return beside

    layers, one, two, _ = exchange(
        own.reshape(grid + (8, slots)), lambda: (wide,), keep(lambda: volume_part(0, own))
    )
    (volume,) = volume_part(3, two, volume_part(2, one, volume_part(1, layers, early)))

    layers, one, two, _ = exchange(
        volume.reshape(grid + (1, slots)),
        keep(lambda: density_part(0, volume, span=(0, cut))),
        keep(lambda: density_part(0, volume, early, span=(cut, leaves))),
    )
    acc = density_part(2, one, density_part(1, layers, early))
    (state,) = density_part(3, two, acc, [own, volume, energy])

    wide_state = call(
        "widen_state", functools.partial(widen_kernel, (0, 1, 2)), [state],
        [floats(leaves, 3, slots, slots)], cycles=1000,
    )[0]
    layers, one, two, _ = exchange(
        state.reshape(grid + (4, slots)),
        keep(lambda: force_part(0, state, span=(0, cut))),
        keep(lambda: force_part(0, state, early, span=(cut, leaves))),
    )
    push, heat = force_part(3, two, force_part(2, one, force_part(1, layers, early)))
    return jnp.swapaxes(push, 2, 3), heat


def solution(mesh):
    placed = (
        P("gx", "gy", "gz", None, None),
        P("gx", "gy", "gz", None, None),
        P("gx", "gy", "gz", None),
        P("gx", "gy", "gz", None),
        P("gx", "gy", "gz", None),
        P("gx", "gy", "gz"),
    )
    return jax.shard_map(
        shards,
        mesh=mesh,
        in_specs=placed,
        out_specs=(P("gx", "gy", "gz", None, None), P("gx", "gy", "gz", None)),
        check_vma=False,
    )
```

time: 55.7 us -> 56.3 us (1.011); the launches traced: 54.9 us -> 56.5 us
  Pallas kernels: 25.8 us -> 29.7 us
  starting transfers between devices: 18.3 us -> 16.6 us
  waiting for transfers between devices: 7.98 us -> 6.64 us
  local copies, waits for them, and re-layouts: 0.84 us -> 1.52 us
    pallas_call x14 -> x17, Pallas kernels: 25.8 us -> 29.7 us  [call(): pl.pallas_call(body, out_shape=outs, in_specs=[spec(x) for x in inputs],...]
    ppermute x6, waiting for transfers between devices: 3.36 us -> 0.83 us  [ends_of(): two = lax.ppermute(jnp.where(even, first, last), axis, far_pairs)]
    ppermute x3, starting transfers between devices: 4.03 us -> 1.7 us  [ends_of(): ends = lax.ppermute(ends, axis, [(0, 1), (1, 0)])]
    ppermute x3, waiting for transfers between devices: 2.28 us -> 4.1 us  [ends_of(): ends = lax.ppermute(ends, axis, [(0, 1), (1, 0)])]
    ppermute x6, starting transfers between devices: 11.4 us -> 12.9 us  [ends_of(): two = lax.ppermute(jnp.where(even, first, last), axis, far_pairs)]
    ppermute x6, starting transfers between devices: 2.93 us -> 2.04 us  [ends_of(): one = lax.ppermute(jnp.where(even, last, first), axis, near_pairs)]
    reshape x1, local copies, waits for them, and re-layouts: 0.08 us -> 0.77 us  [shards(): mask = jnp.concatenate([partner_mask.reshape(-1), one_is_high])]
    ppermute x6, waiting for transfers between devices: 2.35 us -> 1.71 us  [ends_of(): one = lax.ppermute(jnp.where(even, last, first), axis, near_pairs)]
  transfers between devices with their start and end apart: 15 -> 15, of which waited for: 9 -> 6; matrix products, arithmetic and copies ran while one was open for 0% -> 2% of each run, Pallas kernels for 30% -> 41%
where the time goes in v2:
time: 56.3 us; the launch traced here: 56.5 us
  Pallas kernels  29.7 us (53%)
  starting transfers between devices  16.6 us (29%)
  waiting for transfers between devices  6.64 us (12%)
  local copies, waits for them, and re-layouts  1.52 us (3%)
  between operations  1.05 us (2%)
  other arithmetic  0.98 us (2%)
    pallas_call x17, Pallas kernels, call(): pl.pallas_call(body, out_shape=outs, in_specs=[spec(x) for x in inputs],...  29.7 us
    ppermute x6, starting transfers between devices, ends_of(): two = lax.ppermute(jnp.where(even, first, last), axis, far_pairs)  12.9 us
    ppermute x3, waiting for transfers between devices, ends_of(): ends = lax.ppermute(ends, axis, [(0, 1), (1, 0)])  4.1 us
    ppermute x6, starting transfers between devices, ends_of(): one = lax.ppermute(jnp.where(even, last, first), axis, near_pairs)  2.04 us
    ppermute x6, waiting for transfers between devices, ends_of(): one = lax.ppermute(jnp.where(even, last, first), axis, near_pairs)  1.71 us
    ppermute x3, starting transfers between devices, ends_of(): ends = lax.ppermute(ends, axis, [(0, 1), (1, 0)])  1.7 us
  transfers between devices with their start and end apart: 15, of which 6 were waited for; matrix products, arithmetic and copies ran while one was open for 2% of the time, Pallas kernels for 41%

profile of v2, /device:TPU:0, one launch (start us, length us, event | category | flops | bytes accessed | tf_op | source)
XLA Modules:
  0.0 56.5 jit_solution(11131684025663674596)
XLA Ops:
  2.7 2.6 %collective-permute-start = (f32[1,2,2,8,128]{4,3,1,0,2:T(8,128)S(1)}, f32[1,2,2,8,128]{4,3,1,0,2:T(8,128)S(1)}, u32[]{:S(2)}, u32[]{:S(2)}) collective-permute-start(f32[1,2,2,8,128]{4,3,1,0,2:T(8,128)S(1)} %copy.19), channel_id=1, source_target_pairs={{0,24},{8,16},{16,8},{24,0},{1,25},{9,17},{17,9},{25,1},{2,26},{10... | collective-permute-start | bytes 49160 | tf_op jit(solution)/shard_map/ppermute | solution.py:39
  7.1 1.6 %collective-permute-start.2 = (f32[4,2,2,8,128]{4,3,1,0,2:T(8,128)S(1)}, f32[4,2,2,8,128]{4,3,1,0,2:T(8,128)S(1)}, u32[]{:S(2)}, u32[]{:S(2)}) collective-permute-start(f32[4,2,2,8,128]{4,3,1,0,2:T(8,128)S(1)} %pad_maximum_fusion.1), channel_id=1, source_target_pairs={{0,4},{4,0},{1,5},{5,1},{2,6},{6,2},{3,7},{7,3},{8,12},{12,8},{9,1... | collective-permute-start | bytes 196616 | tf_op jit(solution)/shard_map/ppermute | solution.py:29
  8.7 3.2 %volume_0.1 = (f32[8,1,128,128]{3,2,1,0:T(8,128)S(1)}, s32[9]{0:T(128)S(1)}, f32[8,10,8,128]{3,2,1,0:T(8,128)S(1)}, s32[72]{0:T(128)S(1)}, s32[72]{0:T(128)S(1)}...) custom-call(s32[217]{0:T(256)S(1)} %pad_add_fusion.refs_0_.refs_1_, f32[8,8,128]{2,1,0:T(8,128)S(1)} %prepare.1.block_ref.refs_1_.refs_9_, ...), custom_call_target="tpu_custom_call" | custom-call | flops 12288000 | bytes 1048576 | tf_op jit(solution)/shard_map/volume_0/pallas_call | solution.py:421
  12.0 1.2 %collective-permute-start.4 = (f32[4,4,1,8,128]{4,3,1,0,2:T(8,128)S(1)}, f32[4,4,1,8,128]{4,3,1,0,2:T(8,128)S(1)}, u32[]{:S(2)}, u32[]{:S(2)}) collective-permute-start(f32[4,4,1,8,128]{4,3,1,0,2:T(8,128)S(1)} %get-tuple-element.70), channel_id=1, source_target_pairs={{0,1},{1,0},{2,3},{3,2},{4,5},{5,4},{6,7},{7,6},{8,9},{9,8},{10,11... | collective-permute-start | bytes 196616 | tf_op jit(solution)/shard_map/ppermute | solution.py:38
  13.2 2.5 %collective-permute-start.3 = (f32[4,4,1,8,128]{4,3,1,0,2:T(8,128)S(1)}, f32[4,4,1,8,128]{4,3,1,0,2:T(8,128)S(1)}, u32[]{:S(2)}, u32[]{:S(2)}) collective-permute-start(f32[4,4,1,8,128]{4,3,1,0,2:T(8,128)S(1)} %get-tuple-element.71), channel_id=1, source_target_pairs={{0,3},{1,2},{2,1},{3,0},{4,7},{5,6},{6,5},{7,4},{8,11},{9,10},{10,... | collective-permute-start | bytes 196616 | tf_op jit(solution)/shard_map/ppermute | solution.py:39
  15.7 3.1 %volume_1.1 = (f32[8,1,128,128]{3,2,1,0:T(8,128)S(1)}, s32[32]{0:T(128)}, f32[8,12,8,128]{3,2,1,0:T(8,128)S(1)}, s32[88]{0:T(128)S(1)}, s32[88]{0:T(128)S(1)}, /...) custom-call(s32[9]{0:T(128)S(1)} %get-tuple-element.36.refs_0_, ...), custom_call_target="tpu_custom_call", output_to_operand_aliasing={{0}: (4, {})} | custom-call | flops 12288000 | bytes 1048576 | tf_op jit(solution)/shard_map/volume_1/pallas_call | solution.py:421
  18.8 2.2 %volume_2.1 = (f32[8,1,128,128]{3,2,1,0:T(8,128)S(1)}, s32[16]{0:T(128)}, f32[4,11,8,128]{3,2,1,0:T(8,128)S(1)}, s32[40]{0:T(128)S(1)}, s32[40]{0:T(128)S(1)}, /...) custom-call(s32[9]{0:T(128)S(1)} %get-tuple-element.36.refs_0_, ...), custom_call_target="tpu_custom_call", output_to_operand_aliasing={{0}: (4, {})} | custom-call | flops 12288000 | bytes 1048576 | tf_op jit(solution)/shard_map/volume_2/pallas_call | solution.py:421
  21.0 2.2 %volume_3.1 = (f32[8,1,128,128]{3,2,1,0:T(8,128)S(1)}, s32[16]{0:T(128)}, f32[4,11,8,128]{3,2,1,0:T(8,128)S(1)}, s32[40]{0:T(128)S(1)}, s32[40]{0:T(128)S(1)}, /...) custom-call(s32[9]{0:T(128)S(1)} %get-tuple-element.36.refs_0_, ...), custom_call_target="tpu_custom_call", output_to_operand_aliasing={{0}: (4, {})} | custom-call | flops 12288000 | bytes 1048576 | tf_op jit(solution)/shard_map/volume_3/pallas_call | solution.py:421
  23.3 4.2 %collective-permute-start.5 = (f32[1,2,2,1,128]{4,1,0,3,2:T(2,128)S(1)}, f32[1,2,2,1,128]{4,1,0,3,2:T(2,128)S(1)}, u32[]{:S(2)}, u32[]{:S(2)}) collective-permute-start(f32[1,2,2,1,128]{4,1,0,3,2:T(2,128)S(1)} %copy.23), channel_id=1, source_target_pairs={{0,24},{8,16},{16,8},{24,0},{1,25},{9,17},{17,9},{25,1},{2,26},{10... | collective-permute-start | bytes 6152 | tf_op jit(solution)/shard_map/ppermute | solution.py:39
  27.6 1.3 %density_0.2.refs_8_ = f32[8,3,128,128]{3,2,1,0:T(8,128)S(1)} custom-call(s32[9]{0:T(128)S(1)} %get-tuple-element.36.refs_0_, f32[8,10,8,128]{3,2,1,0:T(8,128)S(1)} %get-tuple-element.48.refs_1_, s32[72]{0:T(128)S(1)} %get-tuple-element.49.refs_2_, s32[72]{0:T(128)S(1)} %get-tuple-element.50.refs_3_, s32[8]{0:T(128)S(1)} %get-tuple-element.51.refs_4_, ...), custom_call_target="tpu_custom_call" | custom-call | flops 16384000 | bytes 1048576 | tf_op jit(solution)/shard_map/density_0/pallas_call | solution.py:421
  29.0 1.6 %density_0.3.refs_8_ = f32[8,3,128,128]{3,2,1,0:T(8,128)S(1)} custom-call(s32[9]{0:T(128)S(1)} %get-tuple-element.36.refs_0_, f32[8,10,8,128]{3,2,1,0:T(8,128)S(1)} %get-tuple-element.48.refs_1_, s32[72]{0:T(128)S(1)} %get-tuple-element.49.refs_2_, s32[72]{0:T(128)S(1)} %get-tuple-element.50.refs_3_, ...), custom_call_target="tpu_custom_call", output_to_operand_aliasing={{}: (8, {})} | custom-call | flops 16384000 | bytes 1048576 | tf_op jit(solution)/shard_map/density_0/pallas_call | solution.py:421
  30.6 2.0 %collective-permute-done.7 = f32[4,2,2,1,128]{4,1,0,3,2:T(2,128)S(1)} collective-permute-done((f32[4,2,2,1,128]{4,1,0,3,2:T(2,128)S(1)}, f32[4,2,2,1,128]{4,1,0,3,2:T(2,128)S(1)}, u32[]{:S(2)}, u32[]{:S(2)}) %collective-permute-start.7) | collective-permute-done | bytes 8224 | tf_op jit(solution)/shard_map/ppermute | solution.py:29
  33.1 2.0 %density_1.1.refs_8_ = f32[8,3,128,128]{3,2,1,0:T(8,128)S(1)} custom-call(s32[9]{0:T(128)S(1)} %get-tuple-element.36.refs_0_, f32[8,12,8,128]{3,2,1,0:T(8,128)S(1)} %get-tuple-element.60.refs_1_, s32[88]{0:T(128)S(1)} %get-tuple-element.61.refs_2_, s32[88]{0:T(128)S(1)} %get-tuple-element.62.refs_3_, ...), custom_call_target="tpu_custom_call", output_to_operand_aliasing={{}: (8, {})} | custom-call | flops 16384000 | bytes 1048576 | tf_op jit(solution)/shard_map/density_1/pallas_call | solution.py:421
  35.1 1.3 %collective-permute-done.9 = f32[4,4,1,1,128]{4,1,0,3,2:T(4,128)S(1)} collective-permute-done((f32[4,4,1,1,128]{4,1,0,3,2:T(4,128)S(1)}, f32[4,4,1,1,128]{4,1,0,3,2:T(4,128)S(1)}, u32[]{:S(2)}, u32[]{:S(2)}) %collective-permute-start.9) | collective-permute-done | bytes 8224 | tf_op jit(solution)/shard_map/ppermute | solution.py:38
  36.4 1.4 %density_2.1.refs_8_ = f32[8,3,128,128]{3,2,1,0:T(8,128)S(1)} custom-call(s32[9]{0:T(128)S(1)} %get-tuple-element.36.refs_0_, f32[4,11,8,128]{3,2,1,0:T(8,128)S(1)} %get-tuple-element.55.refs_1_, s32[40]{0:T(128)S(1)} %get-tuple-element.56.refs_2_, s32[40]{0:T(128)S(1)} %get-tuple-element.57.refs_3_, ...), custom_call_target="tpu_custom_call", output_to_operand_aliasing={{}: (8, {})} | custom-call | flops 16384000 | bytes 1048576 | tf_op jit(solution)/shard_map/density_2/pallas_call | solution.py:421
  38.3 1.7 %density_3.1 = (f32[8,3,128,128]{3,2,1,0:T(8,128)S(1)}, f32[8,4,128]{2,1,0:T(4,128)S(1)}) custom-call(s32[9]{0:T(128)S(1)} %get-tuple-element.36.refs_0_, f32[4,11,8,128]{3,2,1,0:T(8,128)S(1)} %get-tuple-element.42.refs_1_, s32[40]{0:T(128)S(1)} %get-tuple-element.43.refs_2_, s32[40]{0:T(128)S(1)} %get-tuple-element.44.refs_3_, ...), custom_call_target="tpu_custom_call", output_to_operand_aliasing={{0}: (8, {})} | custom-call | flops 16384000 | bytes 1048576 | tf_op jit(solution)/shard_map/density_3/pallas_call | solution.py:421
  40.1 2.0 %collective-permute-start.10 = (f32[1,2,2,4,128]{4,3,1,0,2:T(4,128)S(1)}, f32[1,2,2,4,128]{4,3,1,0,2:T(4,128)S(1)}, u32[]{:S(2)}, u32[]{:S(2)}) collective-permute-start(f32[1,2,2,4,128]{4,3,1,0,2:T(4,128)S(1)} %copy.27), channel_id=1, source_target_pairs={{0,24},{8,16},{16,8},{24,0},{1,25},{9,17},{17,9},{25,1},{2,26},{10... | collective-permute-start | bytes 24584 | tf_op jit(solution)/shard_map/ppermute | solution.py:39
  42.6 1.5 %force_0.2.refs_9_ = f32[8,4,128,128]{3,2,1,0:T(8,128)S(1)} custom-call(s32[9]{0:T(128)S(1)} %get-tuple-element.36.refs_0_, f32[8,10,8,128]{3,2,1,0:T(8,128)S(1)} %get-tuple-element.48.refs_1_, s32[72]{0:T(128)S(1)} %get-tuple-element.49.refs_2_, s32[72]{0:T(128)S(1)} %get-tuple-element.50.refs_3_, s32[8]{0:T(128)S(1)} %get-tuple-element.51.refs_4_, ...), custom_call_target="tpu_custom_call" | custom-call | flops 20480000 | bytes 1048576 | tf_op jit(solution)/shard_map/force_0/pallas_call | solution.py:421
  44.2 1.8 %force_0.3.refs_9_ = f32[8,4,128,128]{3,2,1,0:T(8,128)S(1)} custom-call(s32[9]{0:T(128)S(1)} %get-tuple-element.36.refs_0_, f32[8,10,8,128]{3,2,1,0:T(8,128)S(1)} %get-tuple-element.48.refs_1_, s32[72]{0:T(128)S(1)} %get-tuple-element.49.refs_2_, s32[72]{0:T(128)S(1)} %get-tuple-element.50.refs_3_, ...), custom_call_target="tpu_custom_call", output_to_operand_aliasing={{}: (9, {})} | custom-call | flops 20480000 | bytes 1048576 | tf_op jit(solution)/shard_map/force_0/pallas_call | solution.py:421
  46.0 2.1 %collective-permute-done.12 = f32[4,2,2,4,128]{4,3,1,0,2:T(4,128)S(1)} collective-permute-done((f32[4,2,2,4,128]{4,3,1,0,2:T(4,128)S(1)}, f32[4,2,2,4,128]{4,3,1,0,2:T(4,128)S(1)}, u32[]{:S(2)}, u32[]{:S(2)}) %collective-permute-start.12) | collective-permute-done | bytes 32800 | tf_op jit(solution)/shard_map/ppermute | solution.py:29
  48.2 1.2 %collective-permute-start.13 = (f32[4,4,1,4,128]{4,3,1,0,2:T(4,128)S(1)}, f32[4,4,1,4,128]{4,3,1,0,2:T(4,128)S(1)}, u32[]{:S(2)}, u32[]{:S(2)}) collective-permute-start(f32[4,4,1,4,128]{4,3,1,0,2:T(4,128)S(1)} %get-tuple-element.73), channel_id=1, source_target_pairs={{0,3},{1,2},{2,1},{3,0},{4,7},{5,6},{6,5},{7,4},{8,11},{9,10},{10,... | collective-permute-start | bytes 98312 | tf_op jit(solution)/shard_map/ppermute | solution.py:39
  49.4 2.3 %force_1.1.refs_9_ = f32[8,4,128,128]{3,2,1,0:T(8,128)S(1)} custom-call(s32[9]{0:T(128)S(1)} %get-tuple-element.36.refs_0_, f32[8,12,8,128]{3,2,1,0:T(8,128)S(1)} %get-tuple-element.60.refs_1_, s32[88]{0:T(128)S(1)} %get-tuple-element.61.refs_2_, s32[88]{0:T(128)S(1)} %get-tuple-element.62.refs_3_, ...), custom_call_target="tpu_custom_call", output_to_operand_aliasing={{}: (9, {})} | custom-call | flops 20480000 | bytes 1048576 | tf_op jit(solution)/shard_map/force_1/pallas_call | solution.py:421
  52.1 1.6 %force_2.1.refs_9_ = f32[8,4,128,128]{3,2,1,0:T(8,128)S(1)} custom-call(s32[9]{0:T(128)S(1)} %get-tuple-element.36.refs_0_, f32[4,11,8,128]{3,2,1,0:T(8,128)S(1)} %get-tuple-element.55.refs_1_, s32[40]{0:T(128)S(1)} %get-tuple-element.56.refs_2_, s32[40]{0:T(128)S(1)} %get-tuple-element.57.refs_3_, ...), custom_call_target="tpu_custom_call", output_to_operand_aliasing={{}: (9, {})} | custom-call | flops 20480000 | bytes 1048576 | tf_op jit(solution)/shard_map/force_2/pallas_call | solution.py:421
  54.0 2.5 %force_3.1 = (f32[8,4,128,128]{3,2,1,0:T(8,128)S(1)}, f32[2,2,3,2,128]{4,3,2,1,0:T(2,128)}, f32[2,2,2,128]{3,2,1,0:T(2,128)}) custom-call(s32[9]{0:T(128)S(1)} %get-tuple-element.36.refs_0_, f32[4,11,8,128]{3,2,1,0:T(8,128)S(1)} %get-tuple-element.42.refs_1_, s32[40]{0:T(128)S(1)} %get-tuple-element.43.refs_2_, ...), custom_call_target="tpu_custom_call", output_to_operand_aliasing={{0}: (9, {})} | custom-call | flops 20480000 | bytes 1048576 | tf_op jit(solution)/shard_map/force_3/pallas_call | solution.py:421
  (58 shorter events, 6.4 us)
Async XLA Ops:
  1.4 0.7 %copy-start.1 = (s32[2,2,2]{2,1,0:T(2,128)S(1)}, s32[2,2,2]{2,1,0:T(2,128)}, u32[]{:S(2)}) copy-start(s32[2,2,2]{2,1,0:T(2,128)} %counts_ref.1) | copy-start | bytes 100
  2.2 4.8 %collective-permute-start.1 = (f32[1,2,2,8,128]{4,3,1,0,2:T(8,128)S(1)}, f32[1,2,2,8,128]{4,3,1,0,2:T(8,128)S(1)}, u32[]{:S(2)}, u32[]{:S(2)}) collective-permute-start(f32[1,2,2,8,128]{4,3,1,0,2:T(8,128)S(1)} %copy.20), channel_id=1, source_target_pairs={{0,8},{8,0},{16,24},{24,16},{1,9},{9,1},{17,25},{25,17},{2,10},{10... | collective-permute-start | bytes 49160 | tf_op jit(solution)/shard_map/ppermute | solution.py:38
  2.7 4.3 %collective-permute-start = (f32[1,2,2,8,128]{4,3,1,0,2:T(8,128)S(1)}, f32[1,2,2,8,128]{4,3,1,0,2:T(8,128)S(1)}, u32[]{:S(2)}, u32[]{:S(2)}) collective-permute-start(f32[1,2,2,8,128]{4,3,1,0,2:T(8,128)S(1)} %copy.19), channel_id=1, source_target_pairs={{0,24},{8,16},{16,8},{24,0},{1,25},{9,17},{17,9},{25,1},{2,26},{10... | collective-permute-start | bytes 49160 | tf_op jit(solution)/shard_map/ppermute | solution.py:39
  7.1 4.8 %collective-permute-start.2 = (f32[4,2,2,8,128]{4,3,1,0,2:T(8,128)S(1)}, f32[4,2,2,8,128]{4,3,1,0,2:T(8,128)S(1)}, u32[]{:S(2)}, u32[]{:S(2)}) collective-permute-start(f32[4,2,2,8,128]{4,3,1,0,2:T(8,128)S(1)} %pad_maximum_fusion.1), channel_id=1, source_target_pairs={{0,4},{4,0},{1,5},{5,1},{2,6},{6,2},{3,7},{7,3},{8,12},{12,8},{9,1... | collective-permute-start | bytes 196616 | tf_op jit(solution)/shard_map/ppermute | solution.py:29
  12.0 6.8 %collective-permute-start.4 = (f32[4,4,1,8,128]{4,3,1,0,2:T(8,128)S(1)}, f32[4,4,1,8,128]{4,3,1,0,2:T(8,128)S(1)}, u32[]{:S(2)}, u32[]{:S(2)}) collective-permute-start(f32[4,4,1,8,128]{4,3,1,0,2:T(8,128)S(1)} %get-tuple-element.70), channel_id=1, source_target_pairs={{0,1},{1,0},{2,3},{3,2},{4,5},{5,4},{6,7},{7,6},{8,9},{9,8},{10,11... | collective-permute-start | bytes 196616 | tf_op jit(solution)/shard_map/ppermute | solution.py:38
  13.2 7.8 %collective-permute-start.3 = (f32[4,4,1,8,128]{4,3,1,0,2:T(8,128)S(1)}, f32[4,4,1,8,128]{4,3,1,0,2:T(8,128)S(1)}, u32[]{:S(2)}, u32[]{:S(2)}) collective-permute-start(f32[4,4,1,8,128]{4,3,1,0,2:T(8,128)S(1)} %get-tuple-element.71), channel_id=1, source_target_pairs={{0,3},{1,2},{2,1},{3,0},{4,7},{5,6},{6,5},{7,4},{8,11},{9,10},{10,... | collective-permute-start | bytes 196616 | tf_op jit(solution)/shard_map/ppermute | solution.py:39
  23.3 5.6 %collective-permute-start.6 = (f32[1,2,2,1,128]{4,1,0,3,2:T(2,128)S(1)}, f32[1,2,2,1,128]{4,1,0,3,2:T(2,128)S(1)}, u32[]{:S(2)}, u32[]{:S(2)}) collective-permute-start(f32[1,2,2,1,128]{4,1,0,3,2:T(2,128)S(1)} %copy.24), channel_id=1, source_target_pairs={{0,8},{8,0},{16,24},{24,16},{1,9},{9,1},{17,25},{25,17},{2,10},{10... | collective-permute-start | bytes 6152 | tf_op jit(solution)/shard_map/ppermute | solution.py:38
  23.3 5.5 %collective-permute-start.5 = (f32[1,2,2,1,128]{4,1,0,3,2:T(2,128)S(1)}, f32[1,2,2,1,128]{4,1,0,3,2:T(2,128)S(1)}, u32[]{:S(2)}, u32[]{:S(2)}) collective-permute-start(f32[1,2,2,1,128]{4,1,0,3,2:T(2,128)S(1)} %copy.23), channel_id=1, source_target_pairs={{0,24},{8,16},{16,8},{24,0},{1,25},{9,17},{17,9},{25,1},{2,26},{10... | collective-permute-start | bytes 6152 | tf_op jit(solution)/shard_map/ppermute | solution.py:39
  28.9 3.7 %collective-permute-start.7 = (f32[4,2,2,1,128]{4,1,0,3,2:T(2,128)S(1)}, f32[4,2,2,1,128]{4,1,0,3,2:T(2,128)S(1)}, u32[]{:S(2)}, u32[]{:S(2)}) collective-permute-start(f32[4,2,2,1,128]{4,1,0,3,2:T(2,128)S(1)} %pad_maximum_fusion.6), channel_id=1, source_target_pairs={{0,4},{4,0},{1,5},{5,1},{2,6},{6,2},{3,7},{7,3},{8,12},{12,8},{9,1... | collective-permute-start | bytes 24584 | tf_op jit(solution)/shard_map/ppermute | solution.py:29
  32.7 3.7 %collective-permute-start.9 = (f32[4,4,1,1,128]{4,1,0,3,2:T(4,128)S(1)}, f32[4,4,1,1,128]{4,1,0,3,2:T(4,128)S(1)}, u32[]{:S(2)}, u32[]{:S(2)}) collective-permute-start(f32[4,4,1,1,128]{4,1,0,3,2:T(4,128)S(1)} %get-tuple-element.86), channel_id=1, source_target_pairs={{0,1},{1,0},{2,3},{3,2},{4,5},{5,4},{6,7},{7,6},{8,9},{9,8},{10,11... | collective-permute-start | bytes 24584 | tf_op jit(solution)/shard_map/ppermute | solution.py:38
  32.8 5.5 %collective-permute-start.8 = (f32[4,4,1,1,128]{4,1,0,3,2:T(4,128)S(1)}, f32[4,4,1,1,128]{4,1,0,3,2:T(4,128)S(1)}, u32[]{:S(2)}, u32[]{:S(2)}) collective-permute-start(f32[4,4,1,1,128]{4,1,0,3,2:T(4,128)S(1)} %get-tuple-element.87), channel_id=1, source_target_pairs={{0,3},{1,2},{2,1},{3,0},{4,7},{5,6},{6,5},{7,4},{8,11},{9,10},{10,... | collective-permute-start | bytes 24584 | tf_op jit(solution)/shard_map/ppermute | solution.py:39
  36.4 1.9 %copy-start = (f32[2,2,2,128]{3,2,1,0:T(2,128)S(1)}, f32[2,2,2,128]{3,2,1,0:T(2,128)}, u32[]{:S(2)}) copy-start(f32[2,2,2,128]{3,2,1,0:T(2,128)} %refs_11_.1) | copy-start | bytes 12292
  40.0 4.0 %collective-permute-start.11 = (f32[1,2,2,4,128]{4,3,1,0,2:T(4,128)S(1)}, f32[1,2,2,4,128]{4,3,1,0,2:T(4,128)S(1)}, u32[]{:S(2)}, u32[]{:S(2)}) collective-permute-start(f32[1,2,2,4,128]{4,3,1,0,2:T(4,128)S(1)} %copy.28), channel_id=1, source_target_pairs={{0,8},{8,0},{16,24},{24,16},{1,9},{9,1},{17,25},{25,17},{2,10},{10... | collective-permute-start | bytes 24584 | tf_op jit(solution)/shard_map/ppermute | solution.py:38
  40.1 4.0 %collective-permute-start.10 = (f32[1,2,2,4,128]{4,3,1,0,2:T(4,128)S(1)}, f32[1,2,2,4,128]{4,3,1,0,2:T(4,128)S(1)}, u32[]{:S(2)}, u32[]{:S(2)}) collective-permute-start(f32[1,2,2,4,128]{4,3,1,0,2:T(4,128)S(1)} %copy.27), channel_id=1, source_target_pairs={{0,24},{8,16},{16,8},{24,0},{1,25},{9,17},{17,9},{25,1},{2,26},{10... | collective-permute-start | bytes 24584 | tf_op jit(solution)/shard_map/ppermute | solution.py:39
  44.1 4.0 %collective-permute-start.12 = (f32[4,2,2,4,128]{4,3,1,0,2:T(4,128)S(1)}, f32[4,2,2,4,128]{4,3,1,0,2:T(4,128)S(1)}, u32[]{:S(2)}, u32[]{:S(2)}) collective-permute-start(f32[4,2,2,4,128]{4,3,1,0,2:T(4,128)S(1)} %pad_maximum_fusion.3), channel_id=1, source_target_pairs={{0,4},{4,0},{1,5},{5,1},{2,6},{6,2},{3,7},{7,3},{8,12},{12,8},{9,1... | collective-permute-start | bytes 98312 | tf_op jit(solution)/shard_map/ppermute | solution.py:29
  48.1 4.0 %collective-permute-start.14 = (f32[4,4,1,4,128]{4,3,1,0,2:T(4,128)S(1)}, f32[4,4,1,4,128]{4,3,1,0,2:T(4,128)S(1)}, u32[]{:S(2)}, u32[]{:S(2)}) collective-permute-start(f32[4,4,1,4,128]{4,3,1,0,2:T(4,128)S(1)} %get-tuple-element.72), channel_id=1, source_target_pairs={{0,1},{1,0},{2,3},{3,2},{4,5},{5,4},{6,7},{7,6},{8,9},{9,8},{10,11... | collective-permute-start | bytes 98312 | tf_op jit(solution)/shard_map/ppermute | solution.py:38
  48.2 5.8 %collective-permute-start.13 = (f32[4,4,1,4,128]{4,3,1,0,2:T(4,128)S(1)}, f32[4,4,1,4,128]{4,3,1,0,2:T(4,128)S(1)}, u32[]{:S(2)}, u32[]{:S(2)}) collective-permute-start(f32[4,4,1,4,128]{4,3,1,0,2:T(4,128)S(1)} %get-tuple-element.73), channel_id=1, source_target_pairs={{0,3},{1,2},{2,1},{3,0},{4,7},{5,6},{6,5},{7,4},{8,11},{9,10},{10,... | collective-permute-start | bytes 98312 | tf_op jit(solution)/shard_map/ppermute | solution.py:39

commit v3 on v2

--- a/solution.py
+++ b/solution.py
@@ -115,13 +115,25 @@
     )
 
 
-def prepare_kernel(counts_ref, base_ref, out_ref):
-    nx, ny, channels, nz, slots = base_ref.shape
+def prepare_kernel(*refs):
+    sources, out_ref, holds, sems = refs[:4], refs[4], refs[5:9], refs[9]
+    copies = [
+        pltpu.make_async_copy(source, hold, sems.at[i])
+        for i, (source, hold) in enumerate(zip(sources, holds))
+    ]
+    for copy in copies:
+        copy.start()
+    for copy in copies:
+        copy.wait()
+    counts_ref, offsets_ref, velocity_ref, mass_ref = holds
+    nx, ny, nz = mass_ref.shape[:3]
     for leaf, (x, y, z) in enumerate(itertools.product(range(nx), range(ny), range(nz))):
-        for c in range(channels):
-            out_ref[leaf, c : c + 1, :] = base_ref[x, y, c, z : z + 1, :]
+        for c in range(3):
+            out_ref[leaf, c : c + 1, :] = offsets_ref[x, y, c, z : z + 1, :]
+            out_ref[leaf, 4 + c : 5 + c, :] = velocity_ref[x, y, c, z : z + 1, :]
+        out_ref[leaf, 3:4, :] = mass_ref[x, y, z : z + 1, :]
         number = counts_ref[x, y : y + 1, z : z + 1].astype(jnp.float32)
-        out_ref[leaf, channels : channels + 1, :] = jnp.broadcast_to(number, (1, slots))
+        out_ref[leaf, 7:8, :] = jnp.broadcast_to(number, (1, mass_ref.shape[3]))
 
 
 def partners(grid):
@@ -211,34 +223,38 @@
     return lax.broadcasted_iota(jnp.int32, (rows, 128), 1)
 
 
-def pack_places(part, mask_ref, counts_ref, source_ref, list_ref, shift_ref, tile_ref, last_ref, all_ref):
+def pack_places(part, mask_ref, counts_ref, source_ref, list_ref, start_ref, last_ref, all_ref, other_ref):
+    stride = longest(part.lists) + 1
+    for index, found in enumerate(part.lists):
+        kept, other = jnp.int32(0), jnp.int32(0)
+        for number, (k, place) in enumerate(found):
+            start_ref[index * stride + number] = kept
+            other_ref[index * stride + number] = other
+            size = counts_ref[place]
+            chosen = size * mask_ref[part.mask_at(index, k)]
+            kept, other = kept + chosen, other + (size - chosen)
+        start_ref[index * stride + len(found)] = kept
+        last_ref[index] = split_place(kept + 127)[1]
+        other_ref[index * stride + len(found)] = other
+        all_ref[index] = split_place(kept + other + 127)[1]
+
     lanes = lane_ids(8)
     only_places = lax.broadcasted_iota(jnp.int32, (8, 128), 0) < 3
     far = column_constant((FAR, FAR, FAR), 8)
-    stride = longest(part.lists) + 1
     for index, found in enumerate(part.lists):
-        start = jnp.int32(0)
         for number, (k, place) in enumerate(found):
-            shift, tile = split_place(start)
-            shift_ref[index * stride + number] = shift
-            tile_ref[index * stride + number] = tile
+            shift, tile = split_place(start_ref[index * stride + number])
             put(list_ref, index, shift, tile, source_ref[place] + part.move(k), lanes)
-            start = start + counts_ref[place] * mask_ref[part.mask_at(index, k)]
-        shift, tile = split_place(start)
-        shift_ref[index * stride + len(found)] = shift
-        tile_ref[index * stride + len(found)] = tile
-        last_ref[index] = split_place(start + 127)[1]
-        for k, place in found:
-            shift, tile = split_place(start)
+        kept = start_ref[index * stride + len(found)]
+        for number, (k, place) in enumerate(found):
+            shift, tile = split_place(kept + other_ref[index * stride + number])
             block = jnp.where(only_places, source_ref[place] + part.move(k), 0.0)
             put(list_ref, index, shift, tile, block, lanes)
-            start = start + counts_ref[place] * (1 - mask_ref[part.mask_at(index, k)])
-        shift, tile = split_place(start)
+        shift, tile = split_place(kept + other_ref[index * stride + len(found)])
         close(list_ref, index, shift, tile, far, lanes)
-        all_ref[index] = split_place(start + 127)[1]
-
-
-def pack_side(part, span, source_ref, side_ref, shift_ref, tile_ref, tail):
+
+
+def pack_side(part, span, source_ref, side_ref, start_ref, tail):
     height = source_ref.shape[1]
     lanes = lane_ids(height)
     last = column_constant(tail, height)
@@ -246,10 +262,10 @@
     for index in range(*span):
         found = part.lists[index]
         for number, (_, place) in enumerate(found):
-            at = index * stride + number
-            put(side_ref, index, shift_ref[at], tile_ref[at], source_ref[place], lanes)
-        at = index * stride + len(found)
-        close(side_ref, index, shift_ref[at], tile_ref[at], last, lanes)
+            shift, tile = split_place(start_ref[index * stride + number])
+            put(side_ref, index, shift, tile, source_ref[place], lanes)
+        shift, tile = split_place(start_ref[index * stride + len(found)])
+        close(side_ref, index, shift, tile, last, lanes)
 
 
 def widen_kernel(rows, block_ref, out_ref):
@@ -351,38 +367,38 @@
     numbers_ref = refs.pop(0) if stage else None
     mask_ref, source_ref, wide_ref = refs[:3]
     before_ref = refs[3] if stage else None
-    acc_ref, counts_ref, list_ref, shift_ref, tile_ref, last_ref, kept_ref = refs[4 if stage else 3 :][:7]
-    all_ref = refs[-1]
+    acc_ref, counts_ref, list_ref, start_ref, last_ref, kept_ref = refs[4 if stage else 3 :][:6]
+    all_ref, other_ref = refs[-2:]
     read_counts(source_ref, counts_ref)
     if numbers_ref is None:
         numbers_ref = counts_ref
         numbers_ref[source_ref.shape[0]] = mask_ref[part.mask_count]
     part.bind(mask_ref[part.mask_count])
-    pack_places(part, mask_ref, counts_ref, source_ref, list_ref, shift_ref, tile_ref, last_ref, all_ref)
+    pack_places(part, mask_ref, counts_ref, source_ref, list_ref, start_ref, last_ref, all_ref, other_ref)
     run_pairs(
         part, (0, len(part.lists)), volume_pair, 1, numbers_ref, all_ref,
         own_reader((wide_ref, WIDE)), row_reader(list_ref), kept_ref, before_ref, acc_ref,
     )
     if stage == 3:
-        out_ref = refs[-2]
+        out_ref = refs[-3]
         for index, leaf, sums, valid in leaf_totals(grid, acc_ref, numbers_ref):
             out_ref[leaf] = jnp.where(valid, 1.0 / (1.0 + 4.0 * sums[0]), 1.0)
 
 
 def density_kernel(grid, part, stage, span, *refs):
-    numbers_ref, list_ref, shift_ref, tile_ref, last_ref, kept_ref, wide_ref, source_ref = refs[:8]
-    before_ref = refs[8] if stage or span[0] else None
-    acc_ref = refs[12 if stage == 3 else 9 if before_ref is not None else 8]
+    numbers_ref, list_ref, start_ref, last_ref, kept_ref, wide_ref, source_ref = refs[:7]
+    before_ref = refs[7] if stage or span[0] else None
+    acc_ref = refs[11 if stage == 3 else 8 if before_ref is not None else 7]
     side_ref = refs[-1]
     part.bind(numbers_ref[numbers_ref.shape[0] - 1])
-    pack_side(part, span, source_ref, side_ref, shift_ref, tile_ref, ())
+    pack_side(part, span, source_ref, side_ref, start_ref, ())
     run_pairs(
         part, span, density_pair, 3, numbers_ref, last_ref, own_reader((wide_ref, WIDE)),
         row_reader(list_ref, side_ref, 7), kept_ref, before_ref if stage else None, acc_ref,
     )
     if stage == 3:
-        own_ref, volume_ref, energy_ref = refs[9:12]
-        out_ref = refs[13]
+        own_ref, volume_ref, energy_ref = refs[8:11]
+        out_ref = refs[12]
         for (x, y, z), leaf, sums, valid in leaf_totals(grid, acc_ref, numbers_ref):
             density = (own_ref[leaf, 3:4, :] + 4.0 * sums[0]) / (volume_ref[leaf] + 4.0 * sums[1])
             density = jnp.where(valid, density, 1.0)
@@ -394,19 +410,19 @@
 
 
 def force_kernel(grid, part, stage, span, *refs):
-    numbers_ref, list_ref, shift_ref, tile_ref, last_ref, kept_ref, wide_ref, state_ref, source_ref = refs[:9]
-    before_ref = refs[9] if stage or span[0] else None
-    acc_ref = refs[10 if before_ref is not None else 9]
+    numbers_ref, list_ref, start_ref, last_ref, kept_ref, wide_ref, state_ref, source_ref = refs[:8]
+    before_ref = refs[8] if stage or span[0] else None
+    acc_ref = refs[9 if before_ref is not None else 8]
     side_ref = refs[-1]
     part.bind(numbers_ref[numbers_ref.shape[0] - 1])
-    pack_side(part, span, source_ref, side_ref, shift_ref, tile_ref, (1.0,))
+    pack_side(part, span, source_ref, side_ref, start_ref, (1.0,))
     run_pairs(
         part, span, force_pair, 4, numbers_ref, last_ref,
         own_reader((wide_ref, WIDE), (state_ref, (8, 9, 10))), row_reader(list_ref, side_ref),
         kept_ref, before_ref if stage else None, acc_ref,
     )
     if stage == 3:
-        push_ref, heat_ref = refs[11:13]
+        push_ref, heat_ref = refs[10:12]
         for (x, y, z), leaf, sums, valid in leaf_totals(grid, acc_ref, numbers_ref):
             for c in range(3):
                 push_ref[x, y, c, z : z + 1, :] = jnp.where(valid, 20.0 * sums[c], 0.0)
@@ -449,9 +465,17 @@
     assert slots == 128
     leaves = grid[0] * grid[1] * grid[2]
     parts = [Layers(grid, part) for part in partners(grid)] + [Side(grid, True), Side(grid, False)]
-    pieces = [jnp.swapaxes(x, 2, 3) for x in (offsets, mass[:, :, :, None], velocity)]
-    base = jnp.concatenate(pieces, axis=2)
-    own = call("prepare", prepare_kernel, [counts, base], [floats(leaves, 8, slots)])[0]
+    inputs = [counts, jnp.swapaxes(offsets, 2, 3), jnp.swapaxes(velocity, 2, 3), mass]
+    inputs = [pltpu.with_memory_space_constraint(x, pltpu.HBM) for x in inputs]
+    own = pl.pallas_call(
+        prepare_kernel,
+        out_shape=floats(leaves, 8, slots),
+        in_specs=[pl.BlockSpec(memory_space=pltpu.HBM)] * 4,
+        out_specs=pl.BlockSpec(memory_space=pltpu.VMEM),
+        scratch_shapes=[pltpu.VMEM(x.shape, x.dtype) for x in inputs] + [pltpu.SemaphoreType.DMA((4,))],
+        compiler_params=pltpu.CompilerParams(vmem_limit_bytes=ROOM),
+        name="prepare",
+    )(*inputs)
     one_is_high = jnp.ones((1,), jnp.int32)
     if lax.axis_size("gz") > 2 and lax.axis_size("gz") % 2 == 0:
         one_is_high = 1 - lax.axis_index("gz").astype(jnp.int32)[None] % 2
@@ -473,9 +497,8 @@
     def list_outs(p):
         lists = parts[p].lists
         count, tiles = len(lists), list_tiles(lists)
-        numbers = integers(count * (longest(lists) + 1))
         return [
-            floats(count, tiles, 8, slots), numbers, numbers, integers(count),
+            floats(count, tiles, 8, slots), integers(count * (longest(lists) + 1)), integers(count),
             floats(count, tiles, slots, slots),
         ]
 
@@ -487,12 +510,16 @@
         acc, number, *packed = call(
             f"volume_{p}", functools.partial(volume_kernel, grid, parts[p], p), inputs,
             outs + ([floats(leaves, 1, slots)] if p == 3 else []),
-            [pltpu.SMEM((len(parts[p].lists),), jnp.int32)], cycles=3000,
+            [
+                pltpu.SMEM((len(parts[p].lists),), jnp.int32),
+                pltpu.SMEM((len(parts[p].lists) * (longest(parts[p].lists) + 1),), jnp.int32),
+            ],
+            cycles=3000,
             aliases=[(len(inputs) - 1, 0)] if before else (),
         )
         numbers.append(number)
-        packs.append(packed[:5])
-        return [packed[5] if p == 3 else acc]
+        packs.append(packed[:4])
+        return [packed[4] if p == 3 else acc]
 
     def density_part(p, source, before=(), more=(), span=None):
         span = span or (0, len(parts[p].lists))
@@ -500,7 +527,7 @@
             f"density_{p}", functools.partial(density_kernel, grid, parts[p], p, span),
             [numbers[0], *packs[p], wide, source, *before, *more],
             [spread(3)] + ([floats(leaves, 4, slots)] if p == 3 else []),
-            [side_space(p, 1)], cycles=4000, aliases=[(8, 0)] if before else (),
+            [side_space(p, 1)], cycles=4000, aliases=[(7, 0)] if before else (),
         )[-1:]
 
     def force_part(p, source, before=(), span=None):
@@ -510,7 +537,7 @@
             f"force_{p}", functools.partial(force_kernel, grid, parts[p], p, span),
             [numbers[0], *packs[p], wide, wide_state, source, *before],
             [spread(4)] + (final if p == 3 else []),
-            [side_space(p, 4)], cycles=5000, aliases=[(9, 0)] if before else (),
+            [side_space(p, 4)], cycles=5000, aliases=[(8, 0)] if before else (),
         )[-2:]
 
     early = []

time: 56.3 us -> 54.7 us (0.972)
  waiting for transfers between devices: 6.64 us -> 10.3 us
  starting transfers between devices: 16.6 us -> 14.3 us
  Pallas kernels: 29.7 us -> 27.8 us
  other arithmetic: 0.98 us -> 0.22 us
  local copies, waits for them, and re-layouts: 1.52 us -> 0.84 us
    ppermute x6, starting transfers between devices: 12.9 us -> 5.35 us  [ends_of(): two = lax.ppermute(jnp.where(even, first, last), axis, far_pairs)]
    ppermute x6, starting transfers between devices: 2.04 us -> 6.72 us  [ends_of(): one = lax.ppermute(jnp.where(even, last, first), axis, near_pairs)]
    ppermute x6, waiting for transfers between devices: 0.83 us -> 4.73 us  [ends_of(): two = lax.ppermute(jnp.where(even, first, last), axis, far_pairs)]
    pallas_call x17 -> x16, Pallas kernels: 29.7 us -> 26.9 us  [call(): pl.pallas_call(body, out_shape=outs, in_specs=[spec(x) for x in inputs],...]
    pallas_call x0 -> x1, Pallas kernels: none -> 0.87 us  [shards(): pl.pallas_call(prepare_kernel, out_shape=floats(leaves, 8, slots), in_spe...]
    concatenate x1 -> x0, other arithmetic: 0.76 us -> none  [shards(): base = jnp.concatenate(pieces, axis=2)]
    ppermute x6, waiting for transfers between devices: 1.71 us -> 1.02 us  [ends_of(): one = lax.ppermute(jnp.where(even, last, first), axis, near_pairs)]
    unnamed x4 -> x2, local copies, waits for them, and re-layouts: 0.68 us -> 0.01 us
  transfers between devices with their start and end apart: 15 -> 15, of which waited for: 6 -> 8; matrix products, arithmetic and copies ran while one was open for 2% -> 2% of each run, Pallas kernels for 41% -> 38%
where the time goes in v3:
time: 54.7 us; the launch traced here: 54.4 us
  Pallas kernels  27.8 us (51%)
  starting transfers between devices  14.3 us (26%)
  waiting for transfers between devices  10.3 us (19%)
  between operations  1.01 us (2%)
  local copies, waits for them, and re-layouts  0.84 us (2%)
    pallas_call x16, Pallas kernels, call(): pl.pallas_call(body, out_shape=outs, in_specs=[spec(x) for x in inputs],...  26.9 us
    ppermute x6, starting transfers between devices, ends_of(): one = lax.ppermute(jnp.where(even, last, first), axis, near_pairs)  6.72 us
    ppermute x6, starting transfers between devices, ends_of(): two = lax.ppermute(jnp.where(even, first, last), axis, far_pairs)  5.35 us
    ppermute x6, waiting for transfers between devices, ends_of(): two = lax.ppermute(jnp.where(even, first, last), axis, far_pairs)  4.73 us
    ppermute x3, waiting for transfers between devices, ends_of(): ends = lax.ppermute(ends, axis, [(0, 1), (1, 0)])  4.52 us
    ppermute x3, starting transfers between devices, ends_of(): ends = lax.ppermute(ends, axis, [(0, 1), (1, 0)])  2.23 us
  transfers between devices with their start and end apart: 15, of which 8 were waited for; matrix products, arithmetic and copies ran while one was open for 2% of the time, Pallas kernels for 38%

profile of v3, /device:TPU:0, one launch (start us, length us, event | category | flops | bytes accessed | tf_op | source)
XLA Modules:
  0.0 54.4 jit_solution(15986586439450299732)
XLA Ops:
  2.1 2.6 %collective-permute-start = (f32[1,2,2,8,128]{4,3,1,0,2:T(8,128)S(1)}, f32[1,2,2,8,128]{4,3,1,0,2:T(8,128)S(1)}, u32[]{:S(2)}, u32[]{:S(2)}) collective-permute-start(f32[1,2,2,8,128]{4,3,1,0,2:T(8,128)S(1)} %copy.19), channel_id=1, source_target_pairs={{0,24},{8,16},{16,8},{24,0},{1,25},{9,17},{17,9},{25,1},{2,26},{10... | collective-permute-start | bytes 49160 | tf_op jit(solution)/shard_map/ppermute | solution.py:39
  6.4 1.6 %collective-permute-start.2 = (f32[4,2,2,8,128]{4,3,1,0,2:T(8,128)S(1)}, f32[4,2,2,8,128]{4,3,1,0,2:T(8,128)S(1)}, u32[]{:S(2)}, u32[]{:S(2)}) collective-permute-start(f32[4,2,2,8,128]{4,3,1,0,2:T(8,128)S(1)} %pad_maximum_fusion.1), channel_id=1, source_target_pairs={{0,4},{4,0},{1,5},{5,1},{2,6},{6,2},{3,7},{7,3},{8,12},{12,8},{9,1... | collective-permute-start | bytes 196616 | tf_op jit(solution)/shard_map/ppermute | solution.py:29
  8.1 2.7 %volume_0.1 = (f32[8,1,128,128]{3,2,1,0:T(8,128)S(1)}, s32[9]{0:T(128)S(1)}, f32[8,10,8,128]{3,2,1,0:T(8,128)S(1)}, s32[72]{0:T(128)S(1)}, s32[8]{0:T(128)S(1)}, /*index=5*/f32[8,10,128,128]{3,2,1,0:T(8,128)S(1)}) custom-call(s32[217]{0:T(256)S(1)} %pad_add_fusion.refs_0_.refs_1_, f32[8,8,128]{2,1,0:T(8,128)S(1)} %prepare.1.block_ref.refs_1_.refs_8_, ...), custom_call_target="tpu_custom_call" | custom-call | flops 12288000 | bytes 1048576 | tf_op jit(solution)/shard_map/volume_0/pallas_call | solution.py:437
  10.8 3.2 %collective-permute-start.4 = (f32[4,4,1,8,128]{4,3,1,0,2:T(8,128)S(1)}, f32[4,4,1,8,128]{4,3,1,0,2:T(8,128)S(1)}, u32[]{:S(2)}, u32[]{:S(2)}) collective-permute-start(f32[4,4,1,8,128]{4,3,1,0,2:T(8,128)S(1)} %get-tuple-element.62), channel_id=1, source_target_pairs={{0,1},{1,0},{2,3},{3,2},{4,5},{5,4},{6,7},{7,6},{8,9},{9,8},{10,11... | collective-permute-start | bytes 196616 | tf_op jit(solution)/shard_map/ppermute | solution.py:38
  14.1 1.0 %collective-permute-start.3 = (f32[4,4,1,8,128]{4,3,1,0,2:T(8,128)S(1)}, f32[4,4,1,8,128]{4,3,1,0,2:T(8,128)S(1)}, u32[]{:S(2)}, u32[]{:S(2)}) collective-permute-start(f32[4,4,1,8,128]{4,3,1,0,2:T(8,128)S(1)} %get-tuple-element.63), channel_id=1, source_target_pairs={{0,3},{1,2},{2,1},{3,0},{4,7},{5,6},{6,5},{7,4},{8,11},{9,10},{10,... | collective-permute-start | bytes 196616 | tf_op jit(solution)/shard_map/ppermute | solution.py:39
  15.0 2.9 %volume_1.1 = (f32[8,1,128,128]{3,2,1,0:T(8,128)S(1)}, s32[32]{0:T(128)}, f32[8,12,8,128]{3,2,1,0:T(8,128)S(1)}, s32[88]{0:T(128)S(1)}, s32[8]{0:T(128)S(1)}, /*index=5*/f32[8,12,128,128]{3,2,1,0:T(8,128)S(1)}) custom-call(s32[9]{0:T(128)S(1)} %get-tuple-element.32.refs_0_, s32[217]{0:T(256)S(1)} %pad_add_fusion.refs_0_.refs_1_, ...), custom_call_target="tpu_custom_call", output_to_operand_aliasing={{0}: (4, {})} | custom-call | flops 12288000 | bytes 1048576 | tf_op jit(solution)/shard_map/volume_1/pallas_call | solution.py:437
  18.0 2.1 %volume_2.1 = (f32[8,1,128,128]{3,2,1,0:T(8,128)S(1)}, s32[16]{0:T(128)}, f32[4,11,8,128]{3,2,1,0:T(8,128)S(1)}, s32[40]{0:T(128)S(1)}, s32[4]{0:T(128)S(1)}, /*index=5*/f32[4,11,128,128]{3,2,1,0:T(8,128)S(1)}) custom-call(s32[9]{0:T(128)S(1)} %get-tuple-element.32.refs_0_, s32[217]{0:T(256)S(1)} %pad_add_fusion.refs_0_.refs_1_, ...), custom_call_target="tpu_custom_call", output_to_operand_aliasing={{0}: (4, {})} | custom-call | flops 12288000 | bytes 1048576 | tf_op jit(solution)/shard_map/volume_2/pallas_call | solution.py:437
  20.1 2.0 %volume_3.1 = (f32[8,1,128,128]{3,2,1,0:T(8,128)S(1)}, s32[16]{0:T(128)}, f32[4,11,8,128]{3,2,1,0:T(8,128)S(1)}, s32[40]{0:T(128)S(1)}, s32[4]{0:T(128)S(1)}, /*...) custom-call(s32[9]{0:T(128)S(1)} %get-tuple-element.32.refs_0_, ...), custom_call_target="tpu_custom_call", output_to_operand_aliasing={{0}: (4, {})} | custom-call | flops 12288000 | bytes 1048576 | tf_op jit(solution)/shard_map/volume_3/pallas_call | solution.py:437
  22.8 1.2 %density_0.2.refs_7_ = f32[8,3,128,128]{3,2,1,0:T(8,128)S(1)} custom-call(s32[9]{0:T(128)S(1)} %get-tuple-element.32.refs_0_, f32[8,10,8,128]{3,2,1,0:T(8,128)S(1)} %get-tuple-element.43.refs_1_, s32[72]{0:T(128)S(1)} %get-tuple-element.44.refs_2_, s32[8]{0:T(128)S(1)} %get-tuple-element.45.refs_3_, f32[8,10,128,128]{3,2,1,0:T(8,128)S(1)} %get-tuple-element.46.refs_4_, ...), custom_call_target="tpu_custom_call" | custom-call | flops 16384000 | bytes 1048576 | tf_op jit(solution)/shard_map/density_0/pallas_call | solution.py:437
  24.1 1.2 %collective-permute-done.5 = f32[1,2,2,1,128]{4,1,0,3,2:T(2,128)S(1)} collective-permute-done((f32[1,2,2,1,128]{4,1,0,3,2:T(2,128)S(1)}, f32[1,2,2,1,128]{4,1,0,3,2:T(2,128)S(1)}, u32[]{:S(2)}, u32[]{:S(2)}) %collective-permute-start.5) | collective-permute-done | bytes 2080 | tf_op jit(solution)/shard_map/ppermute | solution.py:39
  25.9 1.2 %density_0.3.refs_7_ = f32[8,3,128,128]{3,2,1,0:T(8,128)S(1)} custom-call(s32[9]{0:T(128)S(1)} %get-tuple-element.32.refs_0_, f32[8,10,8,128]{3,2,1,0:T(8,128)S(1)} %get-tuple-element.43.refs_1_, s32[72]{0:T(128)S(1)} %get-tuple-element.44.refs_2_, s32[8]{0:T(128)S(1)} %get-tuple-element.45.refs_3_, ...), custom_call_target="tpu_custom_call", output_to_operand_aliasing={{}: (7, {})} | custom-call | flops 16384000 | bytes 1048576 | tf_op jit(solution)/shard_map/density_0/pallas_call | solution.py:437
  27.1 1.9 %collective-permute-done.7 = f32[4,2,2,1,128]{4,1,0,3,2:T(2,128)S(1)} collective-permute-done((f32[4,2,2,1,128]{4,1,0,3,2:T(2,128)S(1)}, f32[4,2,2,1,128]{4,1,0,3,2:T(2,128)S(1)}, u32[]{:S(2)}, u32[]{:S(2)}) %collective-permute-start.7) | collective-permute-done | bytes 8224 | tf_op jit(solution)/shard_map/ppermute | solution.py:29
  29.0 2.4 %collective-permute-start.9 = (f32[4,4,1,1,128]{4,1,0,3,2:T(4,128)S(1)}, f32[4,4,1,1,128]{4,1,0,3,2:T(4,128)S(1)}, u32[]{:S(2)}, u32[]{:S(2)}) collective-permute-start(f32[4,4,1,1,128]{4,1,0,3,2:T(4,128)S(1)} %get-tuple-element.78), channel_id=1, source_target_pairs={{0,1},{1,0},{2,3},{3,2},{4,5},{5,4},{6,7},{7,6},{8,9},{9,8},{10,11... | collective-permute-start | bytes 24584 | tf_op jit(solution)/shard_map/ppermute | solution.py:38
  31.5 1.9 %density_1.1.refs_7_ = f32[8,3,128,128]{3,2,1,0:T(8,128)S(1)} custom-call(s32[9]{0:T(128)S(1)} %get-tuple-element.32.refs_0_, f32[8,12,8,128]{3,2,1,0:T(8,128)S(1)} %get-tuple-element.53.refs_1_, s32[88]{0:T(128)S(1)} %get-tuple-element.54.refs_2_, s32[8]{0:T(128)S(1)} %get-tuple-element.55.refs_3_, ...), custom_call_target="tpu_custom_call", output_to_operand_aliasing={{}: (7, {})} | custom-call | flops 16384000 | bytes 1048576 | tf_op jit(solution)/shard_map/density_1/pallas_call | solution.py:437
  33.4 1.3 %density_2.1.refs_7_ = f32[8,3,128,128]{3,2,1,0:T(8,128)S(1)} custom-call(s32[9]{0:T(128)S(1)} %get-tuple-element.32.refs_0_, f32[4,11,8,128]{3,2,1,0:T(8,128)S(1)} %get-tuple-element.49.refs_1_, s32[40]{0:T(128)S(1)} %get-tuple-element.50.refs_2_, s32[4]{0:T(128)S(1)} %get-tuple-element.51.refs_3_, ...), custom_call_target="tpu_custom_call", output_to_operand_aliasing={{}: (7, {})} | custom-call | flops 16384000 | bytes 1048576 | tf_op jit(solution)/shard_map/density_2/pallas_call | solution.py:437
  34.7 2.2 %collective-permute-done.8 = f32[4,4,1,1,128]{4,1,0,3,2:T(4,128)S(1)} collective-permute-done((f32[4,4,1,1,128]{4,1,0,3,2:T(4,128)S(1)}, f32[4,4,1,1,128]{4,1,0,3,2:T(4,128)S(1)}, u32[]{:S(2)}, u32[]{:S(2)}) %collective-permute-start.8) | collective-permute-done | bytes 8224 | tf_op jit(solution)/shard_map/ppermute | solution.py:39
  36.9 1.6 %density_3.1 = (f32[8,3,128,128]{3,2,1,0:T(8,128)S(1)}, f32[8,4,128]{2,1,0:T(4,128)S(1)}) custom-call(s32[9]{0:T(128)S(1)} %get-tuple-element.32.refs_0_, f32[4,11,8,128]{3,2,1,0:T(8,128)S(1)} %get-tuple-element.38.refs_1_, s32[40]{0:T(128)S(1)} %get-tuple-element.39.refs_2_, s32[4]{0:T(128)S(1)} %get-tuple-element.40.refs_3_, ...), custom_call_target="tpu_custom_call", output_to_operand_aliasing={{0}: (7, {})} | custom-call | flops 16384000 | bytes 1048576 | tf_op jit(solution)/shard_map/density_3/pallas_call | solution.py:437
  39.5 1.4 %force_0.2.refs_8_ = f32[8,4,128,128]{3,2,1,0:T(8,128)S(1)} custom-call(s32[9]{0:T(128)S(1)} %get-tuple-element.32.refs_0_, f32[8,10,8,128]{3,2,1,0:T(8,128)S(1)} %get-tuple-element.43.refs_1_, s32[72]{0:T(128)S(1)} %get-tuple-element.44.refs_2_, s32[8]{0:T(128)S(1)} %get-tuple-element.45.refs_3_, f32[8,10,128,128]{3,2,1,0:T(8,128)S(1)} %get-tuple-element.46.refs_4_, ...), custom_call_target="tpu_custom_call" | custom-call | flops 20480000 | bytes 1048576 | tf_op jit(solution)/shard_map/force_0/pallas_call | solution.py:437
  41.9 1.3 %force_0.3.refs_8_ = f32[8,4,128,128]{3,2,1,0:T(8,128)S(1)} custom-call(s32[9]{0:T(128)S(1)} %get-tuple-element.32.refs_0_, f32[8,10,8,128]{3,2,1,0:T(8,128)S(1)} %get-tuple-element.43.refs_1_, s32[72]{0:T(128)S(1)} %get-tuple-element.44.refs_2_, s32[8]{0:T(128)S(1)} %get-tuple-element.45.refs_3_, ...), custom_call_target="tpu_custom_call", output_to_operand_aliasing={{}: (8, {})} | custom-call | flops 20480000 | bytes 1048576 | tf_op jit(solution)/shard_map/force_0/pallas_call | solution.py:437
  43.2 2.6 %collective-permute-done.12 = f32[4,2,2,4,128]{4,3,1,0,2:T(4,128)S(1)} collective-permute-done((f32[4,2,2,4,128]{4,3,1,0,2:T(4,128)S(1)}, f32[4,2,2,4,128]{4,3,1,0,2:T(4,128)S(1)}, u32[]{:S(2)}, u32[]{:S(2)}) %collective-permute-start.12) | collective-permute-done | bytes 32800 | tf_op jit(solution)/shard_map/ppermute | solution.py:29
  46.9 2.2 %force_1.1.refs_8_ = f32[8,4,128,128]{3,2,1,0:T(8,128)S(1)} custom-call(s32[9]{0:T(128)S(1)} %get-tuple-element.32.refs_0_, f32[8,12,8,128]{3,2,1,0:T(8,128)S(1)} %get-tuple-element.53.refs_1_, s32[88]{0:T(128)S(1)} %get-tuple-element.54.refs_2_, s32[8]{0:T(128)S(1)} %get-tuple-element.55.refs_3_, ...), custom_call_target="tpu_custom_call", output_to_operand_aliasing={{}: (8, {})} | custom-call | flops 20480000 | bytes 1048576 | tf_op jit(solution)/shard_map/force_1/pallas_call | solution.py:437
  49.1 1.0 %collective-permute-done.14 = f32[4,4,1,4,128]{4,3,1,0,2:T(4,128)S(1)} collective-permute-done((f32[4,4,1,4,128]{4,3,1,0,2:T(4,128)S(1)}, f32[4,4,1,4,128]{4,3,1,0,2:T(4,128)S(1)}, u32[]{:S(2)}, u32[]{:S(2)}) %collective-permute-start.14) | collective-permute-done | bytes 32800 | tf_op jit(solution)/shard_map/ppermute | solution.py:38
  50.1 1.4 %force_2.1.refs_8_ = f32[8,4,128,128]{3,2,1,0:T(8,128)S(1)} custom-call(s32[9]{0:T(128)S(1)} %get-tuple-element.32.refs_0_, f32[4,11,8,128]{3,2,1,0:T(8,128)S(1)} %get-tuple-element.49.refs_1_, s32[40]{0:T(128)S(1)} %get-tuple-element.50.refs_2_, s32[4]{0:T(128)S(1)} %get-tuple-element.51.refs_3_, ...), custom_call_target="tpu_custom_call", output_to_operand_aliasing={{}: (8, {})} | custom-call | flops 20480000 | bytes 1048576 | tf_op jit(solution)/shard_map/force_2/pallas_call | solution.py:437
  52.0 2.5 %force_3.1 = (f32[8,4,128,128]{3,2,1,0:T(8,128)S(1)}, f32[2,2,3,2,128]{4,3,2,1,0:T(2,128)}, f32[2,2,2,128]{3,2,1,0:T(2,128)}) custom-call(s32[9]{0:T(128)S(1)} %get-tuple-element.32.refs_0_, f32[4,11,8,128]{3,2,1,0:T(8,128)S(1)} %get-tuple-element.38.refs_1_, s32[40]{0:T(128)S(1)} %get-tuple-element.39.refs_2_, ...), custom_call_target="tpu_custom_call", output_to_operand_aliasing={{0}: (8, {})} | custom-call | flops 20480000 | bytes 1048576 | tf_op jit(solution)/shard_map/force_3/pallas_call | solution.py:437
  (55 shorter events, 8.2 us)
Async XLA Ops:
  1.6 4.8 %collective-permute-start.1 = (f32[1,2,2,8,128]{4,3,1,0,2:T(8,128)S(1)}, f32[1,2,2,8,128]{4,3,1,0,2:T(8,128)S(1)}, u32[]{:S(2)}, u32[]{:S(2)}) collective-permute-start(f32[1,2,2,8,128]{4,3,1,0,2:T(8,128)S(1)} %copy.20), channel_id=1, source_target_pairs={{0,8},{8,0},{16,24},{24,16},{1,9},{9,1},{17,25},{25,17},{2,10},{10... | collective-permute-start | bytes 49160 | tf_op jit(solution)/shard_map/ppermute | solution.py:38
  2.1 4.3 %collective-permute-start = (f32[1,2,2,8,128]{4,3,1,0,2:T(8,128)S(1)}, f32[1,2,2,8,128]{4,3,1,0,2:T(8,128)S(1)}, u32[]{:S(2)}, u32[]{:S(2)}) collective-permute-start(f32[1,2,2,8,128]{4,3,1,0,2:T(8,128)S(1)} %copy.19), channel_id=1, source_target_pairs={{0,24},{8,16},{16,8},{24,0},{1,25},{9,17},{17,9},{25,1},{2,26},{10... | collective-permute-start | bytes 49160 | tf_op jit(solution)/shard_map/ppermute | solution.py:39
  6.4 4.4 %collective-permute-start.2 = (f32[4,2,2,8,128]{4,3,1,0,2:T(8,128)S(1)}, f32[4,2,2,8,128]{4,3,1,0,2:T(8,128)S(1)}, u32[]{:S(2)}, u32[]{:S(2)}) collective-permute-start(f32[4,2,2,8,128]{4,3,1,0,2:T(8,128)S(1)} %pad_maximum_fusion.1), channel_id=1, source_target_pairs={{0,4},{4,0},{1,5},{5,1},{2,6},{6,2},{3,7},{7,3},{8,12},{12,8},{9,1... | collective-permute-start | bytes 196616 | tf_op jit(solution)/shard_map/ppermute | solution.py:29
  10.8 7.1 %collective-permute-start.4 = (f32[4,4,1,8,128]{4,3,1,0,2:T(8,128)S(1)}, f32[4,4,1,8,128]{4,3,1,0,2:T(8,128)S(1)}, u32[]{:S(2)}, u32[]{:S(2)}) collective-permute-start(f32[4,4,1,8,128]{4,3,1,0,2:T(8,128)S(1)} %get-tuple-element.62), channel_id=1, source_target_pairs={{0,1},{1,0},{2,3},{3,2},{4,5},{5,4},{6,7},{7,6},{8,9},{9,8},{10,11... | collective-permute-start | bytes 196616 | tf_op jit(solution)/shard_map/ppermute | solution.py:38
  14.1 6.1 %collective-permute-start.3 = (f32[4,4,1,8,128]{4,3,1,0,2:T(8,128)S(1)}, f32[4,4,1,8,128]{4,3,1,0,2:T(8,128)S(1)}, u32[]{:S(2)}, u32[]{:S(2)}) collective-permute-start(f32[4,4,1,8,128]{4,3,1,0,2:T(8,128)S(1)} %get-tuple-element.63), channel_id=1, source_target_pairs={{0,3},{1,2},{2,1},{3,0},{4,7},{5,6},{6,5},{7,4},{8,11},{9,10},{10,... | collective-permute-start | bytes 196616 | tf_op jit(solution)/shard_map/ppermute | solution.py:39
  22.1 1.9 %collective-permute-start.6 = (f32[1,2,2,1,128]{4,1,0,3,2:T(2,128)S(1)}, f32[1,2,2,1,128]{4,1,0,3,2:T(2,128)S(1)}, u32[]{:S(2)}, u32[]{:S(2)}) collective-permute-start(f32[1,2,2,1,128]{4,1,0,3,2:T(2,128)S(1)} %copy.24), channel_id=1, source_target_pairs={{0,8},{8,0},{16,24},{24,16},{1,9},{9,1},{17,25},{25,17},{2,10},{10... | collective-permute-start | bytes 6152 | tf_op jit(solution)/shard_map/ppermute | solution.py:38
  22.2 3.1 %collective-permute-start.5 = (f32[1,2,2,1,128]{4,1,0,3,2:T(2,128)S(1)}, f32[1,2,2,1,128]{4,1,0,3,2:T(2,128)S(1)}, u32[]{:S(2)}, u32[]{:S(2)}) collective-permute-start(f32[1,2,2,1,128]{4,1,0,3,2:T(2,128)S(1)} %copy.23), channel_id=1, source_target_pairs={{0,24},{8,16},{16,8},{24,0},{1,25},{9,17},{17,9},{25,1},{2,26},{10... | collective-permute-start | bytes 6152 | tf_op jit(solution)/shard_map/ppermute | solution.py:39
  25.3 3.7 %collective-permute-start.7 = (f32[4,2,2,1,128]{4,1,0,3,2:T(2,128)S(1)}, f32[4,2,2,1,128]{4,1,0,3,2:T(2,128)S(1)}, u32[]{:S(2)}, u32[]{:S(2)}) collective-permute-start(f32[4,2,2,1,128]{4,1,0,3,2:T(2,128)S(1)} %pad_maximum_fusion.5), channel_id=1, source_target_pairs={{0,4},{4,0},{1,5},{5,1},{2,6},{6,2},{3,7},{7,3},{8,12},{12,8},{9,1... | collective-permute-start | bytes 24584 | tf_op jit(solution)/shard_map/ppermute | solution.py:29
  29.0 4.3 %collective-permute-start.9 = (f32[4,4,1,1,128]{4,1,0,3,2:T(4,128)S(1)}, f32[4,4,1,1,128]{4,1,0,3,2:T(4,128)S(1)}, u32[]{:S(2)}, u32[]{:S(2)}) collective-permute-start(f32[4,4,1,1,128]{4,1,0,3,2:T(4,128)S(1)} %get-tuple-element.78), channel_id=1, source_target_pairs={{0,1},{1,0},{2,3},{3,2},{4,5},{5,4},{6,7},{7,6},{8,9},{9,8},{10,11... | collective-permute-start | bytes 24584 | tf_op jit(solution)/shard_map/ppermute | solution.py:38
  31.4 5.4 %collective-permute-start.8 = (f32[4,4,1,1,128]{4,1,0,3,2:T(4,128)S(1)}, f32[4,4,1,1,128]{4,1,0,3,2:T(4,128)S(1)}, u32[]{:S(2)}, u32[]{:S(2)}) collective-permute-start(f32[4,4,1,1,128]{4,1,0,3,2:T(4,128)S(1)} %get-tuple-element.79), channel_id=1, source_target_pairs={{0,3},{1,2},{2,1},{3,0},{4,7},{5,6},{6,5},{7,4},{8,11},{9,10},{10,... | collective-permute-start | bytes 24584 | tf_op jit(solution)/shard_map/ppermute | solution.py:39
  33.4 3.5 %copy-start = (f32[2,2,2,128]{3,2,1,0:T(2,128)S(1)}, f32[2,2,2,128]{3,2,1,0:T(2,128)}, u32[]{:S(2)}) copy-start(f32[2,2,2,128]{3,2,1,0:T(2,128)} %refs_10_.1) | copy-start | bytes 12292
  38.5 2.3 %collective-permute-start.11 = (f32[1,2,2,4,128]{4,3,1,0,2:T(4,128)S(1)}, f32[1,2,2,4,128]{4,3,1,0,2:T(4,128)S(1)}, u32[]{:S(2)}, u32[]{:S(2)}) collective-permute-start(f32[1,2,2,4,128]{4,3,1,0,2:T(4,128)S(1)} %copy.28), channel_id=1, source_target_pairs={{0,8},{8,0},{16,24},{24,16},{1,9},{9,1},{17,25},{25,17},{2,10},{10... | collective-permute-start | bytes 24584 | tf_op jit(solution)/shard_map/ppermute | solution.py:38
  38.6 3.1 %collective-permute-start.10 = (f32[1,2,2,4,128]{4,3,1,0,2:T(4,128)S(1)}, f32[1,2,2,4,128]{4,3,1,0,2:T(4,128)S(1)}, u32[]{:S(2)}, u32[]{:S(2)}) collective-permute-start(f32[1,2,2,4,128]{4,3,1,0,2:T(4,128)S(1)} %copy.27), channel_id=1, source_target_pairs={{0,24},{8,16},{16,8},{24,0},{1,25},{9,17},{17,9},{25,1},{2,26},{10... | collective-permute-start | bytes 24584 | tf_op jit(solution)/shard_map/ppermute | solution.py:39
  41.8 4.0 %collective-permute-start.12 = (f32[4,2,2,4,128]{4,3,1,0,2:T(4,128)S(1)}, f32[4,2,2,4,128]{4,3,1,0,2:T(4,128)S(1)}, u32[]{:S(2)}, u32[]{:S(2)}) collective-permute-start(f32[4,2,2,4,128]{4,3,1,0,2:T(4,128)S(1)} %pad_maximum_fusion.3), channel_id=1, source_target_pairs={{0,4},{4,0},{1,5},{5,1},{2,6},{6,2},{3,7},{7,3},{8,12},{12,8},{9,1... | collective-permute-start | bytes 98312 | tf_op jit(solution)/shard_map/ppermute | solution.py:29
  45.8 4.3 %collective-permute-start.14 = (f32[4,4,1,4,128]{4,3,1,0,2:T(4,128)S(1)}, f32[4,4,1,4,128]{4,3,1,0,2:T(4,128)S(1)}, u32[]{:S(2)}, u32[]{:S(2)}) collective-permute-start(f32[4,4,1,4,128]{4,3,1,0,2:T(4,128)S(1)} %get-tuple-element.64), channel_id=1, source_target_pairs={{0,1},{1,0},{2,3},{3,2},{4,5},{5,4},{6,7},{7,6},{8,9},{9,8},{10,11... | collective-permute-start | bytes 98312 | tf_op jit(solution)/shard_map/ppermute | solution.py:38
  46.2 5.7 %collective-permute-start.13 = (f32[4,4,1,4,128]{4,3,1,0,2:T(4,128)S(1)}, f32[4,4,1,4,128]{4,3,1,0,2:T(4,128)S(1)}, u32[]{:S(2)}, u32[]{:S(2)}) collective-permute-start(f32[4,4,1,4,128]{4,3,1,0,2:T(4,128)S(1)} %get-tuple-element.65), channel_id=1, source_target_pairs={{0,3},{1,2},{2,1},{3,0},{4,7},{5,6},{6,5},{7,4},{8,11},{9,10},{10,... | collective-permute-start | bytes 98312 | tf_op jit(solution)/shard_map/ppermute | solution.py:39

commit v4 on v3

--- a/solution.py
+++ b/solution.py
@@ -205,18 +205,23 @@
     return longest(lists) + 2
 
 
-def split_place(start):
-    return start & 127, lax.shift_right_logical(start, 7)
-
-
-def put(list_ref, leaf, shift, tile, block, lanes):
-    rolled = pltpu.roll(block, shift, axis=1)
-    pltpu.store(list_ref.at[leaf, tile], rolled, mask=lanes >= shift)
-    list_ref[leaf, tile + 1] = rolled
-
-
-def close(list_ref, leaf, shift, tile, tail, lanes):
-    pltpu.store(list_ref.at[leaf, tile], tail, mask=lanes >= shift)
+def tile_of(start):
+    return lax.shift_right_logical(start, 7)
+
+
+def from_lane(start, lanes):
+    return lanes >= (jnp.broadcast_to(start, lanes.shape) & 127)
+
+
+def put(list_ref, index, start, block, lanes):
+    tile = tile_of(start)
+    rolled = pltpu.roll(block, start, axis=1)
+    pltpu.store(list_ref.at[index, tile], rolled, mask=from_lane(start, lanes))
+    list_ref[index, tile + 1] = rolled
+
+
+def close(list_ref, index, start, tail, lanes):
+    pltpu.store(list_ref.at[index, tile_of(start)], tail, mask=from_lane(start, lanes))
 
 
 def lane_ids(rows):
@@ -234,24 +239,21 @@
             chosen = size * mask_ref[part.mask_at(index, k)]
             kept, other = kept + chosen, other + (size - chosen)
         start_ref[index * stride + len(found)] = kept
-        last_ref[index] = split_place(kept + 127)[1]
+        last_ref[index] = tile_of(kept + 127)
         other_ref[index * stride + len(found)] = other
-        all_ref[index] = split_place(kept + other + 127)[1]
+        all_ref[index] = tile_of(kept + other + 127)
 
     lanes = lane_ids(8)
     only_places = lax.broadcasted_iota(jnp.int32, (8, 128), 0) < 3
     far = column_constant((FAR, FAR, FAR), 8)
     for index, found in enumerate(part.lists):
         for number, (k, place) in enumerate(found):
-            shift, tile = split_place(start_ref[index * stride + number])
-            put(list_ref, index, shift, tile, source_ref[place] + part.move(k), lanes)
+            put(list_ref, index, start_ref[index * stride + number], source_ref[place] + part.move(k), lanes)
         kept = start_ref[index * stride + len(found)]
         for number, (k, place) in enumerate(found):
-            shift, tile = split_place(kept + other_ref[index * stride + number])
             block = jnp.where(only_places, source_ref[place] + part.move(k), 0.0)
-            put(list_ref, index, shift, tile, block, lanes)
-        shift, tile = split_place(kept + other_ref[index * stride + len(found)])
-        close(list_ref, index, shift, tile, far, lanes)
+            put(list_ref, index, kept + other_ref[index * stride + number], block, lanes)
+        close(list_ref, index, kept + other_ref[index * stride + len(found)], far, lanes)
 
 
 def pack_side(part, span, source_ref, side_ref, start_ref, tail):
@@ -262,10 +264,8 @@
     for index in range(*span):
         found = part.lists[index]
         for number, (_, place) in enumerate(found):
-            shift, tile = split_place(start_ref[index * stride + number])
-            put(side_ref, index, shift, tile, source_ref[place], lanes)
-        shift, tile = split_place(start_ref[index * stride + len(found)])
-        close(side_ref, index, shift, tile, last, lanes)
+            put(side_ref, index, start_ref[index * stride + number], source_ref[place], lanes)
+        close(side_ref, index, start_ref[index * stride + len(found)], last, lanes)
 
 
 def widen_kernel(rows, block_ref, out_ref):
@@ -328,16 +328,7 @@
 
 
 def lane_sums(blocks):
-    rows = []
-    left = lane_ids(128) < 64
-    for i in range(0, len(blocks) - 1, 2):
-        one, two = blocks[i : i + 2]
-        both = jnp.where(left, one, two) + pltpu.roll(jnp.where(left, two, one), 64, axis=1)
-        both = jnp.transpose(both)
-        rows += [jnp.sum(half, axis=0, keepdims=True) for half in (both[:64], both[64:])]
-    if len(blocks) % 2:
-        rows.append(jnp.sum(jnp.transpose(blocks[-1]), axis=0, keepdims=True))
-    return rows
+    return [jnp.sum(jnp.transpose(block), axis=0, keepdims=True) for block in blocks]
 
 
 def leaf_totals(grid, acc_ref, counts_ref):

time: 54.7 us -> 54.5 us (level)
  starting transfers between devices: 14.3 us -> 19.5 us
  Pallas kernels: 27.8 us -> 24.9 us
  waiting for transfers between devices: 10.3 us -> 8.26 us
    ppermute x6, starting transfers between devices: 5.35 us -> 15.3 us  [ends_of(): two = lax.ppermute(jnp.where(even, first, last), axis, far_pairs)]
    ppermute x6, starting transfers between devices: 6.72 us -> 2.58 us  [ends_of(): one = lax.ppermute(jnp.where(even, last, first), axis, near_pairs)]
    ppermute x6, waiting for transfers between devices: 4.73 us -> 1.2 us  [ends_of(): two = lax.ppermute(jnp.where(even, first, last), axis, far_pairs)]
    pallas_call x16, Pallas kernels: 26.9 us -> 24 us  [call(): pl.pallas_call(body, out_shape=outs, in_specs=[spec(x) for x in inputs],...]
    ppermute x3, waiting for transfers between devices: 4.52 us -> 5.9 us  [ends_of(): ends = lax.ppermute(ends, axis, [(0, 1), (1, 0)])]
  transfers between devices with their start and end apart: 15 -> 15, of which waited for: 8 -> 6; matrix products, arithmetic and copies ran while one was open for 2% -> 2% of each run, Pallas kernels for 38% -> 32%
where the time goes in v4:
time: 54.5 us; the launch traced here: 54.8 us
  Pallas kernels  24.9 us (46%)
  starting transfers between devices  19.5 us (36%)
  waiting for transfers between devices  8.26 us (15%)
  between operations  1.04 us (2%)
  local copies, waits for them, and re-layouts  0.84 us (2%)
    pallas_call x16, Pallas kernels, call(): pl.pallas_call(body, out_shape=outs, in_specs=[spec(x) for x in inputs],...  24 us
    ppermute x6, starting transfers between devices, ends_of(): two = lax.ppermute(jnp.where(even, first, last), axis, far_pairs)  15.3 us
    ppermute x3, waiting for transfers between devices, ends_of(): ends = lax.ppermute(ends, axis, [(0, 1), (1, 0)])  5.9 us
    ppermute x6, starting transfers between devices, ends_of(): one = lax.ppermute(jnp.where(even, last, first), axis, near_pairs)  2.58 us
    ppermute x3, starting transfers between devices, ends_of(): ends = lax.ppermute(ends, axis, [(0, 1), (1, 0)])  1.7 us
    ppermute x6, waiting for transfers between devices, ends_of(): two = lax.ppermute(jnp.where(even, first, last), axis, far_pairs)  1.2 us
    ppermute x6, waiting for transfers between devices, ends_of(): one = lax.ppermute(jnp.where(even, last, first), axis, near_pairs)  1.16 us
  transfers between devices with their start and end apart: 15, of which 6 were waited for; matrix products, arithmetic and copies ran while one was open for 2% of the time, Pallas kernels for 32%

profile of v4, /device:TPU:0, one launch (start us, length us, event | category | flops | bytes accessed | tf_op | source)
XLA Modules:
  0.0 54.8 jit_solution(9416218341492795471)
XLA Ops:
  2.1 2.6 %collective-permute-start = (f32[1,2,2,8,128]{4,3,1,0,2:T(8,128)S(1)}, f32[1,2,2,8,128]{4,3,1,0,2:T(8,128)S(1)}, u32[]{:S(2)}, u32[]{:S(2)}) collective-permute-start(f32[1,2,2,8,128]{4,3,1,0,2:T(8,128)S(1)} %copy.19), channel_id=1, source_target_pairs={{0,24},{8,16},{16,8},{24,0},{1,25},{9,17},{17,9},{25,1},{2,26},{10... | collective-permute-start | bytes 49160 | tf_op jit(solution)/shard_map/ppermute | solution.py:39
  6.4 1.6 %collective-permute-start.2 = (f32[4,2,2,8,128]{4,3,1,0,2:T(8,128)S(1)}, f32[4,2,2,8,128]{4,3,1,0,2:T(8,128)S(1)}, u32[]{:S(2)}, u32[]{:S(2)}) collective-permute-start(f32[4,2,2,8,128]{4,3,1,0,2:T(8,128)S(1)} %pad_maximum_fusion.1), channel_id=1, source_target_pairs={{0,4},{4,0},{1,5},{5,1},{2,6},{6,2},{3,7},{7,3},{8,12},{12,8},{9,1... | collective-permute-start | bytes 196616 | tf_op jit(solution)/shard_map/ppermute | solution.py:29
  8.1 2.3 %volume_0.1 = (f32[8,1,128,128]{3,2,1,0:T(8,128)S(1)}, s32[9]{0:T(128)S(1)}, f32[8,10,8,128]{3,2,1,0:T(8,128)S(1)}, s32[72]{0:T(128)S(1)}, s32[8]{0:T(128)S(1)}, /*index=5*/f32[8,10,128,128]{3,2,1,0:T(8,128)S(1)}) custom-call(s32[217]{0:T(256)S(1)} %pad_add_fusion.refs_0_.refs_1_, f32[8,8,128]{2,1,0:T(8,128)S(1)} %prepare.1.block_ref.refs_1_.refs_8_, ...), custom_call_target="tpu_custom_call" | custom-call | flops 12288000 | bytes 1048576 | tf_op jit(solution)/shard_map/volume_0/pallas_call | solution.py:428
  10.8 1.7 %collective-permute-start.4 = (f32[4,4,1,8,128]{4,3,1,0,2:T(8,128)S(1)}, f32[4,4,1,8,128]{4,3,1,0,2:T(8,128)S(1)}, u32[]{:S(2)}, u32[]{:S(2)}) collective-permute-start(f32[4,4,1,8,128]{4,3,1,0,2:T(8,128)S(1)} %get-tuple-element.62), channel_id=1, source_target_pairs={{0,1},{1,0},{2,3},{3,2},{4,5},{5,4},{6,7},{7,6},{8,9},{9,8},{10,11... | collective-permute-start | bytes 196616 | tf_op jit(solution)/shard_map/ppermute | solution.py:38
  12.5 2.5 %collective-permute-start.3 = (f32[4,4,1,8,128]{4,3,1,0,2:T(8,128)S(1)}, f32[4,4,1,8,128]{4,3,1,0,2:T(8,128)S(1)}, u32[]{:S(2)}, u32[]{:S(2)}) collective-permute-start(f32[4,4,1,8,128]{4,3,1,0,2:T(8,128)S(1)} %get-tuple-element.63), channel_id=1, source_target_pairs={{0,3},{1,2},{2,1},{3,0},{4,7},{5,6},{6,5},{7,4},{8,11},{9,10},{10,... | collective-permute-start | bytes 196616 | tf_op jit(solution)/shard_map/ppermute | solution.py:39
  15.0 2.7 %volume_1.1 = (f32[8,1,128,128]{3,2,1,0:T(8,128)S(1)}, s32[32]{0:T(128)}, f32[8,12,8,128]{3,2,1,0:T(8,128)S(1)}, s32[88]{0:T(128)S(1)}, s32[8]{0:T(128)S(1)}, /*index=5*/f32[8,12,128,128]{3,2,1,0:T(8,128)S(1)}) custom-call(s32[9]{0:T(128)S(1)} %get-tuple-element.32.refs_0_, s32[217]{0:T(256)S(1)} %pad_add_fusion.refs_0_.refs_1_, ...), custom_call_target="tpu_custom_call", output_to_operand_aliasing={{0}: (4, {})} | custom-call | flops 12288000 | bytes 1048576 | tf_op jit(solution)/shard_map/volume_1/pallas_call | solution.py:428
  17.7 1.7 %volume_2.1 = (f32[8,1,128,128]{3,2,1,0:T(8,128)S(1)}, s32[16]{0:T(128)}, f32[4,11,8,128]{3,2,1,0:T(8,128)S(1)}, s32[40]{0:T(128)S(1)}, s32[4]{0:T(128)S(1)}, /*index=5*/f32[4,11,128,128]{3,2,1,0:T(8,128)S(1)}) custom-call(s32[9]{0:T(128)S(1)} %get-tuple-element.32.refs_0_, s32[217]{0:T(256)S(1)} %pad_add_fusion.refs_0_.refs_1_, ...), custom_call_target="tpu_custom_call", output_to_operand_aliasing={{0}: (4, {})} | custom-call | flops 12288000 | bytes 1048576 | tf_op jit(solution)/shard_map/volume_2/pallas_call | solution.py:428
  19.5 2.1 %volume_3.1 = (f32[8,1,128,128]{3,2,1,0:T(8,128)S(1)}, s32[16]{0:T(128)}, f32[4,11,8,128]{3,2,1,0:T(8,128)S(1)}, s32[40]{0:T(128)S(1)}, s32[4]{0:T(128)S(1)}, /*...) custom-call(s32[9]{0:T(128)S(1)} %get-tuple-element.32.refs_0_, ...), custom_call_target="tpu_custom_call", output_to_operand_aliasing={{0}: (4, {})} | custom-call | flops 12288000 | bytes 1048576 | tf_op jit(solution)/shard_map/volume_3/pallas_call | solution.py:428
  21.6 4.1 %collective-permute-start.5 = (f32[1,2,2,1,128]{4,1,0,3,2:T(2,128)S(1)}, f32[1,2,2,1,128]{4,1,0,3,2:T(2,128)S(1)}, u32[]{:S(2)}, u32[]{:S(2)}) collective-permute-start(f32[1,2,2,1,128]{4,1,0,3,2:T(2,128)S(1)} %copy.23), channel_id=1, source_target_pairs={{0,24},{8,16},{16,8},{24,0},{1,25},{9,17},{17,9},{25,1},{2,26},{10... | collective-permute-start | bytes 6152 | tf_op jit(solution)/shard_map/ppermute | solution.py:39
  25.7 1.0 %density_0.2.refs_7_ = f32[8,3,128,128]{3,2,1,0:T(8,128)S(1)} custom-call(s32[9]{0:T(128)S(1)} %get-tuple-element.32.refs_0_, f32[8,10,8,128]{3,2,1,0:T(8,128)S(1)} %get-tuple-element.43.refs_1_, s32[72]{0:T(128)S(1)} %get-tuple-element.44.refs_2_, s32[8]{0:T(128)S(1)} %get-tuple-element.45.refs_3_, f32[8,10,128,128]{3,2,1,0:T(8,128)S(1)} %get-tuple-element.46.refs_4_, ...), custom_call_target="tpu_custom_call" | custom-call | flops 16384000 | bytes 1048576 | tf_op jit(solution)/shard_map/density_0/pallas_call | solution.py:428
  27.1 1.0 %density_0.3.refs_7_ = f32[8,3,128,128]{3,2,1,0:T(8,128)S(1)} custom-call(s32[9]{0:T(128)S(1)} %get-tuple-element.32.refs_0_, f32[8,10,8,128]{3,2,1,0:T(8,128)S(1)} %get-tuple-element.43.refs_1_, s32[72]{0:T(128)S(1)} %get-tuple-element.44.refs_2_, s32[8]{0:T(128)S(1)} %get-tuple-element.45.refs_3_, ...), custom_call_target="tpu_custom_call", output_to_operand_aliasing={{}: (7, {})} | custom-call | flops 16384000 | bytes 1048576 | tf_op jit(solution)/shard_map/density_0/pallas_call | solution.py:428
  28.1 2.6 %collective-permute-done.7 = f32[4,2,2,1,128]{4,1,0,3,2:T(2,128)S(1)} collective-permute-done((f32[4,2,2,1,128]{4,1,0,3,2:T(2,128)S(1)}, f32[4,2,2,1,128]{4,1,0,3,2:T(2,128)S(1)}, u32[]{:S(2)}, u32[]{:S(2)}) %collective-permute-start.7) | collective-permute-done | bytes 8224 | tf_op jit(solution)/shard_map/ppermute | solution.py:29
  31.7 1.6 %density_1.1.refs_7_ = f32[8,3,128,128]{3,2,1,0:T(8,128)S(1)} custom-call(s32[9]{0:T(128)S(1)} %get-tuple-element.32.refs_0_, f32[8,12,8,128]{3,2,1,0:T(8,128)S(1)} %get-tuple-element.53.refs_1_, s32[88]{0:T(128)S(1)} %get-tuple-element.54.refs_2_, s32[8]{0:T(128)S(1)} %get-tuple-element.55.refs_3_, ...), custom_call_target="tpu_custom_call", output_to_operand_aliasing={{}: (7, {})} | custom-call | flops 16384000 | bytes 1048576 | tf_op jit(solution)/shard_map/density_1/pallas_call | solution.py:428
  33.4 1.1 %collective-permute-done.9 = f32[4,4,1,1,128]{4,1,0,3,2:T(4,128)S(1)} collective-permute-done((f32[4,4,1,1,128]{4,1,0,3,2:T(4,128)S(1)}, f32[4,4,1,1,128]{4,1,0,3,2:T(4,128)S(1)}, u32[]{:S(2)}, u32[]{:S(2)}) %collective-permute-start.9) | collective-permute-done | bytes 8224 | tf_op jit(solution)/shard_map/ppermute | solution.py:38
  34.5 1.0 %density_2.1.refs_7_ = f32[8,3,128,128]{3,2,1,0:T(8,128)S(1)} custom-call(s32[9]{0:T(128)S(1)} %get-tuple-element.32.refs_0_, f32[4,11,8,128]{3,2,1,0:T(8,128)S(1)} %get-tuple-element.49.refs_1_, s32[40]{0:T(128)S(1)} %get-tuple-element.50.refs_2_, s32[4]{0:T(128)S(1)} %get-tuple-element.51.refs_3_, ...), custom_call_target="tpu_custom_call", output_to_operand_aliasing={{}: (7, {})} | custom-call | flops 16384000 | bytes 1048576 | tf_op jit(solution)/shard_map/density_2/pallas_call | solution.py:428
  36.4 1.7 %density_3.1 = (f32[8,3,128,128]{3,2,1,0:T(8,128)S(1)}, f32[8,4,128]{2,1,0:T(4,128)S(1)}) custom-call(s32[9]{0:T(128)S(1)} %get-tuple-element.32.refs_0_, f32[4,11,8,128]{3,2,1,0:T(8,128)S(1)} %get-tuple-element.38.refs_1_, s32[40]{0:T(128)S(1)} %get-tuple-element.39.refs_2_, s32[4]{0:T(128)S(1)} %get-tuple-element.40.refs_3_, ...), custom_call_target="tpu_custom_call", output_to_operand_aliasing={{0}: (7, {})} | custom-call | flops 16384000 | bytes 1048576 | tf_op jit(solution)/shard_map/density_3/pallas_call | solution.py:428
  38.2 2.0 %collective-permute-start.10 = (f32[1,2,2,4,128]{4,3,1,0,2:T(4,128)S(1)}, f32[1,2,2,4,128]{4,3,1,0,2:T(4,128)S(1)}, u32[]{:S(2)}, u32[]{:S(2)}) collective-permute-start(f32[1,2,2,4,128]{4,3,1,0,2:T(4,128)S(1)} %copy.27), channel_id=1, source_target_pairs={{0,24},{8,16},{16,8},{24,0},{1,25},{9,17},{17,9},{25,1},{2,26},{10... | collective-permute-start | bytes 24584 | tf_op jit(solution)/shard_map/ppermute | solution.py:39
  40.6 1.1 %force_0.2.refs_8_ = f32[8,4,128,128]{3,2,1,0:T(8,128)S(1)} custom-call(s32[9]{0:T(128)S(1)} %get-tuple-element.32.refs_0_, f32[8,10,8,128]{3,2,1,0:T(8,128)S(1)} %get-tuple-element.43.refs_1_, s32[72]{0:T(128)S(1)} %get-tuple-element.44.refs_2_, s32[8]{0:T(128)S(1)} %get-tuple-element.45.refs_3_, f32[8,10,128,128]{3,2,1,0:T(8,128)S(1)} %get-tuple-element.46.refs_4_, ...), custom_call_target="tpu_custom_call" | custom-call | flops 20480000 | bytes 1048576 | tf_op jit(solution)/shard_map/force_0/pallas_call | solution.py:428
  41.9 1.1 %force_0.3.refs_8_ = f32[8,4,128,128]{3,2,1,0:T(8,128)S(1)} custom-call(s32[9]{0:T(128)S(1)} %get-tuple-element.32.refs_0_, f32[8,10,8,128]{3,2,1,0:T(8,128)S(1)} %get-tuple-element.43.refs_1_, s32[72]{0:T(128)S(1)} %get-tuple-element.44.refs_2_, s32[8]{0:T(128)S(1)} %get-tuple-element.45.refs_3_, ...), custom_call_target="tpu_custom_call", output_to_operand_aliasing={{}: (8, {})} | custom-call | flops 20480000 | bytes 1048576 | tf_op jit(solution)/shard_map/force_0/pallas_call | solution.py:428
  43.0 2.8 %collective-permute-done.12 = f32[4,2,2,4,128]{4,3,1,0,2:T(4,128)S(1)} collective-permute-done((f32[4,2,2,4,128]{4,3,1,0,2:T(4,128)S(1)}, f32[4,2,2,4,128]{4,3,1,0,2:T(4,128)S(1)}, u32[]{:S(2)}, u32[]{:S(2)}) %collective-permute-start.12) | collective-permute-done | bytes 32800 | tf_op jit(solution)/shard_map/ppermute | solution.py:29
  45.9 3.3 %collective-permute-start.13 = (f32[4,4,1,4,128]{4,3,1,0,2:T(4,128)S(1)}, f32[4,4,1,4,128]{4,3,1,0,2:T(4,128)S(1)}, u32[]{:S(2)}, u32[]{:S(2)}) collective-permute-start(f32[4,4,1,4,128]{4,3,1,0,2:T(4,128)S(1)} %get-tuple-element.65), channel_id=1, source_target_pairs={{0,3},{1,2},{2,1},{3,0},{4,7},{5,6},{6,5},{7,4},{8,11},{9,10},{10,... | collective-permute-start | bytes 98312 | tf_op jit(solution)/shard_map/ppermute | solution.py:39
  49.3 1.9 %force_1.1.refs_8_ = f32[8,4,128,128]{3,2,1,0:T(8,128)S(1)} custom-call(s32[9]{0:T(128)S(1)} %get-tuple-element.32.refs_0_, f32[8,12,8,128]{3,2,1,0:T(8,128)S(1)} %get-tuple-element.53.refs_1_, s32[88]{0:T(128)S(1)} %get-tuple-element.54.refs_2_, s32[8]{0:T(128)S(1)} %get-tuple-element.55.refs_3_, ...), custom_call_target="tpu_custom_call", output_to_operand_aliasing={{}: (8, {})} | custom-call | flops 20480000 | bytes 1048576 | tf_op jit(solution)/shard_map/force_1/pallas_call | solution.py:428
  51.1 1.0 %force_2.1.refs_8_ = f32[8,4,128,128]{3,2,1,0:T(8,128)S(1)} custom-call(s32[9]{0:T(128)S(1)} %get-tuple-element.32.refs_0_, f32[4,11,8,128]{3,2,1,0:T(8,128)S(1)} %get-tuple-element.49.refs_1_, s32[40]{0:T(128)S(1)} %get-tuple-element.50.refs_2_, s32[4]{0:T(128)S(1)} %get-tuple-element.51.refs_3_, ...), custom_call_target="tpu_custom_call", output_to_operand_aliasing={{}: (8, {})} | custom-call | flops 20480000 | bytes 1048576 | tf_op jit(solution)/shard_map/force_2/pallas_call | solution.py:428
  52.2 2.6 %force_3.1 = (f32[8,4,128,128]{3,2,1,0:T(8,128)S(1)}, f32[2,2,3,2,128]{4,3,2,1,0:T(2,128)}, f32[2,2,2,128]{3,2,1,0:T(2,128)}) custom-call(s32[9]{0:T(128)S(1)} %get-tuple-element.32.refs_0_, f32[4,11,8,128]{3,2,1,0:T(8,128)S(1)} %get-tuple-element.38.refs_1_, s32[40]{0:T(128)S(1)} %get-tuple-element.39.refs_2_, ...), custom_call_target="tpu_custom_call", output_to_operand_aliasing={{0}: (8, {})} | custom-call | flops 20480000 | bytes 1048576 | tf_op jit(solution)/shard_map/force_3/pallas_call | solution.py:428
  (55 shorter events, 6.7 us)
Async XLA Ops:
  1.6 4.8 %collective-permute-start.1 = (f32[1,2,2,8,128]{4,3,1,0,2:T(8,128)S(1)}, f32[1,2,2,8,128]{4,3,1,0,2:T(8,128)S(1)}, u32[]{:S(2)}, u32[]{:S(2)}) collective-permute-start(f32[1,2,2,8,128]{4,3,1,0,2:T(8,128)S(1)} %copy.20), channel_id=1, source_target_pairs={{0,8},{8,0},{16,24},{24,16},{1,9},{9,1},{17,25},{25,17},{2,10},{10... | collective-permute-start | bytes 49160 | tf_op jit(solution)/shard_map/ppermute | solution.py:38
  2.1 4.3 %collective-permute-start = (f32[1,2,2,8,128]{4,3,1,0,2:T(8,128)S(1)}, f32[1,2,2,8,128]{4,3,1,0,2:T(8,128)S(1)}, u32[]{:S(2)}, u32[]{:S(2)}) collective-permute-start(f32[1,2,2,8,128]{4,3,1,0,2:T(8,128)S(1)} %copy.19), channel_id=1, source_target_pairs={{0,24},{8,16},{16,8},{24,0},{1,25},{9,17},{17,9},{25,1},{2,26},{10... | collective-permute-start | bytes 49160 | tf_op jit(solution)/shard_map/ppermute | solution.py:39
  6.4 4.3 %collective-permute-start.2 = (f32[4,2,2,8,128]{4,3,1,0,2:T(8,128)S(1)}, f32[4,2,2,8,128]{4,3,1,0,2:T(8,128)S(1)}, u32[]{:S(2)}, u32[]{:S(2)}) collective-permute-start(f32[4,2,2,8,128]{4,3,1,0,2:T(8,128)S(1)} %pad_maximum_fusion.1), channel_id=1, source_target_pairs={{0,4},{4,0},{1,5},{5,1},{2,6},{6,2},{3,7},{7,3},{8,12},{12,8},{9,1... | collective-permute-start | bytes 196616 | tf_op jit(solution)/shard_map/ppermute | solution.py:29
  10.8 6.9 %collective-permute-start.4 = (f32[4,4,1,8,128]{4,3,1,0,2:T(8,128)S(1)}, f32[4,4,1,8,128]{4,3,1,0,2:T(8,128)S(1)}, u32[]{:S(2)}, u32[]{:S(2)}) collective-permute-start(f32[4,4,1,8,128]{4,3,1,0,2:T(8,128)S(1)} %get-tuple-element.62), channel_id=1, source_target_pairs={{0,1},{1,0},{2,3},{3,2},{4,5},{5,4},{6,7},{7,6},{8,9},{9,8},{10,11... | collective-permute-start | bytes 196616 | tf_op jit(solution)/shard_map/ppermute | solution.py:38
  12.5 6.9 %collective-permute-start.3 = (f32[4,4,1,8,128]{4,3,1,0,2:T(8,128)S(1)}, f32[4,4,1,8,128]{4,3,1,0,2:T(8,128)S(1)}, u32[]{:S(2)}, u32[]{:S(2)}) collective-permute-start(f32[4,4,1,8,128]{4,3,1,0,2:T(8,128)S(1)} %get-tuple-element.63), channel_id=1, source_target_pairs={{0,3},{1,2},{2,1},{3,0},{4,7},{5,6},{6,5},{7,4},{8,11},{9,10},{10,... | collective-permute-start | bytes 196616 | tf_op jit(solution)/shard_map/ppermute | solution.py:39
  21.6 5.2 %collective-permute-start.6 = (f32[1,2,2,1,128]{4,1,0,3,2:T(2,128)S(1)}, f32[1,2,2,1,128]{4,1,0,3,2:T(2,128)S(1)}, u32[]{:S(2)}, u32[]{:S(2)}) collective-permute-start(f32[1,2,2,1,128]{4,1,0,3,2:T(2,128)S(1)} %copy.24), channel_id=1, source_target_pairs={{0,8},{8,0},{16,24},{24,16},{1,9},{9,1},{17,25},{25,17},{2,10},{10... | collective-permute-start | bytes 6152 | tf_op jit(solution)/shard_map/ppermute | solution.py:38
  21.6 5.4 %collective-permute-start.5 = (f32[1,2,2,1,128]{4,1,0,3,2:T(2,128)S(1)}, f32[1,2,2,1,128]{4,1,0,3,2:T(2,128)S(1)}, u32[]{:S(2)}, u32[]{:S(2)}) collective-permute-start(f32[1,2,2,1,128]{4,1,0,3,2:T(2,128)S(1)} %copy.23), channel_id=1, source_target_pairs={{0,24},{8,16},{16,8},{24,0},{1,25},{9,17},{17,9},{25,1},{2,26},{10... | collective-permute-start | bytes 6152 | tf_op jit(solution)/shard_map/ppermute | solution.py:39
  27.0 3.7 %collective-permute-start.7 = (f32[4,2,2,1,128]{4,1,0,3,2:T(2,128)S(1)}, f32[4,2,2,1,128]{4,1,0,3,2:T(2,128)S(1)}, u32[]{:S(2)}, u32[]{:S(2)}) collective-permute-start(f32[4,2,2,1,128]{4,1,0,3,2:T(2,128)S(1)} %pad_maximum_fusion.5), channel_id=1, source_target_pairs={{0,4},{4,0},{1,5},{5,1},{2,6},{6,2},{3,7},{7,3},{8,12},{12,8},{9,1... | collective-permute-start | bytes 24584 | tf_op jit(solution)/shard_map/ppermute | solution.py:29
  30.8 3.7 %collective-permute-start.9 = (f32[4,4,1,1,128]{4,1,0,3,2:T(4,128)S(1)}, f32[4,4,1,1,128]{4,1,0,3,2:T(4,128)S(1)}, u32[]{:S(2)}, u32[]{:S(2)}) collective-permute-start(f32[4,4,1,1,128]{4,1,0,3,2:T(4,128)S(1)} %get-tuple-element.78), channel_id=1, source_target_pairs={{0,1},{1,0},{2,3},{3,2},{4,5},{5,4},{6,7},{7,6},{8,9},{9,8},{10,11... | collective-permute-start | bytes 24584 | tf_op jit(solution)/shard_map/ppermute | solution.py:38
  30.9 5.5 %collective-permute-start.8 = (f32[4,4,1,1,128]{4,1,0,3,2:T(4,128)S(1)}, f32[4,4,1,1,128]{4,1,0,3,2:T(4,128)S(1)}, u32[]{:S(2)}, u32[]{:S(2)}) collective-permute-start(f32[4,4,1,1,128]{4,1,0,3,2:T(4,128)S(1)} %get-tuple-element.79), channel_id=1, source_target_pairs={{0,3},{1,2},{2,1},{3,0},{4,7},{5,6},{6,5},{7,4},{8,11},{9,10},{10,... | collective-permute-start | bytes 24584 | tf_op jit(solution)/shard_map/ppermute | solution.py:39
  34.5 1.9 %copy-start = (f32[2,2,2,128]{3,2,1,0:T(2,128)S(1)}, f32[2,2,2,128]{3,2,1,0:T(2,128)}, u32[]{:S(2)}) copy-start(f32[2,2,2,128]{3,2,1,0:T(2,128)} %refs_10_.1) | copy-start | bytes 12292
  38.1 3.6 %collective-permute-start.11 = (f32[1,2,2,4,128]{4,3,1,0,2:T(4,128)S(1)}, f32[1,2,2,4,128]{4,3,1,0,2:T(4,128)S(1)}, u32[]{:S(2)}, u32[]{:S(2)}) collective-permute-start(f32[1,2,2,4,128]{4,3,1,0,2:T(4,128)S(1)} %copy.28), channel_id=1, source_target_pairs={{0,8},{8,0},{16,24},{24,16},{1,9},{9,1},{17,25},{25,17},{2,10},{10... | collective-permute-start | bytes 24584 | tf_op jit(solution)/shard_map/ppermute | solution.py:38
  38.2 3.6 %collective-permute-start.10 = (f32[1,2,2,4,128]{4,3,1,0,2:T(4,128)S(1)}, f32[1,2,2,4,128]{4,3,1,0,2:T(4,128)S(1)}, u32[]{:S(2)}, u32[]{:S(2)}) collective-permute-start(f32[1,2,2,4,128]{4,3,1,0,2:T(4,128)S(1)} %copy.27), channel_id=1, source_target_pairs={{0,24},{8,16},{16,8},{24,0},{1,25},{9,17},{17,9},{25,1},{2,26},{10... | collective-permute-start | bytes 24584 | tf_op jit(solution)/shard_map/ppermute | solution.py:39
  41.8 4.0 %collective-permute-start.12 = (f32[4,2,2,4,128]{4,3,1,0,2:T(4,128)S(1)}, f32[4,2,2,4,128]{4,3,1,0,2:T(4,128)S(1)}, u32[]{:S(2)}, u32[]{:S(2)}) collective-permute-start(f32[4,2,2,4,128]{4,3,1,0,2:T(4,128)S(1)} %pad_maximum_fusion.3), channel_id=1, source_target_pairs={{0,4},{4,0},{1,5},{5,1},{2,6},{6,2},{3,7},{7,3},{8,12},{12,8},{9,1... | collective-permute-start | bytes 98312 | tf_op jit(solution)/shard_map/ppermute | solution.py:29
  45.8 5.3 %collective-permute-start.14 = (f32[4,4,1,4,128]{4,3,1,0,2:T(4,128)S(1)}, f32[4,4,1,4,128]{4,3,1,0,2:T(4,128)S(1)}, u32[]{:S(2)}, u32[]{:S(2)}) collective-permute-start(f32[4,4,1,4,128]{4,3,1,0,2:T(4,128)S(1)} %get-tuple-element.64), channel_id=1, source_target_pairs={{0,1},{1,0},{2,3},{3,2},{4,5},{5,4},{6,7},{7,6},{8,9},{9,8},{10,11... | collective-permute-start | bytes 98312 | tf_op jit(solution)/shard_map/ppermute | solution.py:38
  45.9 6.3 %collective-permute-start.13 = (f32[4,4,1,4,128]{4,3,1,0,2:T(4,128)S(1)}, f32[4,4,1,4,128]{4,3,1,0,2:T(4,128)S(1)}, u32[]{:S(2)}, u32[]{:S(2)}) collective-permute-start(f32[4,4,1,4,128]{4,3,1,0,2:T(4,128)S(1)} %get-tuple-element.65), channel_id=1, source_target_pairs={{0,3},{1,2},{2,1},{3,0},{4,7},{5,6},{6,5},{7,4},{8,11},{9,10},{10,... | collective-permute-start | bytes 98312 | tf_op jit(solution)/shard_map/ppermute | solution.py:39

commit v5 on v4

--- a/solution.py
+++ b/solution.py
@@ -280,7 +280,7 @@
         counts_ref[place] = source_ref[place, 7:8, :].astype(jnp.int32)[0, 0]
 
 
-def run_pairs(part, span, pair, n_sums, counts_ref, tiles_ref, own_of, row_of, kept_ref, before_ref, acc_ref):
+def run_pairs(part, span, pair, n_sums, counts_ref, tiles_ref, own_of, row_of, kept_ref, before_ref, acc_ref, size=GROUP):
     zero = jnp.zeros((8, 128), jnp.float32)
 
     def leaf_step(index, carry):
@@ -290,7 +290,7 @@
 
         def group_step(group, carry):
             places = [
-                pl.ds(pl.multiple_of(group * (8 * GROUP) + 8 * chunk, 8), 8) for chunk in range(GROUP)
+                pl.ds(pl.multiple_of(group * (8 * size) + 8 * chunk, 8), 8) for chunk in range(size)
             ]
             owns = [own_of(leaf, at) for at in places]
 
@@ -321,7 +321,7 @@
                     acc_ref[leaf, i, at, :] = total[i]
             return carry
 
-        groups = lax.shift_right_logical(count + (8 * GROUP - 1), (8 * GROUP).bit_length() - 1)
+        groups = lax.shift_right_logical(count + (8 * size - 1), (8 * size).bit_length() - 1)
         return lax.fori_loop(0, groups, group_step, carry)
 
     lax.fori_loop(*span, leaf_step, 0)
@@ -368,7 +368,7 @@
     pack_places(part, mask_ref, counts_ref, source_ref, list_ref, start_ref, last_ref, all_ref, other_ref)
     run_pairs(
         part, (0, len(part.lists)), volume_pair, 1, numbers_ref, all_ref,
-        own_reader((wide_ref, WIDE)), row_reader(list_ref), kept_ref, before_ref, acc_ref,
+        own_reader((wide_ref, WIDE)), row_reader(list_ref), kept_ref, before_ref, acc_ref, 2 * GROUP,
     )
     if stage == 3:
         out_ref = refs[-3]

time: 54.5 us -> 52.9 us (0.971)
  waiting for transfers between devices: 8.26 us -> 4.94 us
  starting transfers between devices: 19.5 us -> 21.4 us
  Pallas kernels: 24.9 us -> 24.3 us
    ppermute x3, starting transfers between devices: 1.7 us -> 5.76 us  [ends_of(): ends = lax.ppermute(ends, axis, [(0, 1), (1, 0)])]
    ppermute x3, waiting for transfers between devices: 5.9 us -> 2.22 us  [ends_of(): ends = lax.ppermute(ends, axis, [(0, 1), (1, 0)])]
    ppermute x6, starting transfers between devices: 15.3 us -> 12.5 us  [ends_of(): two = lax.ppermute(jnp.where(even, first, last), axis, far_pairs)]
    ppermute x6, waiting for transfers between devices: 1.2 us -> 2.43 us  [ends_of(): two = lax.ppermute(jnp.where(even, first, last), axis, far_pairs)]
    ppermute x6, waiting for transfers between devices: 1.16 us -> 0.29 us  [ends_of(): one = lax.ppermute(jnp.where(even, last, first), axis, near_pairs)]
    pallas_call x16, Pallas kernels: 24 us -> 23.4 us  [call(): pl.pallas_call(body, out_shape=outs, in_specs=[spec(x) for x in inputs],...]
    ppermute x6, starting transfers between devices: 2.58 us -> 3.14 us  [ends_of(): one = lax.ppermute(jnp.where(even, last, first), axis, near_pairs)]
  transfers between devices with their start and end apart: 15 -> 15, of which waited for: 6 -> 7; matrix products, arithmetic and copies ran while one was open for 2% -> 2% of each run, Pallas kernels for 32% -> 34%
where the time goes in v5:
time: 52.9 us; the launch traced here: 52.7 us
  Pallas kernels  24.3 us (46%)
  starting transfers between devices  21.4 us (40%)
  waiting for transfers between devices  4.94 us (9%)
  between operations  1 us (2%)
  local copies, waits for them, and re-layouts  0.84 us (2%)
    pallas_call x16, Pallas kernels, call(): pl.pallas_call(body, out_shape=outs, in_specs=[spec(x) for x in inputs],...  23.4 us
    ppermute x6, starting transfers between devices, ends_of(): two = lax.ppermute(jnp.where(even, first, last), axis, far_pairs)  12.5 us
    ppermute x3, starting transfers between devices, ends_of(): ends = lax.ppermute(ends, axis, [(0, 1), (1, 0)])  5.76 us
    ppermute x6, starting transfers between devices, ends_of(): one = lax.ppermute(jnp.where(even, last, first), axis, near_pairs)  3.14 us
    ppermute x6, waiting for transfers between devices, ends_of(): two = lax.ppermute(jnp.where(even, first, last), axis, far_pairs)  2.43 us
    ppermute x3, waiting for transfers between devices, ends_of(): ends = lax.ppermute(ends, axis, [(0, 1), (1, 0)])  2.22 us
  transfers between devices with their start and end apart: 15, of which 7 were waited for; matrix products, arithmetic and copies ran while one was open for 2% of the time, Pallas kernels for 34%

profile of v5, /device:TPU:0, one launch (start us, length us, event | category | flops | bytes accessed | tf_op | source)
XLA Modules:
  0.0 52.7 jit_solution(7077055937043648760)
XLA Ops:
  2.1 2.6 %collective-permute-start = (f32[1,2,2,8,128]{4,3,1,0,2:T(8,128)S(1)}, f32[1,2,2,8,128]{4,3,1,0,2:T(8,128)S(1)}, u32[]{:S(2)}, u32[]{:S(2)}) collective-permute-start(f32[1,2,2,8,128]{4,3,1,0,2:T(8,128)S(1)} %copy.19), channel_id=1, source_target_pairs={{0,24},{8,16},{16,8},{24,0},{1,25},{9,17},{17,9},{25,1},{2,26},{10... | collective-permute-start | bytes 49160 | tf_op jit(solution)/shard_map/ppermute | solution.py:39
  6.4 1.6 %collective-permute-start.2 = (f32[4,2,2,8,128]{4,3,1,0,2:T(8,128)S(1)}, f32[4,2,2,8,128]{4,3,1,0,2:T(8,128)S(1)}, u32[]{:S(2)}, u32[]{:S(2)}) collective-permute-start(f32[4,2,2,8,128]{4,3,1,0,2:T(8,128)S(1)} %pad_maximum_fusion.1), channel_id=1, source_target_pairs={{0,4},{4,0},{1,5},{5,1},{2,6},{6,2},{3,7},{7,3},{8,12},{12,8},{9,1... | collective-permute-start | bytes 196616 | tf_op jit(solution)/shard_map/ppermute | solution.py:29
  8.1 2.4 %volume_0.1 = (f32[8,1,128,128]{3,2,1,0:T(8,128)S(1)}, s32[9]{0:T(128)S(1)}, f32[8,10,8,128]{3,2,1,0:T(8,128)S(1)}, s32[72]{0:T(128)S(1)}, s32[8]{0:T(128)S(1)}, /*index=5*/f32[8,10,128,128]{3,2,1,0:T(8,128)S(1)}) custom-call(s32[217]{0:T(256)S(1)} %pad_add_fusion.refs_0_.refs_1_, f32[8,8,128]{2,1,0:T(8,128)S(1)} %prepare.1.block_ref.refs_1_.refs_8_, ...), custom_call_target="tpu_custom_call" | custom-call | flops 12288000 | bytes 1048576 | tf_op jit(solution)/shard_map/volume_0/pallas_call | solution.py:428
  10.8 1.7 %collective-permute-start.4 = (f32[4,4,1,8,128]{4,3,1,0,2:T(8,128)S(1)}, f32[4,4,1,8,128]{4,3,1,0,2:T(8,128)S(1)}, u32[]{:S(2)}, u32[]{:S(2)}) collective-permute-start(f32[4,4,1,8,128]{4,3,1,0,2:T(8,128)S(1)} %get-tuple-element.62), channel_id=1, source_target_pairs={{0,1},{1,0},{2,3},{3,2},{4,5},{5,4},{6,7},{7,6},{8,9},{9,8},{10,11... | collective-permute-start | bytes 196616 | tf_op jit(solution)/shard_map/ppermute | solution.py:38
  12.5 2.9 %collective-permute-start.3 = (f32[4,4,1,8,128]{4,3,1,0,2:T(8,128)S(1)}, f32[4,4,1,8,128]{4,3,1,0,2:T(8,128)S(1)}, u32[]{:S(2)}, u32[]{:S(2)}) collective-permute-start(f32[4,4,1,8,128]{4,3,1,0,2:T(8,128)S(1)} %get-tuple-element.63), channel_id=1, source_target_pairs={{0,3},{1,2},{2,1},{3,0},{4,7},{5,6},{6,5},{7,4},{8,11},{9,10},{10,... | collective-permute-start | bytes 196616 | tf_op jit(solution)/shard_map/ppermute | solution.py:39
  15.4 2.8 %volume_1.1 = (f32[8,1,128,128]{3,2,1,0:T(8,128)S(1)}, s32[32]{0:T(128)}, f32[8,12,8,128]{3,2,1,0:T(8,128)S(1)}, s32[88]{0:T(128)S(1)}, s32[8]{0:T(128)S(1)}, /*index=5*/f32[8,12,128,128]{3,2,1,0:T(8,128)S(1)}) custom-call(s32[9]{0:T(128)S(1)} %get-tuple-element.32.refs_0_, s32[217]{0:T(256)S(1)} %pad_add_fusion.refs_0_.refs_1_, ...), custom_call_target="tpu_custom_call", output_to_operand_aliasing={{0}: (4, {})} | custom-call | flops 12288000 | bytes 1048576 | tf_op jit(solution)/shard_map/volume_1/pallas_call | solution.py:428
  18.3 1.9 %volume_2.1 = (f32[8,1,128,128]{3,2,1,0:T(8,128)S(1)}, s32[16]{0:T(128)}, f32[4,11,8,128]{3,2,1,0:T(8,128)S(1)}, s32[40]{0:T(128)S(1)}, s32[4]{0:T(128)S(1)}, /*index=5*/f32[4,11,128,128]{3,2,1,0:T(8,128)S(1)}) custom-call(s32[9]{0:T(128)S(1)} %get-tuple-element.32.refs_0_, s32[217]{0:T(256)S(1)} %pad_add_fusion.refs_0_.refs_1_, ...), custom_call_target="tpu_custom_call", output_to_operand_aliasing={{0}: (4, {})} | custom-call | flops 12288000 | bytes 1048576 | tf_op jit(solution)/shard_map/volume_2/pallas_call | solution.py:428
  20.1 1.9 %volume_3.1 = (f32[8,1,128,128]{3,2,1,0:T(8,128)S(1)}, s32[16]{0:T(128)}, f32[4,11,8,128]{3,2,1,0:T(8,128)S(1)}, s32[40]{0:T(128)S(1)}, s32[4]{0:T(128)S(1)}, /*...) custom-call(s32[9]{0:T(128)S(1)} %get-tuple-element.32.refs_0_, ...), custom_call_target="tpu_custom_call", output_to_operand_aliasing={{0}: (4, {})} | custom-call | flops 12288000 | bytes 1048576 | tf_op jit(solution)/shard_map/volume_3/pallas_call | solution.py:428
  22.2 1.5 %collective-permute-start.5 = (f32[1,2,2,1,128]{4,1,0,3,2:T(2,128)S(1)}, f32[1,2,2,1,128]{4,1,0,3,2:T(2,128)S(1)}, u32[]{:S(2)}, u32[]{:S(2)}) collective-permute-start(f32[1,2,2,1,128]{4,1,0,3,2:T(2,128)S(1)} %copy.23), channel_id=1, source_target_pairs={{0,24},{8,16},{16,8},{24,0},{1,25},{9,17},{17,9},{25,1},{2,26},{10... | collective-permute-start | bytes 6152 | tf_op jit(solution)/shard_map/ppermute | solution.py:39
  23.7 1.0 %density_0.2.refs_7_ = f32[8,3,128,128]{3,2,1,0:T(8,128)S(1)} custom-call(s32[9]{0:T(128)S(1)} %get-tuple-element.32.refs_0_, f32[8,10,8,128]{3,2,1,0:T(8,128)S(1)} %get-tuple-element.43.refs_1_, s32[72]{0:T(128)S(1)} %get-tuple-element.44.refs_2_, s32[8]{0:T(128)S(1)} %get-tuple-element.45.refs_3_, f32[8,10,128,128]{3,2,1,0:T(8,128)S(1)} %get-tuple-element.46.refs_4_, ...), custom_call_target="tpu_custom_call" | custom-call | flops 16384000 | bytes 1048576 | tf_op jit(solution)/shard_map/density_0/pallas_call | solution.py:428
  25.3 2.2 %collective-permute-start.7 = (f32[4,2,2,1,128]{4,1,0,3,2:T(2,128)S(1)}, f32[4,2,2,1,128]{4,1,0,3,2:T(2,128)S(1)}, u32[]{:S(2)}, u32[]{:S(2)}) collective-permute-start(f32[4,2,2,1,128]{4,1,0,3,2:T(2,128)S(1)} %pad_maximum_fusion.5), channel_id=1, source_target_pairs={{0,4},{4,0},{1,5},{5,1},{2,6},{6,2},{3,7},{7,3},{8,12},{12,8},{9,1... | collective-permute-start | bytes 24584 | tf_op jit(solution)/shard_map/ppermute | solution.py:29
  29.6 1.5 %collective-permute-start.8 = (f32[4,4,1,1,128]{4,1,0,3,2:T(4,128)S(1)}, f32[4,4,1,1,128]{4,1,0,3,2:T(4,128)S(1)}, u32[]{:S(2)}, u32[]{:S(2)}) collective-permute-start(f32[4,4,1,1,128]{4,1,0,3,2:T(4,128)S(1)} %get-tuple-element.79), channel_id=1, source_target_pairs={{0,3},{1,2},{2,1},{3,0},{4,7},{5,6},{6,5},{7,4},{8,11},{9,10},{10,... | collective-permute-start | bytes 24584 | tf_op jit(solution)/shard_map/ppermute | solution.py:39
  31.1 1.5 %density_1.1.refs_7_ = f32[8,3,128,128]{3,2,1,0:T(8,128)S(1)} custom-call(s32[9]{0:T(128)S(1)} %get-tuple-element.32.refs_0_, f32[8,12,8,128]{3,2,1,0:T(8,128)S(1)} %get-tuple-element.53.refs_1_, s32[88]{0:T(128)S(1)} %get-tuple-element.54.refs_2_, s32[8]{0:T(128)S(1)} %get-tuple-element.55.refs_3_, ...), custom_call_target="tpu_custom_call", output_to_operand_aliasing={{}: (7, {})} | custom-call | flops 16384000 | bytes 1048576 | tf_op jit(solution)/shard_map/density_1/pallas_call | solution.py:428
  33.9 1.2 %collective-permute-done.8 = f32[4,4,1,1,128]{4,1,0,3,2:T(4,128)S(1)} collective-permute-done((f32[4,4,1,1,128]{4,1,0,3,2:T(4,128)S(1)}, f32[4,4,1,1,128]{4,1,0,3,2:T(4,128)S(1)}, u32[]{:S(2)}, u32[]{:S(2)}) %collective-permute-start.8) | collective-permute-done | bytes 8224 | tf_op jit(solution)/shard_map/ppermute | solution.py:39
  35.0 1.5 %density_3.1 = (f32[8,3,128,128]{3,2,1,0:T(8,128)S(1)}, f32[8,4,128]{2,1,0:T(4,128)S(1)}) custom-call(s32[9]{0:T(128)S(1)} %get-tuple-element.32.refs_0_, f32[4,11,8,128]{3,2,1,0:T(8,128)S(1)} %get-tuple-element.38.refs_1_, s32[40]{0:T(128)S(1)} %get-tuple-element.39.refs_2_, s32[4]{0:T(128)S(1)} %get-tuple-element.40.refs_3_, ...), custom_call_target="tpu_custom_call", output_to_operand_aliasing={{0}: (7, {})} | custom-call | flops 16384000 | bytes 1048576 | tf_op jit(solution)/shard_map/density_3/pallas_call | solution.py:428
  36.7 1.8 %collective-permute-start.10 = (f32[1,2,2,4,128]{4,3,1,0,2:T(4,128)S(1)}, f32[1,2,2,4,128]{4,3,1,0,2:T(4,128)S(1)}, u32[]{:S(2)}, u32[]{:S(2)}) collective-permute-start(f32[1,2,2,4,128]{4,3,1,0,2:T(4,128)S(1)} %copy.27), channel_id=1, source_target_pairs={{0,24},{8,16},{16,8},{24,0},{1,25},{9,17},{17,9},{25,1},{2,26},{10... | collective-permute-start | bytes 24584 | tf_op jit(solution)/shard_map/ppermute | solution.py:39
  38.9 1.1 %force_0.2.refs_8_ = f32[8,4,128,128]{3,2,1,0:T(8,128)S(1)} custom-call(s32[9]{0:T(128)S(1)} %get-tuple-element.32.refs_0_, f32[8,10,8,128]{3,2,1,0:T(8,128)S(1)} %get-tuple-element.43.refs_1_, s32[72]{0:T(128)S(1)} %get-tuple-element.44.refs_2_, s32[8]{0:T(128)S(1)} %get-tuple-element.45.refs_3_, f32[8,10,128,128]{3,2,1,0:T(8,128)S(1)} %get-tuple-element.46.refs_4_, ...), custom_call_target="tpu_custom_call" | custom-call | flops 20480000 | bytes 1048576 | tf_op jit(solution)/shard_map/force_0/pallas_call | solution.py:428
  40.1 2.0 %collective-permute-start.12 = (f32[4,2,2,4,128]{4,3,1,0,2:T(4,128)S(1)}, f32[4,2,2,4,128]{4,3,1,0,2:T(4,128)S(1)}, u32[]{:S(2)}, u32[]{:S(2)}) collective-permute-start(f32[4,2,2,4,128]{4,3,1,0,2:T(4,128)S(1)} %pad_maximum_fusion.3), channel_id=1, source_target_pairs={{0,4},{4,0},{1,5},{5,1},{2,6},{6,2},{3,7},{7,3},{8,12},{12,8},{9,1... | collective-permute-start | bytes 98312 | tf_op jit(solution)/shard_map/ppermute | solution.py:29
  42.0 1.1 %force_0.3.refs_8_ = f32[8,4,128,128]{3,2,1,0:T(8,128)S(1)} custom-call(s32[9]{0:T(128)S(1)} %get-tuple-element.32.refs_0_, f32[8,10,8,128]{3,2,1,0:T(8,128)S(1)} %get-tuple-element.43.refs_1_, s32[72]{0:T(128)S(1)} %get-tuple-element.44.refs_2_, s32[8]{0:T(128)S(1)} %get-tuple-element.45.refs_3_, ...), custom_call_target="tpu_custom_call", output_to_operand_aliasing={{}: (8, {})} | custom-call | flops 20480000 | bytes 1048576 | tf_op jit(solution)/shard_map/force_0/pallas_call | solution.py:428
  43.1 1.2 %collective-permute-done.12 = f32[4,2,2,4,128]{4,3,1,0,2:T(4,128)S(1)} collective-permute-done((f32[4,2,2,4,128]{4,3,1,0,2:T(4,128)S(1)}, f32[4,2,2,4,128]{4,3,1,0,2:T(4,128)S(1)}, u32[]{:S(2)}, u32[]{:S(2)}) %collective-permute-start.12) | collective-permute-done | bytes 32800 | tf_op jit(solution)/shard_map/ppermute | solution.py:29
  44.6 2.2 %collective-permute-start.13 = (f32[4,4,1,4,128]{4,3,1,0,2:T(4,128)S(1)}, f32[4,4,1,4,128]{4,3,1,0,2:T(4,128)S(1)}, u32[]{:S(2)}, u32[]{:S(2)}) collective-permute-start(f32[4,4,1,4,128]{4,3,1,0,2:T(4,128)S(1)} %get-tuple-element.65), channel_id=1, source_target_pairs={{0,3},{1,2},{2,1},{3,0},{4,7},{5,6},{6,5},{7,4},{8,11},{9,10},{10,... | collective-permute-start | bytes 98312 | tf_op jit(solution)/shard_map/ppermute | solution.py:39
  46.9 1.7 %force_1.1.refs_8_ = f32[8,4,128,128]{3,2,1,0:T(8,128)S(1)} custom-call(s32[9]{0:T(128)S(1)} %get-tuple-element.32.refs_0_, f32[8,12,8,128]{3,2,1,0:T(8,128)S(1)} %get-tuple-element.53.refs_1_, s32[88]{0:T(128)S(1)} %get-tuple-element.54.refs_2_, s32[8]{0:T(128)S(1)} %get-tuple-element.55.refs_3_, ...), custom_call_target="tpu_custom_call", output_to_operand_aliasing={{}: (8, {})} | custom-call | flops 20480000 | bytes 1048576 | tf_op jit(solution)/shard_map/force_1/pallas_call | solution.py:428
  48.6 1.0 %force_2.1.refs_8_ = f32[8,4,128,128]{3,2,1,0:T(8,128)S(1)} custom-call(s32[9]{0:T(128)S(1)} %get-tuple-element.32.refs_0_, f32[4,11,8,128]{3,2,1,0:T(8,128)S(1)} %get-tuple-element.49.refs_1_, s32[40]{0:T(128)S(1)} %get-tuple-element.50.refs_2_, s32[4]{0:T(128)S(1)} %get-tuple-element.51.refs_3_, ...), custom_call_target="tpu_custom_call", output_to_operand_aliasing={{}: (8, {})} | custom-call | flops 20480000 | bytes 1048576 | tf_op jit(solution)/shard_map/force_2/pallas_call | solution.py:428
  50.4 2.3 %force_3.1 = (f32[8,4,128,128]{3,2,1,0:T(8,128)S(1)}, f32[2,2,3,2,128]{4,3,2,1,0:T(2,128)}, f32[2,2,2,128]{3,2,1,0:T(2,128)}) custom-call(s32[9]{0:T(128)S(1)} %get-tuple-element.32.refs_0_, f32[4,11,8,128]{3,2,1,0:T(8,128)S(1)} %get-tuple-element.38.refs_1_, s32[40]{0:T(128)S(1)} %get-tuple-element.39.refs_2_, ...), custom_call_target="tpu_custom_call", output_to_operand_aliasing={{0}: (8, {})} | custom-call | flops 20480000 | bytes 1048576 | tf_op jit(solution)/shard_map/force_3/pallas_call | solution.py:428
  (55 shorter events, 9.1 us)
Async XLA Ops:
  1.6 4.8 %collective-permute-start.1 = (f32[1,2,2,8,128]{4,3,1,0,2:T(8,128)S(1)}, f32[1,2,2,8,128]{4,3,1,0,2:T(8,128)S(1)}, u32[]{:S(2)}, u32[]{:S(2)}) collective-permute-start(f32[1,2,2,8,128]{4,3,1,0,2:T(8,128)S(1)} %copy.20), channel_id=1, source_target_pairs={{0,8},{8,0},{16,24},{24,16},{1,9},{9,1},{17,25},{25,17},{2,10},{10... | collective-permute-start | bytes 49160 | tf_op jit(solution)/shard_map/ppermute | solution.py:38
  2.1 4.3 %collective-permute-start = (f32[1,2,2,8,128]{4,3,1,0,2:T(8,128)S(1)}, f32[1,2,2,8,128]{4,3,1,0,2:T(8,128)S(1)}, u32[]{:S(2)}, u32[]{:S(2)}) collective-permute-start(f32[1,2,2,8,128]{4,3,1,0,2:T(8,128)S(1)} %copy.19), channel_id=1, source_target_pairs={{0,24},{8,16},{16,8},{24,0},{1,25},{9,17},{17,9},{25,1},{2,26},{10... | collective-permute-start | bytes 49160 | tf_op jit(solution)/shard_map/ppermute | solution.py:39
  6.4 4.3 %collective-permute-start.2 = (f32[4,2,2,8,128]{4,3,1,0,2:T(8,128)S(1)}, f32[4,2,2,8,128]{4,3,1,0,2:T(8,128)S(1)}, u32[]{:S(2)}, u32[]{:S(2)}) collective-permute-start(f32[4,2,2,8,128]{4,3,1,0,2:T(8,128)S(1)} %pad_maximum_fusion.1), channel_id=1, source_target_pairs={{0,4},{4,0},{1,5},{5,1},{2,6},{6,2},{3,7},{7,3},{8,12},{12,8},{9,1... | collective-permute-start | bytes 196616 | tf_op jit(solution)/shard_map/ppermute | solution.py:29
  10.8 7.5 %collective-permute-start.4 = (f32[4,4,1,8,128]{4,3,1,0,2:T(8,128)S(1)}, f32[4,4,1,8,128]{4,3,1,0,2:T(8,128)S(1)}, u32[]{:S(2)}, u32[]{:S(2)}) collective-permute-start(f32[4,4,1,8,128]{4,3,1,0,2:T(8,128)S(1)} %get-tuple-element.62), channel_id=1, source_target_pairs={{0,1},{1,0},{2,3},{3,2},{4,5},{5,4},{6,7},{7,6},{8,9},{9,8},{10,11... | collective-permute-start | bytes 196616 | tf_op jit(solution)/shard_map/ppermute | solution.py:38
  12.5 7.6 %collective-permute-start.3 = (f32[4,4,1,8,128]{4,3,1,0,2:T(8,128)S(1)}, f32[4,4,1,8,128]{4,3,1,0,2:T(8,128)S(1)}, u32[]{:S(2)}, u32[]{:S(2)}) collective-permute-start(f32[4,4,1,8,128]{4,3,1,0,2:T(8,128)S(1)} %get-tuple-element.63), channel_id=1, source_target_pairs={{0,3},{1,2},{2,1},{3,0},{4,7},{5,6},{6,5},{7,4},{8,11},{9,10},{10,... | collective-permute-start | bytes 196616 | tf_op jit(solution)/shard_map/ppermute | solution.py:39
  22.1 2.6 %collective-permute-start.6 = (f32[1,2,2,1,128]{4,1,0,3,2:T(2,128)S(1)}, f32[1,2,2,1,128]{4,1,0,3,2:T(2,128)S(1)}, u32[]{:S(2)}, u32[]{:S(2)}) collective-permute-start(f32[1,2,2,1,128]{4,1,0,3,2:T(2,128)S(1)} %copy.24), channel_id=1, source_target_pairs={{0,8},{8,0},{16,24},{24,16},{1,9},{9,1},{17,25},{25,17},{2,10},{10... | collective-permute-start | bytes 6152 | tf_op jit(solution)/shard_map/ppermute | solution.py:38
  22.2 3.0 %collective-permute-start.5 = (f32[1,2,2,1,128]{4,1,0,3,2:T(2,128)S(1)}, f32[1,2,2,1,128]{4,1,0,3,2:T(2,128)S(1)}, u32[]{:S(2)}, u32[]{:S(2)}) collective-permute-start(f32[1,2,2,1,128]{4,1,0,3,2:T(2,128)S(1)} %copy.23), channel_id=1, source_target_pairs={{0,24},{8,16},{16,8},{24,0},{1,25},{9,17},{17,9},{25,1},{2,26},{10... | collective-permute-start | bytes 6152 | tf_op jit(solution)/shard_map/ppermute | solution.py:39
  25.3 3.9 %collective-permute-start.7 = (f32[4,2,2,1,128]{4,1,0,3,2:T(2,128)S(1)}, f32[4,2,2,1,128]{4,1,0,3,2:T(2,128)S(1)}, u32[]{:S(2)}, u32[]{:S(2)}) collective-permute-start(f32[4,2,2,1,128]{4,1,0,3,2:T(2,128)S(1)} %pad_maximum_fusion.5), channel_id=1, source_target_pairs={{0,4},{4,0},{1,5},{5,1},{2,6},{6,2},{3,7},{7,3},{8,12},{12,8},{9,1... | collective-permute-start | bytes 24584 | tf_op jit(solution)/shard_map/ppermute | solution.py:29
  29.2 3.7 %collective-permute-start.9 = (f32[4,4,1,1,128]{4,1,0,3,2:T(4,128)S(1)}, f32[4,4,1,1,128]{4,1,0,3,2:T(4,128)S(1)}, u32[]{:S(2)}, u32[]{:S(2)}) collective-permute-start(f32[4,4,1,1,128]{4,1,0,3,2:T(4,128)S(1)} %get-tuple-element.78), channel_id=1, source_target_pairs={{0,1},{1,0},{2,3},{3,2},{4,5},{5,4},{6,7},{7,6},{8,9},{9,8},{10,11... | collective-permute-start | bytes 24584 | tf_op jit(solution)/shard_map/ppermute | solution.py:38
  29.6 5.4 %collective-permute-start.8 = (f32[4,4,1,1,128]{4,1,0,3,2:T(4,128)S(1)}, f32[4,4,1,1,128]{4,1,0,3,2:T(4,128)S(1)}, u32[]{:S(2)}, u32[]{:S(2)}) collective-permute-start(f32[4,4,1,1,128]{4,1,0,3,2:T(4,128)S(1)} %get-tuple-element.79), channel_id=1, source_target_pairs={{0,3},{1,2},{2,1},{3,0},{4,7},{5,6},{6,5},{7,4},{8,11},{9,10},{10,... | collective-permute-start | bytes 24584 | tf_op jit(solution)/shard_map/ppermute | solution.py:39
  32.9 2.1 %copy-start = (f32[2,2,2,128]{3,2,1,0:T(2,128)S(1)}, f32[2,2,2,128]{3,2,1,0:T(2,128)}, u32[]{:S(2)}) copy-start(f32[2,2,2,128]{3,2,1,0:T(2,128)} %refs_10_.1) | copy-start | bytes 12292
  36.6 3.4 %collective-permute-start.11 = (f32[1,2,2,4,128]{4,3,1,0,2:T(4,128)S(1)}, f32[1,2,2,4,128]{4,3,1,0,2:T(4,128)S(1)}, u32[]{:S(2)}, u32[]{:S(2)}) collective-permute-start(f32[1,2,2,4,128]{4,3,1,0,2:T(4,128)S(1)} %copy.28), channel_id=1, source_target_pairs={{0,8},{8,0},{16,24},{24,16},{1,9},{9,1},{17,25},{25,17},{2,10},{10... | collective-permute-start | bytes 24584 | tf_op jit(solution)/shard_map/ppermute | solution.py:38
  36.7 3.4 %collective-permute-start.10 = (f32[1,2,2,4,128]{4,3,1,0,2:T(4,128)S(1)}, f32[1,2,2,4,128]{4,3,1,0,2:T(4,128)S(1)}, u32[]{:S(2)}, u32[]{:S(2)}) collective-permute-start(f32[1,2,2,4,128]{4,3,1,0,2:T(4,128)S(1)} %copy.27), channel_id=1, source_target_pairs={{0,24},{8,16},{16,8},{24,0},{1,25},{9,17},{17,9},{25,1},{2,26},{10... | collective-permute-start | bytes 24584 | tf_op jit(solution)/shard_map/ppermute | solution.py:39
  40.1 4.3 %collective-permute-start.12 = (f32[4,2,2,4,128]{4,3,1,0,2:T(4,128)S(1)}, f32[4,2,2,4,128]{4,3,1,0,2:T(4,128)S(1)}, u32[]{:S(2)}, u32[]{:S(2)}) collective-permute-start(f32[4,2,2,4,128]{4,3,1,0,2:T(4,128)S(1)} %pad_maximum_fusion.3), channel_id=1, source_target_pairs={{0,4},{4,0},{1,5},{5,1},{2,6},{6,2},{3,7},{7,3},{8,12},{12,8},{9,1... | collective-permute-start | bytes 98312 | tf_op jit(solution)/shard_map/ppermute | solution.py:29
  44.4 4.2 %collective-permute-start.14 = (f32[4,4,1,4,128]{4,3,1,0,2:T(4,128)S(1)}, f32[4,4,1,4,128]{4,3,1,0,2:T(4,128)S(1)}, u32[]{:S(2)}, u32[]{:S(2)}) collective-permute-start(f32[4,4,1,4,128]{4,3,1,0,2:T(4,128)S(1)} %get-tuple-element.64), channel_id=1, source_target_pairs={{0,1},{1,0},{2,3},{3,2},{4,5},{5,4},{6,7},{7,6},{8,9},{9,8},{10,11... | collective-permute-start | bytes 98312 | tf_op jit(solution)/shard_map/ppermute | solution.py:38
  44.6 5.7 %collective-permute-start.13 = (f32[4,4,1,4,128]{4,3,1,0,2:T(4,128)S(1)}, f32[4,4,1,4,128]{4,3,1,0,2:T(4,128)S(1)}, u32[]{:S(2)}, u32[]{:S(2)}) collective-permute-start(f32[4,4,1,4,128]{4,3,1,0,2:T(4,128)S(1)} %get-tuple-element.65), channel_id=1, source_target_pairs={{0,3},{1,2},{2,1},{3,0},{4,7},{5,6},{6,5},{7,4},{8,11},{9,10},{10,... | collective-permute-start | bytes 98312 | tf_op jit(solution)/shard_map/ppermute | solution.py:39
